TPU v7x, 128 devices: a whole 4x4x4 slice. The times are simulated.
128 devices in a mesh: gx: 8 (over y, z_hi), gy: 16 (over x, z_lo, core).
Axes of the slice: x: 4, y: 4, z: 4 (z_hi: 2, z_lo: 2; z = z_hi * 2 + z_lo), core: 2. Of those that a mesh axis runs over, the one named last changes fastest.
Arguments:
- electric: float32 [3, 128, 128, 256], P(None, 'gx', 'gy'), may hold values from -1.5 to 1.5
- magnetic: float32 [3, 128, 128, 256], P(None, 'gx', 'gy'), may hold values from -6 to 6
- material: int32 [128, 128, 256], P('gx', 'gy'), may hold values from 0 to 7
- permittivity: float32 [8], replicated, may hold values from 1 to 4
- conductivity: float32 [8], replicated, may hold values from 0.01 to 1
Outputs:
- advanced_electric: float32 [3, 128, 128, 256], P(None, 'gx', 'gy')
- advanced_magnetic: float32 [3, 128, 128, 256], P(None, 'gx', 'gy')
All inputs are finite; a program needn't handle non-finite values.
Results may differ from a plain program's by a relative error of at most 0.0003.
Values sent between devices are 32-bit elements; how exact they have to be, the bound alone decides.
No kernel may reach another device: no remote copies, remote signals or barrier semaphores. Data moves between devices by JAX's collectives and lax.ppermute only.
A program may use at most 64 MiB of HBM per device.

v0:
```python
import jax
import jax.numpy as jnp
from jax import lax
from jax.sharding import PartitionSpec as P

half_step = 12.0


def shifted_2(array, axis, by):
    count = lax.axis_size(axis)
    pairs = [(i, i + by) for i in range(count) if 0 <= i + by < count]
    return lax.ppermute(array, axis, pairs)


def forward_diff(field, line_axis):
    length = field.shape[line_axis]
    zero_plane = jnp.zeros_like(lax.slice_in_dim(field, 0, 1, axis=line_axis))
    shifted = jnp.concatenate(
        [lax.slice_in_dim(field, 1, length, axis=line_axis), zero_plane], axis=line_axis
    )
    return shifted - field


def backward_diff(field, line_axis):
    length = field.shape[line_axis]
    zero_plane = jnp.zeros_like(lax.slice_in_dim(field, 0, 1, axis=line_axis))
    shifted = jnp.concatenate(
        [zero_plane, lax.slice_in_dim(field, 0, length - 1, axis=line_axis)], axis=line_axis
    )
    return field - shifted


def forward_with(field, upper_plane, line_axis):
    length = field.shape[line_axis]
    shifted = jnp.concatenate(
        [lax.slice_in_dim(field, 1, length, axis=line_axis), upper_plane], axis=line_axis
    )
    return shifted - field


def backward_with(field, lower_plane, line_axis):
    length = field.shape[line_axis]
    shifted = jnp.concatenate(
        [lower_plane, lax.slice_in_dim(field, 0, length - 1, axis=line_axis)], axis=line_axis
    )
    return field - shifted


def build_system(source, stiffness, position, line_length):
    below = jnp.where(position == 0, 0.0, -stiffness)
    above = jnp.where(position == line_length - 1, 0.0, -stiffness)
    diagonal = jnp.where(position == 0, 1.0 + stiffness, 1.0 + 2.0 * stiffness)
    return jnp.stack([below, diagonal, above, source])


def reduce_level(system, preceding, following):
    divisor_below = jnp.where(preceding[1] == 0.0, 1.0, preceding[1])
    divisor_above = jnp.where(following[1] == 0.0, 1.0, following[1])
    factor_below = -system[0] / divisor_below
    factor_above = -system[2] / divisor_above
    return jnp.stack(
        [
            factor_below * preceding[0],
            system[1] + factor_below * preceding[2] + factor_above * following[0],
            factor_above * following[2],
            system[3] + factor_below * preceding[3] + factor_above * following[3],
        ]
    )


def shift_local(system, stride, stack_axis, from_before):
    length = system.shape[stack_axis]
    zero_block = jnp.zeros_like(lax.slice_in_dim(system, 0, stride, axis=stack_axis))
    if from_before:
        return jnp.concatenate(
            [zero_block, lax.slice_in_dim(system, 0, length - stride, axis=stack_axis)],
            axis=stack_axis,
        )
    return jnp.concatenate(
        [lax.slice_in_dim(system, stride, length, axis=stack_axis), zero_block], axis=stack_axis
    )


def solve_local(source, stiffness, line_axis):
    length = source.shape[line_axis]
    position = lax.broadcasted_iota(jnp.int32, source.shape, line_axis)
    system = build_system(source, stiffness, position, length)
    stride = 1
    while stride < length:
        system = reduce_level(
            system,
            shift_local(system, stride, line_axis + 1, True),
            shift_local(system, stride, line_axis + 1, False),
        )
        stride = stride * 2
    return system[3] / system[1]


def solve_x(source, stiffness):

    def along_lines(pieces):
        solution = solve_local(pieces[0], pieces[1], 0)
        return lax.all_to_all(solution, "gx", split_axis=0, concat_axis=1, tiled=True)

    return along_lines(
        (
            lax.all_to_all(source, "gx", split_axis=1, concat_axis=0, tiled=True),
            lax.all_to_all(stiffness, "gx", split_axis=1, concat_axis=0, tiled=True),
        )
    )


def solve_y(source, stiffness):

    def along_lines(pieces):
        solution = solve_local(pieces[0], pieces[1], 1)
        return lax.all_to_all(solution, "gy", split_axis=1, concat_axis=0, tiled=True)

    return along_lines(
        (
            lax.all_to_all(source, "gy", split_axis=0, concat_axis=1, tiled=True),
            lax.all_to_all(stiffness, "gy", split_axis=0, concat_axis=1, tiled=True),
        )
    )


def from_lower_x(planes):
    return shifted_2(planes, "gx", 1)


def from_upper_x(planes):
    return shifted_2(planes, "gx", -1)


def from_lower_y(planes):
    return shifted_2(planes, "gy", 1)


def from_upper_y(planes):
    return shifted_2(planes, "gy", -1)


def coefficients(permittivity, conductivity):
    denom_table = permittivity / half_step + 0.5 * conductivity
    damp_table = (permittivity / half_step - 0.5 * conductivity) / denom_table
    couple_table = 1.0 / denom_table
    return (damp_table, couple_table)


def per_device(electric, magnetic, material, permittivity, conductivity):
    damp_table, couple_table = coefficients(permittivity, conductivity)
    damping = jnp.zeros(material.shape, jnp.float32)
    coupling = jnp.zeros(material.shape, jnp.float32)
    for table_row in range(permittivity.shape[0]):
        chosen = material == table_row
        damping = jnp.where(chosen, damp_table[table_row], damping)
        coupling = jnp.where(chosen, couple_table[table_row], coupling)
    stiffness = half_step * coupling
    above_start = from_upper_x(electric[1][0:1])
    beside_start = from_upper_y(electric[2][:, 0:1])
    interim_z = magnetic[2] - half_step * forward_with(electric[1], above_start, 0)
    interim_x = magnetic[0] - half_step * forward_with(electric[2], beside_start, 1)
    interim_y = magnetic[1] - half_step * forward_diff(electric[0], 2)
    beneath_first = from_lower_x(jnp.stack([magnetic[2][-1:], interim_y[-1:]]))
    behind_first = from_lower_y(jnp.stack([magnetic[0][:, -1:], interim_z[:, -1:]]))
    center_x = solve_y(
        damping * electric[0]
        + coupling * (backward_with(interim_z, behind_first[1], 1) - backward_diff(magnetic[1], 2)),
        stiffness,
    )
    center_y = solve_local(
        damping * electric[1]
        + coupling
        * (backward_diff(interim_x, 2) - backward_with(magnetic[2], beneath_first[0], 0)),
        stiffness,
        2,
    )
    center_z = solve_x(
        damping * electric[2]
        + coupling
        * (
            backward_with(interim_y, beneath_first[1], 0)
            - backward_with(magnetic[0], behind_first[0], 1)
        ),
        stiffness,
    )
    beside_center = from_upper_y(center_x[:, 0:1])
    above_center = from_upper_x(center_z[0:1])
    curl_for_z = half_step * forward_with(center_x, beside_center, 1)
    curl_for_x = half_step * forward_diff(center_y, 2)
    curl_for_y = half_step * forward_with(center_z, above_center, 0)
    middle_z = interim_z + curl_for_z
    middle_x = interim_x + curl_for_x
    middle_y = interim_y + curl_for_y
    second_z = middle_z + curl_for_z
    second_x = middle_x + curl_for_x
    second_y = middle_y + curl_for_y
    beneath_second = from_lower_x(jnp.stack([second_z[-1:], middle_y[-1:]]))
    behind_second = from_lower_y(jnp.stack([middle_z[:, -1:], second_x[:, -1:]]))
    final_x = solve_local(
        damping * center_x
        + coupling * (backward_with(middle_z, behind_second[0], 1) - backward_diff(second_y, 2)),
        stiffness,
        2,
    )
    final_y = solve_x(
        damping * center_y
        + coupling * (backward_diff(middle_x, 2) - backward_with(second_z, beneath_second[0], 0)),
        stiffness,
    )
    final_z = solve_y(
        damping * center_z
        + coupling
        * (
            backward_with(middle_y, beneath_second[1], 0)
            - backward_with(second_x, behind_second[1], 1)
        ),
        stiffness,
    )
    above_final = from_upper_x(final_y[0:1])
    beside_final = from_upper_y(final_z[:, 0:1])
    magnet_z = second_z - half_step * forward_with(final_y, above_final, 0)
    magnet_x = second_x - half_step * forward_with(final_z, beside_final, 1)
    magnet_y = second_y - half_step * forward_diff(final_x, 2)
    return (jnp.stack([final_x, final_y, final_z]), jnp.stack([magnet_x, magnet_y, magnet_z]))


def solution(mesh):
    return jax.shard_map(
        per_device,
        mesh=mesh,
        in_specs=(
            P(None, "gx", "gy", None),
            P(None, "gx", "gy", None),
            P("gx", "gy", None),
            P(),
            P(),
        ),
        out_specs=(P(None, "gx", "gy", None), P(None, "gx", "gy", None)),
        check_vma=False,
    )
```

profile of v0, /device:TPU:1, one launch (start us, length us, event | category | flops | bytes accessed | tf_op | source)
XLA Modules:
  0.0 184.5 jit_solution(4386900384595699389)
XLA Ops:
  1.7 3.3 %collective-permute-start.3 = (f32[16,1,256]{2,1,0:T(1,128)S(1)}, f32[16,1,256]{2,1,0:T(1,128)S(1)}, u32[]{:S(2)}, u32[]{:S(2)}) collective-permute-start(f32[16,1,256]{2,1,0:T(1,128)S(1)} %slice.2123), channel_id=1, source_target_pairs={{1,0},{2,1},{3,2},{4,3},{5,4},{6,5},{7,6},{8,7},{9,8},{10,9},{11,1... | collective-permute-start | bytes 49160 | tf_op jit(solution)/shard_map/ppermute | solution.py:12
  8.6 5.1 %fusion.656 = (f32[1,16,8,256]{3,2,1,0:T(8,128)S(1)}, f32[16,8,256]{2,1,0:T(8,128)S(1)}, pred[16,8,256]{2,1,0:T(8,128)(4,1)S(1)}, pred[16,8,256]{2,1,0:T(8,128)(...) fusion(pred[256]{0:T(512)(128)(4,1)S(1)} %iota_compare_fusion.1, ...), kind=kLoop, calls=%fused_computation.1428 | loop fusion | flops 622592 | bytes 655648 | tf_op jit(solution)/shard_map/stack | solution.py:53
  14.6 6.2 %collective-permute-start.4 = (f32[2,1,8,256]{3,2,1,0:T(8,128)S(1)}, f32[2,1,8,256]{3,2,1,0:T(8,128)S(1)}, u32[]{:S(2)}, u32[]{:S(2)}) collective-permute-start(f32[2,1,8,256]{3,2,1,0:T(8,128)S(1)} %pad_maximum_fusion.51), channel_id=1, source_target_pairs={{0,16},{16,32},{32,48},{48,64},{64,80},{80,96},{96,112},{1,17},{17... | collective-permute-start | bytes 49160 | tf_op jit(solution)/shard_map/ppermute | solution.py:12
  20.9 3.4 %collective-permute-start.1 = (f32[2,16,1,256]{3,2,1,0:T(1,128)S(1)}, f32[2,16,1,256]{3,2,1,0:T(1,128)S(1)}, u32[]{:S(2)}, u32[]{:S(2)}) collective-permute-start(f32[2,16,1,256]{3,2,1,0:T(1,128)S(1)} %pad_maximum_fusion.49), channel_id=1, source_target_pairs={{0,1},{1,2},{2,3},{3,4},{4,5},{5,6},{6,7},{7,8},{8,9},{9,10},{10,1... | collective-permute-start | bytes 98312 | tf_op jit(solution)/shard_map/ppermute | solution.py:12
  24.2 5.4 %fusion.489 = (f32[16,8,256]{2,1,0:T(8,128)S(1)}, f32[16,8,256]{2,1,0:T(8,128)S(1)}) fusion(f32[16,8,256]{2,1,0:T(8,128)S(1)} %get-tuple-element.65, f32[15,8,256]{2,1,0:T(8,128)S(1)} %slice_bitcast_fusion.6, f32[1,8,256]{2,1,0:T(8,128)S(1)} %get-tuple-element.328, f32[16,8,256]{2,1,0:T(8,128)S(1)} %get-tuple-element.128, f32[16,8,255]{2,1,0:T(8,128)S(1)} %bitcast.2398, ...), kind=kLoop, calls=%fused_computation.1020 | loop fusion | flops 491520 | bytes 1310240 | tf_op jit(solution)/shard_map/add | solution.py:172
  36.6 1.6 copy.44
  38.2 8.1 %all-to-all-start.4 = ((f32[16,8,256]{2,0,1:T(8,128)}), f32[16,8,256]{2,0,1:T(8,128)S(1)}, u32[]{:S(2)}, u32[]{:S(2)}) async-start(f32[16,8,256]{2,0,1:T(8,128)} %copy.44), calls=%async_computation.4 | async-start | bytes 262144 | tf_op jit(solution)/shard_map/all_to_all | solution.py:108
  47.6 5.6 %all-to-all-done.4 = f32[16,8,256]{2,0,1:T(8,128)S(1)} async-done(((f32[16,8,256]{2,0,1:T(8,128)}), f32[16,8,256]{2,0,1:T(8,128)S(1)}, u32[]{:S(2)}, u32[]{:S(2)}) %all-to-all-start.4) | async-done | bytes 131104 | tf_op jit(solution)/shard_map/all_to_all | solution.py:108
  53.2 3.4 %all-to-all-start.3 = ((f32[16,8,256]{2,0,1:T(8,128)}), f32[16,8,256]{2,0,1:T(8,128)S(1)}, u32[]{:S(2)}, u32[]{:S(2)}) async-start(f32[16,8,256]{2,0,1:T(8,128)} %copy.43), calls=%async_computation.3 | async-start | bytes 262144 | tf_op jit(solution)/shard_map/all_to_all | solution.py:107
  57.0 6.3 %all-to-all-done.3 = f32[16,8,256]{2,0,1:T(8,128)S(1)} async-done(((f32[16,8,256]{2,0,1:T(8,128)}), f32[16,8,256]{2,0,1:T(8,128)S(1)}, u32[]{:S(2)}, u32[]{:S(2)}) %all-to-all-start.3) | async-done | bytes 131104 | tf_op jit(solution)/shard_map/all_to_all | solution.py:107
  63.3 6.9 %all-to-all-start.1 = ((f32[16,8,256]{2,1,0:T(8,128)}), f32[16,8,256]{2,1,0:T(8,128)S(1)}, u32[]{:S(2)}, u32[]{:S(2)}) async-start(f32[16,8,256]{2,1,0:T(8,128)} %get-tuple-element.312), calls=%async_computation.1 | async-start | bytes 262144 | tf_op jit(solution)/shard_map/all_to_all | solution.py:122
  73.4 3.0 %all-to-all-done.1 = f32[16,8,256]{2,1,0:T(8,128)S(1)} async-done(((f32[16,8,256]{2,1,0:T(8,128)}), f32[16,8,256]{2,1,0:T(8,128)S(1)}, u32[]{:S(2)}, u32[]{:S(2)}) %all-to-all-start.1) | async-done | bytes 131104 | tf_op jit(solution)/shard_map/all_to_all | solution.py:122
  76.4 3.7 %all-to-all-start = ((f32[16,8,256]{2,1,0:T(8,128)}), f32[16,8,256]{2,1,0:T(8,128)S(1)}, u32[]{:S(2)}, u32[]{:S(2)}) async-start(f32[16,8,256]{2,1,0:T(8,128)} %get-tuple-element.314), calls=%async_computation | async-start | bytes 262144 | tf_op jit(solution)/shard_map/all_to_all | solution.py:121
  80.2 6.1 %all-to-all-done = f32[16,8,256]{2,1,0:T(8,128)S(1)} async-done(((f32[16,8,256]{2,1,0:T(8,128)}), f32[16,8,256]{2,1,0:T(8,128)S(1)}, u32[]{:S(2)}, u32[]{:S(2)}) %all-to-all-start) | async-done | bytes 131104 | tf_op jit(solution)/shard_map/all_to_all | solution.py:121
  86.3 4.0 %all-to-all-start.5 = ((f32[128,1,256]{2,1,0:T(1,128)}), f32[128,1,256]{2,1,0:T(1,128)}, u32[]{:S(2)}, u32[]{:S(2)}) async-start(f32[128,1,256]{2,1,0:T(1,128)} %copy.51), calls=%async_computation.5 | async-start | bytes 262144 | tf_op jit(solution)/shard_map/all_to_all | solution.py:103
  93.5 3.6 %all-to-all-done.5 = f32[128,1,256]{2,1,0:T(1,128)} async-done(((f32[128,1,256]{2,1,0:T(1,128)}), f32[128,1,256]{2,1,0:T(1,128)}, u32[]{:S(2)}, u32[]{:S(2)}) %all-to-all-start.5) | async-done | bytes 131104 | tf_op jit(solution)/shard_map/all_to_all | solution.py:103
  97.1 5.1 %all-to-all-start.2 = ((f32[1,128,256]{2,0,1:T(1,128)}), f32[1,128,256]{2,0,1:T(1,128)S(1)}, u32[]{:S(2)}, u32[]{:S(2)}) async-start(f32[1,128,256]{2,0,1:T(1,128)} %copy.42), calls=%async_computation.2 | async-start | bytes 262144 | tf_op jit(solution)/shard_map/all_to_all | solution.py:117
  104.6 4.6 %collective-permute-done.6 = f32[1,8,256]{2,1,0:T(8,128)S(1)} collective-permute-done((f32[1,8,256]{2,1,0:T(8,128)S(1)}, f32[1,8,256]{2,1,0:T(8,128)S(1)}, u32[]{:S(2)}, u32[]{:S(2)}) %collective-permute-start.6) | collective-permute-done | bytes 8224 | tf_op jit(solution)/shard_map/ppermute | solution.py:12
  110.0 3.3 %collective-permute-start.2 = (f32[16,1,256]{2,1,0:T(1,128)S(1)}, f32[16,1,256]{2,1,0:T(1,128)S(1)}, u32[]{:S(2)}, u32[]{:S(2)}) collective-permute-start(f32[16,1,256]{2,1,0:T(1,128)S(1)} %slice.2120), channel_id=1, source_target_pairs={{1,0},{2,1},{3,2},{4,3},{5,4},{6,5},{7,6},{8,7},{9,8},{10,9},{11,1... | collective-permute-start | bytes 49160 | tf_op jit(solution)/shard_map/ppermute | solution.py:12
  113.9 2.1 %collective-permute-done.2 = f32[16,1,256]{2,1,0:T(1,128)S(1)} collective-permute-done((f32[16,1,256]{2,1,0:T(1,128)S(1)}, f32[16,1,256]{2,1,0:T(1,128)S(1)}, u32[]{:S(2)}, u32[]{:S(2)}) %collective-permute-start.2) | collective-permute-done | bytes 16416 | tf_op jit(solution)/shard_map/ppermute | solution.py:12
  116.2 3.5 %collective-permute-start.7 = (f32[2,1,8,256]{3,2,1,0:T(8,128)S(1)}, f32[2,1,8,256]{3,2,1,0:T(8,128)S(1)}, u32[]{:S(2)}, u32[]{:S(2)}) collective-permute-start(f32[2,1,8,256]{3,2,1,0:T(8,128)S(1)} %pad_maximum_fusion.52), channel_id=1, source_target_pairs={{0,16},{16,32},{32,48},{48,64},{64,80},{80,96},{96,112},{1,17},{17... | collective-permute-start | bytes 49160 | tf_op jit(solution)/shard_map/ppermute | solution.py:12
  119.7 2.1 %collective-permute-start.5 = (f32[2,16,1,256]{3,2,1,0:T(1,128)S(1)}, f32[2,16,1,256]{3,2,1,0:T(1,128)S(1)}, u32[]{:S(2)}, u32[]{:S(2)}) collective-permute-start(f32[2,16,1,256]{3,2,1,0:T(1,128)S(1)} %pad_maximum_fusion.50), channel_id=1, source_target_pairs={{0,1},{1,2},{2,3},{3,4},{4,5},{5,6},{6,7},{7,8},{8,9},{9,10},{10,1... | collective-permute-start | bytes 98312 | tf_op jit(solution)/shard_map/ppermute | solution.py:12
  128.4 4.9 %all-to-all-start.6 = ((f32[16,8,256]{2,0,1:T(8,128)}), f32[16,8,256]{2,0,1:T(8,128)S(1)}, u32[]{:S(2)}, u32[]{:S(2)}) async-start(f32[16,8,256]{2,0,1:T(8,128)} %copy.53), calls=%async_computation.6 | async-start | bytes 262144 | tf_op jit(solution)/shard_map/all_to_all | solution.py:107
  140.6 7.1 %all-to-all-start.8 = ((f32[16,8,256]{2,1,0:T(8,128)}), f32[16,8,256]{2,1,0:T(8,128)S(1)}, u32[]{:S(2)}, u32[]{:S(2)}) async-start(f32[16,8,256]{2,1,0:T(8,128)} %get-tuple-element.302), calls=%async_computation.8 | async-start | bytes 262144 | tf_op jit(solution)/shard_map/all_to_all | solution.py:121
  151.8 2.1 %all-to-all-done.8 = f32[16,8,256]{2,1,0:T(8,128)S(1)} async-done(((f32[16,8,256]{2,1,0:T(8,128)}), f32[16,8,256]{2,1,0:T(8,128)S(1)}, u32[]{:S(2)}, u32[]{:S(2)}) %all-to-all-start.8) | async-done | bytes 131104 | tf_op jit(solution)/shard_map/all_to_all | solution.py:121
  153.9 5.4 %all-to-all-start.7 = ((f32[128,1,256]{2,1,0:T(1,128)}), f32[128,1,256]{2,1,0:T(1,128)S(1)}, u32[]{:S(2)}, u32[]{:S(2)}) async-start(f32[128,1,256]{2,1,0:T(1,128)} %copy.54), calls=%async_computation.7 | async-start | bytes 262144 | tf_op jit(solution)/shard_map/all_to_all | solution.py:103
  162.5 3.8 %all-to-all-done.7 = f32[128,1,256]{2,1,0:T(1,128)S(1)} async-done(((f32[128,1,256]{2,1,0:T(1,128)}), f32[128,1,256]{2,1,0:T(1,128)S(1)}, u32[]{:S(2)}, u32[]{:S(2)}) %all-to-all-start.7) | async-done | bytes 131104 | tf_op jit(solution)/shard_map/all_to_all | solution.py:103
  166.2 4.9 %all-to-all-start.9 = ((f32[1,128,256]{2,0,1:T(1,128)}), f32[1,128,256]{2,0,1:T(1,128)S(1)}, u32[]{:S(2)}, u32[]{:S(2)}) async-start(f32[1,128,256]{2,0,1:T(1,128)} %copy.56), calls=%async_computation.9 | async-start | bytes 262144 | tf_op jit(solution)/shard_map/all_to_all | solution.py:117
  171.3 1.4 collective-permute-start.9
  172.8 4.7 %collective-permute-done.9 = f32[1,8,256]{2,1,0:T(8,128)S(1)} collective-permute-done((f32[1,8,256]{2,1,0:T(8,128)S(1)}, f32[1,8,256]{2,1,0:T(8,128)S(1)}, u32[]{:S(2)}, u32[]{:S(2)}) %collective-permute-start.9) | collective-permute-done | bytes 8224 | tf_op jit(solution)/shard_map/ppermute | solution.py:12
  177.7 3.2 %collective-permute-start.8 = (f32[16,1,256]{2,1,0:T(1,128)S(1)}, f32[16,1,256]{2,1,0:T(1,128)S(1)}, u32[]{:S(2)}, u32[]{:S(2)}) collective-permute-start(f32[16,1,256]{2,1,0:T(1,128)S(1)} %slice.2223), channel_id=1, source_target_pairs={{1,0},{2,1},{3,2},{4,3},{5,4},{6,5},{7,6},{8,7},{9,8},{10,9},{11,1... | collective-permute-start | bytes 49160 | tf_op jit(solution)/shard_map/ppermute | solution.py:12
  181.7 2.0 %collective-permute-done.8 = f32[16,1,256]{2,1,0:T(1,128)S(1)} collective-permute-done((f32[16,1,256]{2,1,0:T(1,128)S(1)}, f32[16,1,256]{2,1,0:T(1,128)S(1)}, u32[]{:S(2)}, u32[]{:S(2)}) %collective-permute-start.8) | collective-permute-done | bytes 16416 | tf_op jit(solution)/shard_map/ppermute | solution.py:12
  (320 shorter events, 46.2 us)
Async XLA Ops:
  0.6 6.4 %copy-start = (f32[3,16,8,256]{3,2,1,0:T(8,128)S(1)}, f32[3,16,8,256]{3,2,1,0:T(8,128)}, u32[]{:S(2)}) copy-start(f32[3,16,8,256]{3,2,1,0:T(8,128)} %param.6) | copy-start | bytes 1179652
  1.7 12.2 %collective-permute-start.3 = (f32[16,1,256]{2,1,0:T(1,128)S(1)}, f32[16,1,256]{2,1,0:T(1,128)S(1)}, u32[]{:S(2)}, u32[]{:S(2)}) collective-permute-start(f32[16,1,256]{2,1,0:T(1,128)S(1)} %slice.2123), channel_id=1, source_target_pairs={{1,0},{2,1},{3,2},{4,3},{5,4},{6,5},{7,6},{8,7},{9,8},{10,9},{11,1... | collective-permute-start | bytes 49160 | tf_op jit(solution)/shard_map/ppermute | solution.py:12
  5.1 8.9 %collective-permute-start = (f32[1,8,256]{2,1,0:T(8,128)S(1)}, f32[1,8,256]{2,1,0:T(8,128)S(1)}, u32[]{:S(2)}, u32[]{:S(2)}) collective-permute-start(f32[1,8,256]{2,1,0:T(8,128)S(1)} %slice_bitcast_fusion.24), channel_id=1, source_target_pairs={{16,0},{32,16},{48,32},{64,48},{80,64},{96,80},{112,96},{17,1},{33... | collective-permute-start | bytes 24584 | tf_op jit(solution)/shard_map/ppermute | solution.py:12
  6.4 24.4 %copy-start.33 = (pred[256]{0:T(512)(128)(4,1)}, pred[256]{0:T(512)(128)(4,1)S(1)}, u32[]{:S(2)}) copy-start(pred[256]{0:T(512)(128)(4,1)S(1)} %iota_compare_fusion.1) | copy-start | bytes 772
  7.1 23.7 %copy-start.35 = (pred[256]{0:T(512)(128)(4,1)}, pred[256]{0:T(512)(128)(4,1)S(1)}, u32[]{:S(2)}) copy-start(pred[256]{0:T(512)(128)(4,1)S(1)} %iota_compare_fusion) | copy-start | bytes 772
  13.7 15.9 %copy-start.19 = (f32[1,16,8,256]{3,2,1,0:T(8,128)}, f32[1,16,8,256]{3,2,1,0:T(8,128)S(1)}, u32[]{:S(2)}) copy-start(f32[1,16,8,256]{3,2,1,0:T(8,128)S(1)} %get-tuple-element.64) | copy-start | bytes 393220
  13.8 15.9 %copy-start.15 = (f32[1,16,8,256]{3,2,1,0:T(8,128)}, f32[1,16,8,256]{3,2,1,0:T(8,128)S(1)}, u32[]{:S(2)}) copy-start(f32[1,16,8,256]{3,2,1,0:T(8,128)S(1)} %get-tuple-element.315) | copy-start | bytes 393220
  13.8 15.9 %copy-start.17 = (f32[1,16,8,256]{3,2,1,0:T(8,128)}, f32[1,16,8,256]{3,2,1,0:T(8,128)S(1)}, u32[]{:S(2)}) copy-start(f32[1,16,8,256]{3,2,1,0:T(8,128)S(1)} %get-tuple-element.316) | copy-start | bytes 393220
  13.8 78.1 %copy-start.29 = (pred[128]{0:T(512)(128)(4,1)}, pred[128]{0:T(512)(128)(4,1)S(1)}, u32[]{:S(2)}) copy-start(pred[128]{0:T(512)(128)(4,1)S(1)} %get-tuple-element.357) | copy-start | bytes 388
  13.8 78.1 %copy-start.31 = (pred[128]{0:T(512)(128)(4,1)}, pred[128]{0:T(512)(128)(4,1)S(1)}, u32[]{:S(2)}) copy-start(pred[128]{0:T(512)(128)(4,1)S(1)} %get-tuple-element.358) | copy-start | bytes 388
  14.6 9.7 %collective-permute-start.4 = (f32[2,1,8,256]{3,2,1,0:T(8,128)S(1)}, f32[2,1,8,256]{3,2,1,0:T(8,128)S(1)}, u32[]{:S(2)}, u32[]{:S(2)}) collective-permute-start(f32[2,1,8,256]{3,2,1,0:T(8,128)S(1)} %pad_maximum_fusion.51), channel_id=1, source_target_pairs={{0,16},{16,32},{32,48},{48,64},{64,80},{80,96},{96,112},{1,17},{17... | collective-permute-start | bytes 49160 | tf_op jit(solution)/shard_map/ppermute | solution.py:12
  20.9 9.0 %collective-permute-start.1 = (f32[2,16,1,256]{3,2,1,0:T(1,128)S(1)}, f32[2,16,1,256]{3,2,1,0:T(1,128)S(1)}, u32[]{:S(2)}, u32[]{:S(2)}) collective-permute-start(f32[2,16,1,256]{3,2,1,0:T(1,128)S(1)} %pad_maximum_fusion.49), channel_id=1, source_target_pairs={{0,1},{1,2},{2,3},{3,4},{4,5},{5,6},{6,7},{7,8},{8,9},{9,10},{10,1... | collective-permute-start | bytes 98312 | tf_op jit(solution)/shard_map/ppermute | solution.py:12
  38.2 15.0 %all-to-all-start.4 = ((f32[16,8,256]{2,0,1:T(8,128)}), f32[16,8,256]{2,0,1:T(8,128)S(1)}, u32[]{:S(2)}, u32[]{:S(2)}) async-start(f32[16,8,256]{2,0,1:T(8,128)} %copy.44), calls=%async_computation.4 | async-start | bytes 262144 | tf_op jit(solution)/shard_map/all_to_all | solution.py:108
  53.2 10.1 %all-to-all-start.3 = ((f32[16,8,256]{2,0,1:T(8,128)}), f32[16,8,256]{2,0,1:T(8,128)S(1)}, u32[]{:S(2)}, u32[]{:S(2)}) async-start(f32[16,8,256]{2,0,1:T(8,128)} %copy.43), calls=%async_computation.3 | async-start | bytes 262144 | tf_op jit(solution)/shard_map/all_to_all | solution.py:107
  56.8 15.0 %copy-start.2 = (f32[8,16,1,256]{3,1,0,2:T(8,128)}, f32[8,16,1,256]{3,1,0,2:T(8,128)S(1)}, u32[]{:S(2)}) copy-start(f32[8,16,1,256]{3,1,0,2:T(8,128)S(1)} %copy.48) | copy-start | bytes 393220
  56.8 15.0 %copy-start.4 = (f32[8,16,1,256]{3,1,0,2:T(8,128)}, f32[8,16,1,256]{3,1,0,2:T(8,128)S(1)}, u32[]{:S(2)}) copy-start(f32[8,16,1,256]{3,1,0,2:T(8,128)S(1)} %copy.46) | copy-start | bytes 393220
  56.9 15.0 %copy-start.6 = (f32[16,8,256]{2,0,1:T(8,128)}, f32[16,8,256]{2,0,1:T(8,128)S(1)}, u32[]{:S(2)}) copy-start(f32[16,8,256]{2,0,1:T(8,128)S(1)} %neg.2142) | copy-start | bytes 393220
  63.3 13.1 %all-to-all-start.1 = ((f32[16,8,256]{2,1,0:T(8,128)}), f32[16,8,256]{2,1,0:T(8,128)S(1)}, u32[]{:S(2)}, u32[]{:S(2)}) async-start(f32[16,8,256]{2,1,0:T(8,128)} %get-tuple-element.312), calls=%async_computation.1 | async-start | bytes 262144 | tf_op jit(solution)/shard_map/all_to_all | solution.py:122
  76.4 9.9 %all-to-all-start = ((f32[16,8,256]{2,1,0:T(8,128)}), f32[16,8,256]{2,1,0:T(8,128)S(1)}, u32[]{:S(2)}, u32[]{:S(2)}) async-start(f32[16,8,256]{2,1,0:T(8,128)} %get-tuple-element.314), calls=%async_computation | async-start | bytes 262144 | tf_op jit(solution)/shard_map/all_to_all | solution.py:121
  86.3 10.8 %all-to-all-start.5 = ((f32[128,1,256]{2,1,0:T(1,128)}), f32[128,1,256]{2,1,0:T(1,128)}, u32[]{:S(2)}, u32[]{:S(2)}) async-start(f32[128,1,256]{2,1,0:T(1,128)} %copy.51), calls=%async_computation.5 | async-start | bytes 262144 | tf_op jit(solution)/shard_map/all_to_all | solution.py:103
  97.1 12.8 %all-to-all-start.2 = ((f32[1,128,256]{2,0,1:T(1,128)}), f32[1,128,256]{2,0,1:T(1,128)S(1)}, u32[]{:S(2)}, u32[]{:S(2)}) async-start(f32[1,128,256]{2,0,1:T(1,128)} %copy.42), calls=%async_computation.2 | async-start | bytes 262144 | tf_op jit(solution)/shard_map/all_to_all | solution.py:117
  103.3 5.9 %collective-permute-start.6 = (f32[1,8,256]{2,1,0:T(8,128)S(1)}, f32[1,8,256]{2,1,0:T(8,128)S(1)}, u32[]{:S(2)}, u32[]{:S(2)}) collective-permute-start(f32[1,8,256]{2,1,0:T(8,128)S(1)} %slice_bitcast_fusion.20), channel_id=1, source_target_pairs={{16,0},{32,16},{48,32},{64,48},{80,64},{96,80},{112,96},{17,1},{33... | collective-permute-start | bytes 24584 | tf_op jit(solution)/shard_map/ppermute | solution.py:12
  110.0 6.1 %collective-permute-start.2 = (f32[16,1,256]{2,1,0:T(1,128)S(1)}, f32[16,1,256]{2,1,0:T(1,128)S(1)}, u32[]{:S(2)}, u32[]{:S(2)}) collective-permute-start(f32[16,1,256]{2,1,0:T(1,128)S(1)} %slice.2120), channel_id=1, source_target_pairs={{1,0},{2,1},{3,2},{4,3},{5,4},{6,5},{7,6},{8,7},{9,8},{10,9},{11,1... | collective-permute-start | bytes 49160 | tf_op jit(solution)/shard_map/ppermute | solution.py:12
  116.2 5.6 %collective-permute-start.7 = (f32[2,1,8,256]{3,2,1,0:T(8,128)S(1)}, f32[2,1,8,256]{3,2,1,0:T(8,128)S(1)}, u32[]{:S(2)}, u32[]{:S(2)}) collective-permute-start(f32[2,1,8,256]{3,2,1,0:T(8,128)S(1)} %pad_maximum_fusion.52), channel_id=1, source_target_pairs={{0,16},{16,32},{32,48},{48,64},{64,80},{80,96},{96,112},{1,17},{17... | collective-permute-start | bytes 49160 | tf_op jit(solution)/shard_map/ppermute | solution.py:12
  119.7 3.2 %collective-permute-start.5 = (f32[2,16,1,256]{3,2,1,0:T(1,128)S(1)}, f32[2,16,1,256]{3,2,1,0:T(1,128)S(1)}, u32[]{:S(2)}, u32[]{:S(2)}) collective-permute-start(f32[2,16,1,256]{3,2,1,0:T(1,128)S(1)} %pad_maximum_fusion.50), channel_id=1, source_target_pairs={{0,1},{1,2},{2,3},{3,4},{4,5},{5,6},{6,7},{7,8},{8,9},{9,10},{10,1... | collective-permute-start | bytes 98312 | tf_op jit(solution)/shard_map/ppermute | solution.py:12
  128.4 12.2 %all-to-all-start.6 = ((f32[16,8,256]{2,0,1:T(8,128)}), f32[16,8,256]{2,0,1:T(8,128)S(1)}, u32[]{:S(2)}, u32[]{:S(2)}) async-start(f32[16,8,256]{2,0,1:T(8,128)} %copy.53), calls=%async_computation.6 | async-start | bytes 262144 | tf_op jit(solution)/shard_map/all_to_all | solution.py:107
  140.6 13.2 %all-to-all-start.8 = ((f32[16,8,256]{2,1,0:T(8,128)}), f32[16,8,256]{2,1,0:T(8,128)S(1)}, u32[]{:S(2)}, u32[]{:S(2)}) async-start(f32[16,8,256]{2,1,0:T(8,128)} %get-tuple-element.302), calls=%async_computation.8 | async-start | bytes 262144 | tf_op jit(solution)/shard_map/all_to_all | solution.py:121
  153.9 12.4 %all-to-all-start.7 = ((f32[128,1,256]{2,1,0:T(1,128)}), f32[128,1,256]{2,1,0:T(1,128)S(1)}, u32[]{:S(2)}, u32[]{:S(2)}) async-start(f32[128,1,256]{2,1,0:T(1,128)} %copy.54), calls=%async_computation.7 | async-start | bytes 262144 | tf_op jit(solution)/shard_map/all_to_all | solution.py:103
  166.2 11.4 %all-to-all-start.9 = ((f32[1,128,256]{2,0,1:T(1,128)}), f32[1,128,256]{2,0,1:T(1,128)S(1)}, u32[]{:S(2)}, u32[]{:S(2)}) async-start(f32[1,128,256]{2,0,1:T(1,128)} %copy.56), calls=%async_computation.9 | async-start | bytes 262144 | tf_op jit(solution)/shard_map/all_to_all | solution.py:117
  171.3 6.2 %copy-start.28 = (f32[1,8,256]{2,1,0:T(8,128)S(1)}, f32[1,8,256]{2,1,0:T(8,128)}, u32[]{:S(2)}) copy-start(f32[1,8,256]{2,1,0:T(8,128)} %copy-done.27) | copy-start | bytes 24580
  171.3 6.1 %collective-permute-start.9 = (f32[1,8,256]{2,1,0:T(8,128)S(1)}, f32[1,8,256]{2,1,0:T(8,128)S(1)}, u32[]{:S(2)}, u32[]{:S(2)}) collective-permute-start(f32[1,8,256]{2,1,0:T(8,128)S(1)} %slice_bitcast_fusion.15), channel_id=1, source_target_pairs={{16,0},{32,16},{48,32},{64,48},{80,64},{96,80},{112,96},{17,1},{33... | collective-permute-start | bytes 24584 | tf_op jit(solution)/shard_map/ppermute | solution.py:12
  177.7 6.0 %collective-permute-start.8 = (f32[16,1,256]{2,1,0:T(1,128)S(1)}, f32[16,1,256]{2,1,0:T(1,128)S(1)}, u32[]{:S(2)}, u32[]{:S(2)}) collective-permute-start(f32[16,1,256]{2,1,0:T(1,128)S(1)} %slice.2223), channel_id=1, source_target_pairs={{1,0},{2,1},{3,2},{4,3},{5,4},{6,5},{7,6},{8,7},{9,8},{10,9},{11,1... | collective-permute-start | bytes 49160 | tf_op jit(solution)/shard_map/ppermute | solution.py:12
  (27 other events, 53.6 us)
where the time goes:
time: 186 us; the launch traced here: 185 us
  starting transfers between devices  82.4 us (44%)
  waiting for transfers between devices  46.4 us (25%)
  other arithmetic  31.3 us (17%)
  local copies, waits for them, and re-layouts  22 us (12%)
  between operations  2.39 us (1%)
    ppermute x10, starting transfers between devices, shifted_2(): return lax.ppermute(array, axis, pairs)  28.9 us
    ppermute x10, waiting for transfers between devices, shifted_2(): return lax.ppermute(array, axis, pairs)  14.6 us
    all_to_all x2, starting transfers between devices, solve_y(): lax.all_to_all(source, 'gy', split_axis=0, concat_axis=1, tiled=True)  10.8 us
    all_to_all x2, starting transfers between devices, along_lines(): lax.all_to_all(solution, 'gy', split_axis=1, concat_axis=0, tiled=True)  10.1 us
    all_to_all x2, starting transfers between devices, along_lines(): lax.all_to_all(solution, 'gx', split_axis=0, concat_axis=1, tiled=True)  9.41 us
    all_to_all x2, starting transfers between devices, solve_x(): lax.all_to_all(source, 'gx', split_axis=1, concat_axis=0, tiled=True)  8.25 us
    all_to_all x2, waiting for transfers between devices, solve_y(): lax.all_to_all(source, 'gy', split_axis=0, concat_axis=1, tiled=True)  8.18 us
    all_to_all x1, starting transfers between devices, solve_x(): lax.all_to_all(stiffness, 'gx', split_axis=1, concat_axis=0, tiled=True)  8.11 us
  transfers between devices with their start and end apart: 20, of which 13 were waited for; matrix products, arithmetic and copies ran while one was open for 19% of the time, Pallas kernels for 0%

commit v1 on v0

v1 whole, which is shorter than its diff:
```python
import jax
import jax.numpy as jnp
from jax import lax
from jax.experimental import pallas as pl
from jax.experimental.pallas import tpu as pltpu
from jax.sharding import PartitionSpec as P

H = 12.0
F32 = jnp.float32


def iota(axis, shape):
    return lax.broadcasted_iota(jnp.int32, shape, axis)


def next_z(v):
    n = v.shape[1]
    return jnp.where(iota(1, v.shape) == n - 1, 0.0, pltpu.roll(v, n - 1, 1))


def prev_z(v):
    return jnp.where(iota(1, v.shape) == 0, 0.0, pltpu.roll(v, 1, 1))


def next_y(v, row):
    n = v.shape[0]
    return jnp.where(iota(0, v.shape) == n - 1, row, pltpu.roll(v, n - 1, 0))


def prev_y(v, row):
    return jnp.where(iota(0, v.shape) == 0, row, pltpu.roll(v, 1, 0))


def strides(n):
    out = []
    s = 1
    while s < n:
        out.append(s)
        s *= 2
    return out


def reduce_factors(a, b, c, axis, store):
    n = a.shape[axis]
    for level, s in enumerate(strides(n)):
        inv = 1.0 / b
        ka = -a * pltpu.roll(inv, s, axis)
        kc = -c * pltpu.roll(inv, n - s, axis)
        store(level, ka, kc)
        b = b + ka * pltpu.roll(c, s, axis) + kc * pltpu.roll(a, n - s, axis)
        a = ka * pltpu.roll(a, s, axis)
        c = kc * pltpu.roll(c, n - s, axis)
    return 1.0 / b


def reduce_apply(r, axis, load, inv):
    n = r.shape[axis]
    for level, s in enumerate(strides(n)):
        ka, kc = load(level)
        r = r + ka * pltpu.roll(r, s, axis) + kc * pltpu.roll(r, n - s, axis)
    return r * inv


def sweep_x(rhs, xf, out):
    nx = len(rhs)
    fwd = [rhs[0]]
    for i in range(1, nx):
        fwd.append(rhs[i] + xf[0, i] * fwd[i - 1])
    u = xf[1, nx - 1] * fwd[nx - 1]
    out[nx - 1] = u
    for i in range(nx - 2, -1, -1):
        u = xf[1, i] * fwd[i] + xf[2, i] * u
        out[i] = u


def interface_factors(coef, own, n, k, weights, consts):
    zero = jnp.zeros_like(own[0])
    bs = []
    ds = []
    B = zero
    for j in range(n - 1):
        al, be, de = coef(j)
        g = be / (1.0 - al * B)
        weights[j] = g
        bs.append(B)
        B = jnp.where(j < k, de + g * be * B, B)
    D = zero
    for j in range(n - 1, 0, -1):
        al, be, de = coef(j)
        g = be / (1.0 - de * D)
        weights[j] = jnp.where(j > k, g, weights[j]) if j < n - 1 else g
        ds.append(D)
        D = jnp.where(j > k, al + g * be * D, D)
    ds.append(zero)
    ds = ds[::-1]
    al, be, de = own
    den = 1.0 / (1.0 - al * B)
    gl = be * den
    bp = de + gl * be * B
    consts[0] = gl * B
    consts[1] = be * D / (1.0 - de * D)
    consts[2] = gl
    consts[3] = bp
    consts[4] = 1.0 / (1.0 - bp * D)
    consts[5] = D
    consts[6] = den
    consts[7] = den * al
    consts[8] = B
    return bs, ds


def to_right(f, l, consts):
    return l + consts[0] * f


def to_left(f, l, consts):
    return f + consts[1] * l


def boundary(A, C, f, l, consts):
    v = (to_right(f, l, consts) + consts[2] * A + consts[3] * C) * consts[4]
    upper = C + consts[5] * v
    first = consts[6] * f + consts[7] * A + consts[2] * upper
    lower = A + consts[8] * first
    return lower, upper


def gather_sums(recv, weights, n, k):
    A = jnp.zeros_like(recv[0])
    for j in range(n - 1):
        A = jnp.where(j < k, recv[j] + weights[j] * A, A)
    C = jnp.zeros_like(A)
    for j in range(n - 1, 0, -1):
        C = jnp.where(j > k, recv[j] + weights[j] * C, C)
    return A, C


def fill_send(send, f, l, consts, n, k):
    right = to_right(f, l, consts)
    left = to_left(f, l, consts)
    for j in range(n):
        send[j] = jnp.where(j > k, right, left)


def coef_kernel(nxd, nyd, mat, perm, cond, dm, cp, yk, yib, phy, psy, xf, phx, psx, cy, cx, sendy):
    kx = lax.axis_index("gx")
    ky = lax.axis_index("gy")
    nx, ny, nz = mat.shape
    row = iota(0, (ny, nz))
    for x in range(nx):
        m = mat[x]
        eps = jnp.full(m.shape, perm[0], F32)
        sig = jnp.full(m.shape, cond[0], F32)
        for t in range(1, perm.shape[0]):
            eps = jnp.where(m == t, perm[t], eps)
            sig = jnp.where(m == t, cond[t], sig)
        ea = eps / H
        sh = sig * 0.5
        inv = 1.0 / (ea + sh)
        cp[x] = inv
        dm[x] = (ea - sh) * inv
        s = H * inv
        first = row == 0
        last = row == ny - 1
        a = jnp.where(first, 0.0, -s)
        c = jnp.where(last, 0.0, -s)
        edge = jnp.where(ky == 0, 1.0, 2.0)
        b = 1.0 + s * jnp.where(first, edge, 2.0)

        def store(level, ka, kc):
            yk[2 * level, x] = ka
            yk[2 * level + 1, x] = kc

        def load(level):
            return yk[2 * level, x], yk[2 * level + 1, x]

        ib = reduce_factors(a, b, c, 0, store)
        yib[x] = ib
        lo = reduce_apply(jnp.where(first, jnp.where(ky == 0, 0.0, s), 0.0), 0, load, ib)
        up = reduce_apply(jnp.where(last, jnp.where(ky == nyd - 1, 0.0, s), 0.0), 0, load, ib)
        phy[x] = lo
        psy[x] = up
        cy[0, x:x + 1] = lo[0:1]
        cy[1, x:x + 1] = up[0:1]
        cy[2, x:x + 1] = up[ny - 1:ny]
    for j in range(nyd):
        sendy[j] = cy[...]
    s = H * cp[0]
    d = 1.0 + s * jnp.where(kx == 0, 1.0, 2.0)
    r = jnp.where(kx == 0, 0.0, s)
    phx[0] = r
    xf[0, 0] = jnp.zeros_like(s)
    for x in range(nx):
        e = 1.0 / d
        xf[1, x] = e
        xf[2, x] = s * e
        if x < nx - 1:
            sn = H * cp[x + 1]
            p = sn * e
            xf[0, x + 1] = p
            d = 1.0 + 2.0 * sn - p * s
            r = p * r
            phx[x + 1] = r
            s = sn
    u = xf[1, nx - 1] * r
    w = jnp.where(kx == nxd - 1, 0.0, xf[2, nx - 1])
    phx[nx - 1] = u
    psx[nx - 1] = w
    cx[2] = w
    for x in range(nx - 2, -1, -1):
        u = xf[1, x] * phx[x] + xf[2, x] * u
        w = xf[2, x] * w
        phx[x] = u
        psx[x] = w
    cx[0] = u
    cx[1] = w


def zfactor_kernel(cp, zk, zib):
    nx, ny, nz = cp.shape
    lane = iota(1, (ny, nz))
    for x in range(nx):
        s = H * cp[x]
        a = jnp.where(lane == 0, 0.0, -s)
        c = jnp.where(lane == nz - 1, 0.0, -s)
        b = 1.0 + s * jnp.where(lane == 0, 1.0, 2.0)

        def store(level, ka, kc):
            zk[2 * level, x] = ka
            zk[2 * level + 1, x] = kc

        zib[x] = reduce_factors(a, b, c, 1, store)


def z_load(zk, x):
    return lambda level: (zk[2 * level, x], zk[2 * level + 1, x])


def chain_x_kernel(el, mg, dm, cp, yk, yib, e1_up, iz_out, up_out, f_out, l_out):
    nx, ny, nz = dm.shape
    for x in range(nx):
        above = el[1, x + 1] if x < nx - 1 else e1_up[0]
        iz = mg[2, x] - H * (above - el[1, x])
        iz_out[x] = iz
        h1 = mg[1, x]
        rhs = dm[x] * el[0, x] + cp[x] * ((iz - prev_y(iz, 0.0)) - (h1 - prev_z(h1)))
        u = reduce_apply(rhs, 0, z_load(yk, x), yib[x])
        up_out[x] = u
        f_out[x:x + 1] = u[0:1]
        l_out[x:x + 1] = u[ny - 1:ny] - iz[ny - 1:ny] * (1.0 / H)


def chain_z_kernel(nxd, el, mg, dm, cp, xf, cx, h0_low, iy_out, up_out, send):
    nx, ny, nz = dm.shape
    rhs = []
    below = jnp.zeros((ny, nz), F32)
    for x in range(nx):
        e0 = el[0, x]
        iy = mg[1, x] - H * (next_z(e0) - e0)
        iy_out[x] = iy
        h0 = mg[0, x]
        rhs.append(dm[x] * el[2, x] + cp[x] * ((iy - below) - (h0 - prev_y(h0, h0_low[x]))))
        below = iy
    sweep_x(rhs, xf, up_out)
    f = up_out[0]
    l = up_out[nx - 1] - below * (1.0 / H)
    for j in range(nxd):
        send[j, 0] = cx[0]
        send[j, 1] = cx[1]
        send[j, 2] = cx[2]
        send[j, 3] = f
        send[j, 4] = l


def center_y_kernel(el, mg, dm, cp, zk, zib, e2_up, h2_low, sx_out, t1_out):
    nx, ny, nz = dm.shape
    for x in range(nx):
        e2 = el[2, x]
        ix = mg[0, x] - H * (next_y(e2, e2_up[x]) - e2)
        below = mg[2, x - 1] if x > 0 else h2_low[0]
        rhs = dm[x] * el[1, x] + cp[x] * ((ix - prev_z(ix)) - (mg[2, x] - below))
        cy = reduce_apply(rhs, 1, z_load(zk, x), zib[x])
        curl = H * (next_z(cy) - cy)
        mx = ix + curl
        sx_out[x] = mx + curl
        t1_out[x] = dm[x] * cy + cp[x] * (mx - prev_z(mx))


def scan_y_kernel(recv, own, f, l, weights, consts, send):
    ky = lax.axis_index("gy")
    n = recv.shape[0]
    interface_factors(lambda j: (recv[j, 0], recv[j, 1], recv[j, 2]), (own[0], own[1], own[2]), n, ky, weights, consts)
    fill_send(send, f[...], l[...], consts, n, ky)


def half_x_kernel(recv, weights, consts, f, l, up, iz, t1, dm, cp, phy, psy, xf, sz_out, t4_out, ufy_out, f_out, l_out, edge):
    ky = lax.axis_index("gy")
    nx, ny, nz = dm.shape
    n = recv.shape[0]
    A, C = gather_sums(recv, weights, n, ky)
    lower, upper = boundary(A, C, f[...], l[...], consts)
    edge[0] = lower
    edge[1] = upper
    rhs = []
    below = jnp.zeros((ny, nz), F32)
    for x in range(nx):
        lo = edge[0, x:x + 1]
        hi = edge[1, x:x + 1]
        cx = up[x] + phy[x] * lo + psy[x] * hi
        curl = H * (next_y(cx, hi) - cx)
        mz = iz[x] + curl
        sz = mz + curl
        sz_out[x] = sz
        mlow = jnp.where(ky == 0, 0.0, H * (cx[0:1] - lo))
        t4_out[x] = dm[x] * cx + cp[x] * (mz - prev_y(mz, mlow))
        rhs.append(t1[x] - cp[x] * (sz - below))
        below = sz
    sweep_x(rhs, xf, ufy_out)
    f_out[...] = ufy_out[0]
    l_out[...] = ufy_out[nx - 1] + below * (1.0 / H)


def scan_x_kernel(recv, own, f1, l1, f2, l2, weights, consts, edge, send):
    kx = lax.axis_index("gx")
    n = recv.shape[0]
    bs, ds = interface_factors(lambda j: (recv[j, 0], recv[j, 1], recv[j, 2]), (own[0], own[1], own[2]), n, kx, weights, consts)
    fill_send(send, f2[...], l2[...], consts, n, kx)
    A = jnp.zeros(f1.shape, F32)
    for j in range(n - 1):
        A = jnp.where(j < kx, recv[j, 4] + weights[j] * (A + bs[j] * recv[j, 3]), A)
    C = jnp.zeros(f1.shape, F32)
    for j in range(n - 1, 0, -1):
        C = jnp.where(j > kx, recv[j, 3] + weights[j] * (C + ds[j] * recv[j, 4]), C)
    lower, upper = boundary(A, C, f1[...], l1[...], consts)
    edge[0] = lower
    edge[1] = upper


def half_z_kernel(edge, up, iy, sx, dm, cp, phx, psx, yk, yib, consts_y, sy_out, ufz_out, f_out, l_out, send):
    kx = lax.axis_index("gx")
    ky = lax.axis_index("gy")
    nx, ny, nz = dm.shape
    lower = edge[0]
    upper = edge[1]
    cz = up[0] + phx[0] * lower + psx[0] * upper
    below = jnp.where(kx == 0, 0.0, H * (cz - lower))
    for x in range(nx):
        cn = up[x + 1] + phx[x + 1] * lower + psx[x + 1] * upper if x < nx - 1 else upper
        curl = H * (cn - cz)
        my = iy[x] + curl
        sy_out[x] = my + curl
        s = sx[x]
        rhs = dm[x] * cz + cp[x] * ((my - below) - (s - prev_y(s, 0.0)))
        u = reduce_apply(rhs, 0, z_load(yk, x), yib[x])
        ufz_out[x] = u
        f_out[x:x + 1] = u[0:1]
        l_out[x:x + 1] = u[ny - 1:ny] + s[ny - 1:ny] * (1.0 / H)
        cz = cn
        below = my
    fill_send(send, f_out[...], l_out[...], consts_y, send.shape[0], ky)


def final_x_kernel(t4, sy, cp, zk, zib, fx_out, my_out):
    nx, ny, nz = cp.shape
    for x in range(nx):
        s = sy[x]
        fx = reduce_apply(t4[x] - cp[x] * (s - prev_z(s)), 1, z_load(zk, x), zib[x])
        fx_out[x] = fx
        my_out[x] = s - H * (next_z(fx) - fx)


def final_y_kernel(recv, weights, consts, f, l, up, sz, phx, psx, fy_out, mz_out):
    kx = lax.axis_index("gx")
    nx = up.shape[0]
    A, C = gather_sums(recv, weights, recv.shape[0], kx)
    lower, upper = boundary(A, C, f[...], l[...], consts)
    fy = up[0] + phx[0] * lower + psx[0] * upper
    for x in range(nx):
        fn = up[x + 1] + phx[x + 1] * lower + psx[x + 1] * upper if x < nx - 1 else upper
        fy_out[x] = fy
        mz_out[x] = sz[x] - H * (fn - fy)
        fy = fn


def final_z_kernel(recv, weights, consts, f, l, up, sx, phy, psy, fx, fy, my, mz, e_out, h_out, edge):
    ky = lax.axis_index("gy")
    nx = up.shape[0]
    A, C = gather_sums(recv, weights, recv.shape[0], ky)
    lower, upper = boundary(A, C, f[...], l[...], consts)
    edge[0] = lower
    edge[1] = upper
    for x in range(nx):
        lo = edge[0, x:x + 1]
        hi = edge[1, x:x + 1]
        fz = up[x] + phy[x] * lo + psy[x] * hi
        e_out[0, x] = fx[x]
        e_out[1, x] = fy[x]
        e_out[2, x] = fz
        h_out[0, x] = sx[x] - H * (next_y(fz, hi) - fz)
        h_out[1, x] = my[x]
        h_out[2, x] = mz[x]


def vmem():
    return pl.BlockSpec(memory_space=pltpu.VMEM)


def call(kernel, outs, *args, smem=(), scratch=(), name=None):
    specs = [pl.BlockSpec(memory_space=pltpu.SMEM) if i in smem else vmem() for i in range(len(args))]
    nbytes = sum(a.size * 4 for a in args) + sum(4 * _size(o) for o in outs)
    return pl.pallas_call(
        kernel,
        out_shape=[jax.ShapeDtypeStruct(o, F32) for o in outs],
        in_specs=specs,
        out_specs=[vmem() for _ in outs],
        scratch_shapes=list(scratch),
        cost_estimate=pl.CostEstimate(flops=4 * nbytes, bytes_accessed=nbytes, transcendentals=0),
        compiler_params=pltpu.CompilerParams(vmem_limit_bytes=40 << 20),
        name=name,
    )(*args)


def _size(shape):
    n = 1
    for d in shape:
        n *= d
    return n


def shifted(array, axis, by):
    count = lax.axis_size(axis)
    return lax.ppermute(array, axis, [(i, i + by) for i in range(count) if 0 <= i + by < count])


def exchange(array, axis):
    return lax.all_to_all(array, axis, 0, 0)


def per_device(electric, magnetic, material, permittivity, conductivity):
    nxd = lax.axis_size("gx")
    nyd = lax.axis_size("gy")
    cell = material.shape
    nx, ny, nz = cell
    py = (nx, nz)
    px = (ny, nz)

    def bind(kernel, *lead):
        def body(*refs):
            kernel(*lead, *refs)
        return body

    dm, cp, yk, yib, phy, psy, xf, phx, psx, cy, cx, sendy = call(
        bind(coef_kernel, nxd, nyd),
        [cell, cell, (2 * len(strides(ny)),) + cell, cell, cell, cell, (3,) + cell, cell, cell,
         (3,) + py, (3,) + px, (nyd, 3) + py],
        material, permittivity, conductivity, smem=(1, 2), name="coef")
    recv_cy = exchange(sendy, "gy")

    e1_up = shifted(electric[1, 0:1], "gx", -1)
    h0_low = shifted(magnetic[0, :, ny - 1:ny], "gy", 1)
    e2_up = shifted(electric[2, :, 0:1], "gy", -1)
    h2_low = shifted(magnetic[2, nx - 1:nx], "gx", 1)

    zk, zib = call(zfactor_kernel, [(2 * len(strides(nz)),) + cell, cell], cp, name="zfactor")
    iz, ux, fx1, lx1 = call(chain_x_kernel, [cell, cell, py, py], electric, magnetic, dm, cp, yk, yib, e1_up, name="chain_x")
    wy, ky, send = call(scan_y_kernel, [(nyd,) + py, (9,) + py, (nyd,) + py], recv_cy, cy, fx1, lx1, name="scan_y")
    recv1 = exchange(send, "gy")

    iy, uz, sendx = call(bind(chain_z_kernel, nxd), [cell, cell, (nxd, 5) + px], electric, magnetic, dm, cp, xf, cx, h0_low, name="chain_z")
    recv2 = exchange(sendx, "gx")
    sx, t1 = call(center_y_kernel, [cell, cell], electric, magnetic, dm, cp, zk, zib, e2_up, h2_low, name="center_y")

    sz, t4, ufy, f3, l3 = call(half_x_kernel, [cell, cell, cell, px, px],
                               recv1, wy, ky, fx1, lx1, ux, iz, t1, dm, cp, phy, psy, xf,
                               scratch=[pltpu.VMEM((2,) + py, F32)], name="half_x")
    fz2 = sendx[0, 3]
    lz2 = sendx[0, 4]
    wx, kx, edge2, send3 = call(scan_x_kernel, [(nxd,) + px, (9,) + px, (2,) + px, (nxd,) + px],
                                recv2, cx, fz2, lz2, f3, l3, name="scan_x")
    recv3 = exchange(send3, "gx")
    sy, ufz, f4, l4, send4 = call(half_z_kernel, [cell, cell, py, py, (nyd,) + py],
                                  edge2, uz, iy, sx, dm, cp, phx, psx, yk, yib, ky, name="half_z")
    recv4 = exchange(send4, "gy")
    fx, my = call(final_x_kernel, [cell, cell], t4, sy, cp, zk, zib, name="final_x")
    fy, mz = call(final_y_kernel, [cell, cell], recv3, wx, kx, f3, l3, ufy, sz, phx, psx, name="final_y")
    e, h = call(final_z_kernel, [(3,) + cell, (3,) + cell],
                recv4, wy, ky, f4, l4, ufz, sx, phy, psy, fx, fy, my, mz,
                scratch=[pltpu.VMEM((2,) + py, F32)], name="final_z")
    return e, h


def solution(mesh):
    return jax.shard_map(
        per_device,
        mesh=mesh,
        in_specs=(
            P(None, "gx", "gy", None),
            P(None, "gx", "gy", None),
            P("gx", "gy", None),
            P(),
            P(),
        ),
        out_specs=(P(None, "gx", "gy", None), P(None, "gx", "gy", None)),
        check_vma=False,
    )
```

time: 186 us -> 115 us (0.62)
  waiting for transfers between devices: 46.4 us -> 7.17 us
  starting transfers between devices: 82.4 us -> 43.5 us
  other arithmetic: 31.3 us -> 0 us
  local copies, waits for them, and re-layouts: 22 us -> 47.5 us
  Pallas kernels: 0 us -> 14.3 us
    unnamed x82 -> x160, local copies, waits for them, and re-layouts: 5.88 us -> 44.8 us
    all_to_all x10 -> x5, waiting for transfers between devices: 31.8 us -> 1.92 us  [exchange(): return lax.all_to_all(array, axis, 0, 0)]
    all_to_all x10 -> x5, starting transfers between devices: 53.5 us -> 31.9 us  [exchange(): return lax.all_to_all(array, axis, 0, 0)]
    ppermute x10 -> x4, starting transfers between devices: 28.9 us -> 11.6 us  [shifted(): lax.ppermute(array, axis, [(i, i + by) for i in range(count) if 0 <= i +...]
    another operation x84 -> x0, other arithmetic: 14.8 us -> none  [the longest x68 7.77 us: reduce_level(): jnp.stack([factor_below * preceding[0], system[1] + factor_below * preced...]
    pallas_call x0 -> x12, Pallas kernels: none -> 14.3 us  [call(): pl.pallas_call(kernel, out_shape=[jax.ShapeDtypeStruct(o, F32) for o in o...]
    add x42 -> x0, other arithmetic: 12.6 us -> none  [the longest x36 5.42 us: reduce_level(): system[1] + factor_below * preceding[2] + factor_above * following[0]]
    ppermute x10 -> x4, waiting for transfers between devices: 14.6 us -> 5.25 us  [shifted(): lax.ppermute(array, axis, [(i, i + by) for i in range(count) if 0 <= i +...]
  transfers between devices with their start and end apart: 20 -> 9, of which waited for: 13 -> 2; matrix products, arithmetic and copies ran while one was open for 19% -> 2% of each run, Pallas kernels for 0% -> 9%
where the time goes in v1:
time: 115 us; the launch traced here: 114 us
  local copies, waits for them, and re-layouts  47.5 us (41%)
  starting transfers between devices  43.5 us (38%)
  Pallas kernels  14.3 us (12%)
  waiting for transfers between devices  7.17 us (6%)
    unnamed x160, local copies, waits for them, and re-layouts  44.8 us
    all_to_all x5, starting transfers between devices, exchange(): return lax.all_to_all(array, axis, 0, 0)  31.9 us
    pallas_call x12, Pallas kernels, call(): pl.pallas_call(kernel, out_shape=[jax.ShapeDtypeStruct(o, F32) for o in o...  14.3 us
    ppermute x4, starting transfers between devices, shifted(): lax.ppermute(array, axis, [(i, i + by) for i in range(count) if 0 <= i +...  11.6 us
    ppermute x4, waiting for transfers between devices, shifted(): lax.ppermute(array, axis, [(i, i + by) for i in range(count) if 0 <= i +...  5.25 us
  transfers between devices with their start and end apart: 9, of which 2 were waited for; matrix products, arithmetic and copies ran while one was open for 2% of the time, Pallas kernels for 9%

profile of v1, /device:TPU:1, one launch (start us, length us, event | category | flops | bytes accessed | tf_op | source)
XLA Modules:
  0.0 113.6 jit_solution(4268132682771831170)
XLA Ops:
  2.8 1.3 %coef.1 = (f32[16,8,256]{2,1,0:T(8,128)S(1)}, f32[16,8,256]{2,1,0:T(8,128)S(1)}, f32[6,16,8,256]{3,2,1,0:T(8,128)S(1)}, f32[16,8,256]{2,1,0:T(8,128)S(1)}, f32[1...) custom-call(s32[16,8,256]{2,1,0:T(8,128)S(1)} %copy-done.40, ...), custom_call_target="tpu_custom_call" | custom-call | flops 12353792 | bytes 3088448 | tf_op jit(solution)/shard_map/coef/pallas_call | solution.py:411
  7.6 7.3 %all-to-all-start.1 = ((f32[16,3,16,256]{3,2,1,0:T(8,128)}), f32[16,3,16,256]{3,2,1,0:T(8,128)S(1)}, u32[]{:S(2)}, u32[]{:S(2)}) async-start(f32[16,3,16,256]{3,2,1,0:T(8,128)} %copy-done.15), calls=%async_computation.1 | async-start | bytes 1572864 | tf_op jit(solution)/shard_map/all_to_all | solution.py:436
  15.6 1.3 %collective-permute-start.1 = (f32[1,8,256]{2,1,0:T(8,128)S(1)}, f32[1,8,256]{2,1,0:T(8,128)S(1)}, u32[]{:S(2)}, u32[]{:S(2)}) collective-permute-start(f32[1,8,256]{2,1,0:T(8,128)S(1)} %slice_bitcast_fusion.3), channel_id=1, source_target_pairs={{16,0},{32,16},{48,32},{64,48},{80,64},{96,80},{112,96},{17,1},{33... | collective-permute-start | bytes 24584 | tf_op jit(solution)/shard_map/ppermute | solution.py:432
  16.9 5.2 %collective-permute-done.1.e1_up = f32[1,8,256]{2,1,0:T(8,128)S(1)} collective-permute-done((f32[1,8,256]{2,1,0:T(8,128)S(1)}, f32[1,8,256]{2,1,0:T(8,128)S(1)}, u32[]{:S(2)}, u32[]{:S(2)}) %collective-permute-start.1) | collective-permute-done | bytes 8224 | tf_op jit(solution)/shard_map/ppermute | solution.py:432
  22.2 1.0 copy-done
  23.2 1.0 copy-done.2
  25.7 1.9 %all-to-all-done.1.recv = f32[16,3,16,256]{3,2,1,0:T(8,128)S(1)} async-done(((f32[16,3,16,256]{3,2,1,0:T(8,128)}), f32[16,3,16,256]{3,2,1,0:T(8,128)S(1)}, u32[]{:S(2)}, u32[]{:S(2)}) %all-to-all-start.1) | async-done | bytes 786464 | tf_op jit(solution)/shard_map/all_to_all | solution.py:436
  27.6 1.0 scan_y.1
  29.2 8.8 %all-to-all-start.2 = ((f32[16,16,256]{2,1,0:T(8,128)}), f32[16,16,256]{2,1,0:T(8,128)S(1)}, u32[]{:S(2)}, u32[]{:S(2)}) async-start(f32[16,16,256]{2,1,0:T(8,128)} %get-tuple-element.57), calls=%async_computation.2 | async-start | bytes 524288 | tf_op jit(solution)/shard_map/all_to_all | solution.py:436
  38.1 3.5 %collective-permute-start = (f32[16,1,256]{2,1,0:T(1,128)S(1)}, f32[16,1,256]{2,1,0:T(1,128)S(1)}, u32[]{:S(2)}, u32[]{:S(2)}) collective-permute-start(f32[16,1,256]{2,1,0:T(1,128)S(1)} %slice_bitcast_fusion.1), channel_id=1, source_target_pairs={{0,1},{1,2},{2,3},{3,4},{4,5},{5,6},{6,7},{7,8},{8,9},{9,10},{10,1... | collective-permute-start | bytes 49160 | tf_op jit(solution)/shard_map/ppermute | solution.py:432
  42.2 1.9 %collective-permute-start.2 = (f32[16,1,256]{2,1,0:T(1,128)}, f32[16,1,256]{2,1,0:T(1,128)}, u32[]{:S(2)}, u32[]{:S(2)}) collective-permute-start(f32[16,1,256]{2,1,0:T(1,128)} %slice_bitcast_fusion), channel_id=1, source_target_pairs={{1,0},{2,1},{3,2},{4,3},{5,4},{6,5},{7,6},{8,7},{9,8},{10,9},{11,1... | collective-permute-start | bytes 49160 | tf_op jit(solution)/shard_map/ppermute | solution.py:432
  46.4 4.2 %all-to-all-start = ((f32[8,5,8,256]{3,2,1,0:T(8,128)}), f32[8,5,8,256]{3,2,1,0:T(8,128)}, u32[]{:S(2)}, u32[]{:S(2)}) async-start(f32[8,5,8,256]{3,2,1,0:T(8,128)} %get-tuple-element.50), calls=%async_computation | async-start | bytes 655360 | tf_op jit(solution)/shard_map/all_to_all | solution.py:436
  50.6 4.9 %collective-permute-start.3 = (f32[1,8,256]{2,1,0:T(8,128)S(1)}, f32[1,8,256]{2,1,0:T(8,128)S(1)}, u32[]{:S(2)}, u32[]{:S(2)}) collective-permute-start(f32[1,8,256]{2,1,0:T(8,128)S(1)} %slice_bitcast_fusion.2), channel_id=1, source_target_pairs={{0,16},{16,32},{32,48},{48,64},{64,80},{80,96},{96,112},{1,17},{17... | collective-permute-start | bytes 24584 | tf_op jit(solution)/shard_map/ppermute | solution.py:432
  55.5 4.9 %zfactor.1 = (f32[16,16,8,256]{3,2,1,0:T(8,128)S(1)}, f32[16,8,256]{2,1,0:T(8,128)S(1)}) custom-call(f32[16,8,256]{2,1,0:T(8,128)S(1)} %get-tuple-element.47.refs_3_.cp), custom_call_target="tpu_custom_call" | custom-call | flops 9437184 | bytes 2359296 | tf_op jit(solution)/shard_map/zfactor/pallas_call | solution.py:411
  60.4 1.7 %center_y.1 = (f32[16,8,256]{2,1,0:T(8,128)S(1)}, f32[16,8,256]{2,1,0:T(8,128)S(1)}) custom-call(f32[3,16,8,256]{3,2,1,0:T(8,128)S(1)} %copy-done.1, f32[3,16,8,256]{3,2,1,0:T(8,128)S(1)} %copy-done.3, f32[16,8,256]{2,1,0:T(8,128)S(1)} %get-tuple-element.46.refs_2_.dm, f32[16,8,256]{2,1,0:T(8,128)S(1)} %get-tuple-element.47.refs_3_.cp, ...), custom_call_target="tpu_custom_call" | custom-call | flops 14254080 | bytes 3563520 | tf_op jit(solution)/shard_map/center_y/pallas_call | solution.py:411
  62.8 1.4 %slice_bitcast_fusion.4 = (f32[8,256]{1,0:T(8,128)}, f32[8,256]{1,0:T(8,128)}) fusion(f32[8,5,8,256]{3,2,1,0:T(8,128)} %get-tuple-element.50), kind=kLoop, calls=%fused_computation.4 | loop fusion | bytes 32768 | tf_op jit(solution)/shard_map/squeeze | solution.py:477
  65.1 0.9 copy-done.25
  66.0 0.9 copy-done.28
  66.9 0.9 copy-done.52
  67.8 0.9 copy-done.54
  75.6 1.1 scan_x.1
  78.6 4.6 %all-to-all-start.4 = ((f32[8,8,256]{2,1,0:T(8,128)}), f32[8,8,256]{2,1,0:T(8,128)}, u32[]{:S(2)}, u32[]{:S(2)}) async-start(f32[8,8,256]{2,1,0:T(8,128)} %copy-done.63), calls=%async_computation.4 | async-start | bytes 131072 | tf_op jit(solution)/shard_map/all_to_all | solution.py:436
  84.1 0.9 copy-done.19
  85.0 0.9 copy-done.22
  85.9 0.9 copy-done.31
  87.7 0.9 copy-done.48
  93.7 7.1 %all-to-all-start.3 = ((f32[16,16,256]{2,1,0:T(8,128)}), f32[16,16,256]{2,1,0:T(8,128)S(1)}, u32[]{:S(2)}, u32[]{:S(2)}) async-start(f32[16,16,256]{2,1,0:T(8,128)} %copy-done.35), calls=%async_computation.3 | async-start | bytes 524288 | tf_op jit(solution)/shard_map/all_to_all | solution.py:436
  106.2 0.9 copy-done.42
  107.1 0.9 copy-done.44
  108.0 0.9 final_y.1
  109.9 0.9 copy-done.29
  112.6 1.0 final_z.1
  (163 shorter events, 36.6 us)
Async XLA Ops:
  7.6 20.0 %copy-start.33 = (f32[16,8,256]{2,1,0:T(8,128)}, f32[16,8,256]{2,1,0:T(8,128)S(1)}, u32[]{:S(2)}) copy-start(f32[16,8,256]{2,1,0:T(8,128)S(1)} %get-tuple-element.54.yib) | copy-start | bytes 393220
  7.6 21.0 %copy-start.4 = (f32[6,16,8,256]{3,2,1,0:T(8,128)}, f32[6,16,8,256]{3,2,1,0:T(8,128)S(1)}, u32[]{:S(2)}) copy-start(f32[6,16,8,256]{3,2,1,0:T(8,128)S(1)} %get-tuple-element.53.yk) | copy-start | bytes 2359300
  7.6 36.5 %copy-start.55 = (f32[3,8,256]{2,1,0:T(8,128)}, f32[3,8,256]{2,1,0:T(8,128)S(1)}, u32[]{:S(2)}) copy-start(f32[3,8,256]{2,1,0:T(8,128)S(1)} %get-tuple-element.49.refs_5_.own) | copy-start | bytes 73732
  7.6 30.4 %copy-start.3 = (f32[3,16,8,256]{3,2,1,0:T(8,128)S(1)}, f32[3,16,8,256]{3,2,1,0:T(8,128)}, u32[]{:S(2)}) copy-start(f32[3,16,8,256]{3,2,1,0:T(8,128)} %mg.3) | copy-start | bytes 1179652
  7.6 34.0 %copy-start.1 = (f32[3,16,8,256]{3,2,1,0:T(8,128)S(1)}, f32[3,16,8,256]{3,2,1,0:T(8,128)}, u32[]{:S(2)}) copy-start(f32[3,16,8,256]{3,2,1,0:T(8,128)} %el.3) | copy-start | bytes 1179652
  7.6 20.0 %all-to-all-start.1 = ((f32[16,3,16,256]{3,2,1,0:T(8,128)}), f32[16,3,16,256]{3,2,1,0:T(8,128)S(1)}, u32[]{:S(2)}, u32[]{:S(2)}) async-start(f32[16,3,16,256]{3,2,1,0:T(8,128)} %copy-done.15), calls=%async_computation.1 | async-start | bytes 1572864 | tf_op jit(solution)/shard_map/all_to_all | solution.py:436
  15.6 6.5 %collective-permute-start.1 = (f32[1,8,256]{2,1,0:T(8,128)S(1)}, f32[1,8,256]{2,1,0:T(8,128)S(1)}, u32[]{:S(2)}, u32[]{:S(2)}) collective-permute-start(f32[1,8,256]{2,1,0:T(8,128)S(1)} %slice_bitcast_fusion.3), channel_id=1, source_target_pairs={{16,0},{32,16},{48,32},{64,48},{80,64},{96,80},{112,96},{17,1},{33... | collective-permute-start | bytes 24584 | tf_op jit(solution)/shard_map/ppermute | solution.py:432
  22.2 1.0 copy-start
  23.2 1.0 copy-start.2
  25.7 24.9 %copy-start.59 = (f32[16,256]{1,0:T(8,128)}, f32[16,256]{1,0:T(8,128)S(1)}, u32[]{:S(2)}) copy-start(f32[16,256]{1,0:T(8,128)S(1)} %get-tuple-element.56.l) | copy-start | bytes 49156
  29.2 21.3 %copy-start.12 = (f32[16,16,256]{2,1,0:T(8,128)}, f32[16,16,256]{2,1,0:T(8,128)S(1)}, u32[]{:S(2)}) copy-start(f32[16,16,256]{2,1,0:T(8,128)S(1)} %get-tuple-element.58.weights) | copy-start | bytes 786436
  29.2 17.1 %all-to-all-start.2 = ((f32[16,16,256]{2,1,0:T(8,128)}), f32[16,16,256]{2,1,0:T(8,128)S(1)}, u32[]{:S(2)}, u32[]{:S(2)}) async-start(f32[16,16,256]{2,1,0:T(8,128)} %get-tuple-element.57), calls=%async_computation.2 | async-start | bytes 524288 | tf_op jit(solution)/shard_map/all_to_all | solution.py:436
  38.1 6.1 %collective-permute-start = (f32[16,1,256]{2,1,0:T(1,128)S(1)}, f32[16,1,256]{2,1,0:T(1,128)S(1)}, u32[]{:S(2)}, u32[]{:S(2)}) collective-permute-start(f32[16,1,256]{2,1,0:T(1,128)S(1)} %slice_bitcast_fusion.1), channel_id=1, source_target_pairs={{0,1},{1,2},{2,3},{3,4},{4,5},{5,6},{6,7},{7,8},{8,9},{9,10},{10,1... | collective-permute-start | bytes 49160 | tf_op jit(solution)/shard_map/ppermute | solution.py:432
  42.2 18.2 %collective-permute-start.2 = (f32[16,1,256]{2,1,0:T(1,128)}, f32[16,1,256]{2,1,0:T(1,128)}, u32[]{:S(2)}, u32[]{:S(2)}) collective-permute-start(f32[16,1,256]{2,1,0:T(1,128)} %slice_bitcast_fusion), channel_id=1, source_target_pairs={{1,0},{2,1},{3,2},{4,3},{5,4},{6,5},{7,6},{8,7},{9,8},{10,9},{11,1... | collective-permute-start | bytes 49160 | tf_op jit(solution)/shard_map/ppermute | solution.py:432
  46.4 4.2 %copy-start.10 = (f32[16,16,256]{2,1,0:T(8,128)}, f32[16,16,256]{2,1,0:T(8,128)S(1)}, u32[]{:S(2)}) copy-start(f32[16,16,256]{2,1,0:T(8,128)S(1)} %all-to-all-done.2.recv) | copy-start | bytes 786436
  46.4 25.7 %all-to-all-start = ((f32[8,5,8,256]{3,2,1,0:T(8,128)}), f32[8,5,8,256]{3,2,1,0:T(8,128)}, u32[]{:S(2)}, u32[]{:S(2)}) async-start(f32[8,5,8,256]{3,2,1,0:T(8,128)} %get-tuple-element.50), calls=%async_computation | async-start | bytes 655360 | tf_op jit(solution)/shard_map/all_to_all | solution.py:436
  50.6 9.8 %collective-permute-start.3 = (f32[1,8,256]{2,1,0:T(8,128)S(1)}, f32[1,8,256]{2,1,0:T(8,128)S(1)}, u32[]{:S(2)}, u32[]{:S(2)}) collective-permute-start(f32[1,8,256]{2,1,0:T(8,128)S(1)} %slice_bitcast_fusion.2), channel_id=1, source_target_pairs={{0,16},{16,32},{32,48},{48,64},{64,80},{80,96},{96,112},{1,17},{17... | collective-permute-start | bytes 24584 | tf_op jit(solution)/shard_map/ppermute | solution.py:432
  55.5 8.7 %copy-start.11 = (f32[16,16,256]{2,1,0:T(8,128)S(1)}, f32[16,16,256]{2,1,0:T(8,128)}, u32[]{:S(2)}) copy-start(f32[16,16,256]{2,1,0:T(8,128)} %copy-done.10) | copy-start | bytes 786436
  55.5 8.7 %copy-start.13 = (f32[16,16,256]{2,1,0:T(8,128)S(1)}, f32[16,16,256]{2,1,0:T(8,128)}, u32[]{:S(2)}) copy-start(f32[16,16,256]{2,1,0:T(8,128)} %copy-done.12) | copy-start | bytes 786436
  55.5 8.7 %copy-start.60 = (f32[16,256]{1,0:T(8,128)S(1)}, f32[16,256]{1,0:T(8,128)}, u32[]{:S(2)}) copy-start(f32[16,256]{1,0:T(8,128)} %copy-done.59) | copy-start | bytes 49156
  60.4 3.8 %copy-start.16 = (f32[16,8,256]{2,1,0:T(8,128)}, f32[16,8,256]{2,1,0:T(8,128)S(1)}, u32[]{:S(2)}) copy-start(f32[16,8,256]{2,1,0:T(8,128)S(1)} %get-tuple-element.63.zib) | copy-start | bytes 393220
  62.8 20.4 %copy-start.5 = (f32[6,16,8,256]{3,2,1,0:T(8,128)S(1)}, f32[6,16,8,256]{3,2,1,0:T(8,128)}, u32[]{:S(2)}) copy-start(f32[6,16,8,256]{3,2,1,0:T(8,128)} %copy-done.4) | copy-start | bytes 2359300
  78.6 4.6 %copy-start.61 = (f32[8,8,256]{2,1,0:T(8,128)}, f32[8,8,256]{2,1,0:T(8,128)S(1)}, u32[]{:S(2)}) copy-start(f32[8,8,256]{2,1,0:T(8,128)S(1)} %get-tuple-element.83.weights) | copy-start | bytes 196612
  78.6 15.1 %all-to-all-start.4 = ((f32[8,8,256]{2,1,0:T(8,128)}), f32[8,8,256]{2,1,0:T(8,128)}, u32[]{:S(2)}, u32[]{:S(2)}) async-start(f32[8,8,256]{2,1,0:T(8,128)} %copy-done.63), calls=%async_computation.4 | async-start | bytes 131072 | tf_op jit(solution)/shard_map/all_to_all | solution.py:436
  90.2 14.1 %copy-start.66 = (f32[8,256]{1,0:T(8,128)S(1)}, f32[8,256]{1,0:T(8,128)}, u32[]{:S(2)}) copy-start(f32[8,256]{1,0:T(8,128)} %copy-done.64) | copy-start | bytes 24580
  90.2 14.1 %copy-start.69 = (f32[8,256]{1,0:T(8,128)S(1)}, f32[8,256]{1,0:T(8,128)}, u32[]{:S(2)}) copy-start(f32[8,256]{1,0:T(8,128)} %copy-done.67) | copy-start | bytes 24580
  93.6 10.7 %copy-start.58 = (f32[9,8,256]{2,1,0:T(8,128)S(1)}, f32[9,8,256]{2,1,0:T(8,128)}, u32[]{:S(2)}) copy-start(f32[9,8,256]{2,1,0:T(8,128)} %copy-done.57) | copy-start | bytes 221188
  93.6 15.3 %copy-start.9 = (f32[9,16,256]{2,1,0:T(8,128)S(1)}, f32[9,16,256]{2,1,0:T(8,128)}, u32[]{:S(2)}) copy-start(f32[9,16,256]{2,1,0:T(8,128)} %copy-done.6) | copy-start | bytes 442372
  93.6 15.3 %copy-start.14 = (f32[16,16,256]{2,1,0:T(8,128)S(1)}, f32[16,16,256]{2,1,0:T(8,128)}, u32[]{:S(2)}) copy-start(f32[16,16,256]{2,1,0:T(8,128)} %copy-done.12) | copy-start | bytes 786436
  93.7 15.3 %copy-start.73 = (f32[16,256]{1,0:T(8,128)S(1)}, f32[16,256]{1,0:T(8,128)}, u32[]{:S(2)}) copy-start(f32[16,256]{1,0:T(8,128)} %copy-done.72) | copy-start | bytes 49156
  93.7 15.3 %copy-start.75 = (f32[16,256]{1,0:T(8,128)S(1)}, f32[16,256]{1,0:T(8,128)}, u32[]{:S(2)}) copy-start(f32[16,256]{1,0:T(8,128)} %copy-done.74) | copy-start | bytes 49156
  93.7 15.2 %all-to-all-start.3 = ((f32[16,16,256]{2,1,0:T(8,128)}), f32[16,16,256]{2,1,0:T(8,128)S(1)}, u32[]{:S(2)}, u32[]{:S(2)}) async-start(f32[16,16,256]{2,1,0:T(8,128)} %copy-done.35), calls=%async_computation.3 | async-start | bytes 524288 | tf_op jit(solution)/shard_map/all_to_all | solution.py:436
  (57 other events, 43.7 us)

commit v2 on v1

--- a/solution.py
+++ b/solution.py
@@ -7,6 +7,7 @@
 
 H = 12.0
 F32 = jnp.float32
+HBM = pltpu.HBM
 
 
 def iota(axis, shape):
@@ -73,26 +74,24 @@
         out[i] = u
 
 
-def interface_factors(coef, own, n, k, weights, consts):
+def interface_factors(coef, own, n, k, weights, mixed, consts):
     zero = jnp.zeros_like(own[0])
-    bs = []
-    ds = []
     B = zero
     for j in range(n - 1):
         al, be, de = coef(j)
         g = be / (1.0 - al * B)
+        h = g * B
         weights[j] = g
-        bs.append(B)
-        B = jnp.where(j < k, de + g * be * B, B)
+        mixed[j] = h
+        B = jnp.where(j < k, de + h * be, B)
     D = zero
     for j in range(n - 1, 0, -1):
         al, be, de = coef(j)
         g = be / (1.0 - de * D)
+        h = g * D
         weights[j] = jnp.where(j > k, g, weights[j]) if j < n - 1 else g
-        ds.append(D)
-        D = jnp.where(j > k, al + g * be * D, D)
-    ds.append(zero)
-    ds = ds[::-1]
+        mixed[j] = jnp.where(j > k, h, mixed[j]) if j < n - 1 else h
+        D = jnp.where(j > k, al + h * be, D)
     al, be, de = own
     den = 1.0 / (1.0 - al * B)
     gl = be * den
@@ -106,7 +105,6 @@
     consts[6] = den
     consts[7] = den * al
     consts[8] = B
-    return bs, ds
 
 
 def to_right(f, l, consts):
@@ -135,6 +133,18 @@
     return A, C
 
 
+def gather_sums_pair(pair, weights, mixed, n, k):
+    A = jnp.zeros_like(weights[0])
+    for j in range(n - 1):
+        f, l = pair(j)
+        A = jnp.where(j < k, l + mixed[j] * f + weights[j] * A, A)
+    C = jnp.zeros_like(A)
+    for j in range(n - 1, 0, -1):
+        f, l = pair(j)
+        C = jnp.where(j > k, f + mixed[j] * l + weights[j] * C, C)
+    return A, C
+
+
 def fill_send(send, f, l, consts, n, k):
     right = to_right(f, l, consts)
     left = to_left(f, l, consts)
@@ -142,7 +152,7 @@
         send[j] = jnp.where(j > k, right, left)
 
 
-def coef_kernel(nxd, nyd, mat, perm, cond, dm, cp, yk, yib, phy, psy, xf, phx, psx, cy, cx, sendy):
+def coef_kernel(nxd, nyd, mat, perm, cond, dm, cp, yk, yib, phy, psy, xf, phx, psx, cy, cx):
     kx = lax.axis_index("gx")
     ky = lax.axis_index("gy")
     nx, ny, nz = mat.shape
@@ -183,8 +193,6 @@
         cy[0, x:x + 1] = lo[0:1]
         cy[1, x:x + 1] = up[0:1]
         cy[2, x:x + 1] = up[ny - 1:ny]
-    for j in range(nyd):
-        sendy[j] = cy[...]
     s = H * cp[0]
     d = 1.0 + s * jnp.where(kx == 0, 1.0, 2.0)
     r = jnp.where(kx == 0, 0.0, s)
@@ -236,7 +244,7 @@
     return lambda level: (zk[2 * level, x], zk[2 * level + 1, x])
 
 
-def chain_x_kernel(el, mg, dm, cp, yk, yib, e1_up, iz_out, up_out, f_out, l_out):
+def chain_x_kernel(nyd, el, mg, dm, cp, yk, yib, cy, e1_up, iz_out, up_out, send, pair):
     nx, ny, nz = dm.shape
     for x in range(nx):
         above = el[1, x + 1] if x < nx - 1 else e1_up[0]
@@ -246,11 +254,14 @@
         rhs = dm[x] * el[0, x] + cp[x] * ((iz - prev_y(iz, 0.0)) - (h1 - prev_z(h1)))
         u = reduce_apply(rhs, 0, z_load(yk, x), yib[x])
         up_out[x] = u
-        f_out[x:x + 1] = u[0:1]
-        l_out[x:x + 1] = u[ny - 1:ny] - iz[ny - 1:ny] * (1.0 / H)
-
-
-def chain_z_kernel(nxd, el, mg, dm, cp, xf, cx, h0_low, iy_out, up_out, send):
+        pair[0, x:x + 1] = u[0:1]
+        pair[1, x:x + 1] = u[ny - 1:ny] - iz[ny - 1:ny] * (1.0 / H)
+    for j in range(nyd):
+        send[j, 0:3] = cy[...]
+        send[j, 3:5] = pair[...]
+
+
+def chain_z_kernel(el, mg, dm, cp, xf, h0_low, iy_out, up_out, pair):
     nx, ny, nz = dm.shape
     rhs = []
     below = jnp.zeros((ny, nz), F32)
@@ -262,14 +273,8 @@
         rhs.append(dm[x] * el[2, x] + cp[x] * ((iy - below) - (h0 - prev_y(h0, h0_low[x]))))
         below = iy
     sweep_x(rhs, xf, up_out)
-    f = up_out[0]
-    l = up_out[nx - 1] - below * (1.0 / H)
-    for j in range(nxd):
-        send[j, 0] = cx[0]
-        send[j, 1] = cx[1]
-        send[j, 2] = cx[2]
-        send[j, 3] = f
-        send[j, 4] = l
+    pair[0] = up_out[0]
+    pair[1] = up_out[nx - 1] - below * (1.0 / H)
 
 
 def center_y_kernel(el, mg, dm, cp, zk, zib, e2_up, h2_low, sx_out, t1_out):
@@ -286,19 +291,17 @@
         t1_out[x] = dm[x] * cy + cp[x] * (mx - prev_z(mx))
 
 
-def scan_y_kernel(recv, own, f, l, weights, consts, send):
-    ky = lax.axis_index("gy")
-    n = recv.shape[0]
-    interface_factors(lambda j: (recv[j, 0], recv[j, 1], recv[j, 2]), (own[0], own[1], own[2]), n, ky, weights, consts)
-    fill_send(send, f[...], l[...], consts, n, ky)
-
-
-def half_x_kernel(recv, weights, consts, f, l, up, iz, t1, dm, cp, phy, psy, xf, sz_out, t4_out, ufy_out, f_out, l_out, edge):
+def half_x_kernel(nxd, ready, recv, cy, up, iz, t1, dm, cp, phy, psy, xf, coef_x, pair_z, sz_out, t4_out, ufy_out, send, weights, consts, mixed, edge):
     ky = lax.axis_index("gy")
     nx, ny, nz = dm.shape
     n = recv.shape[0]
-    A, C = gather_sums(recv, weights, n, ky)
-    lower, upper = boundary(A, C, f[...], l[...], consts)
+    interface_factors(lambda j: (recv[j, 0], recv[j, 1], recv[j, 2]), (cy[0], cy[1], cy[2]), n, ky, weights, mixed, consts)
+    A, C = gather_sums_pair(lambda j: (recv[j, 3], recv[j, 4]), weights, mixed, n, ky)
+    ready()
+    for x in range(nx):
+        edge[0, x:x + 1] = up[x][0:1]
+        edge[1, x:x + 1] = up[x][ny - 1:ny] - iz[x][ny - 1:ny] * (1.0 / H)
+    lower, upper = boundary(A, C, edge[0], edge[1], consts)
     edge[0] = lower
     edge[1] = upper
     rhs = []
@@ -316,32 +319,30 @@
         rhs.append(t1[x] - cp[x] * (sz - below))
         below = sz
     sweep_x(rhs, xf, ufy_out)
-    f_out[...] = ufy_out[0]
-    l_out[...] = ufy_out[nx - 1] + below * (1.0 / H)
-
-
-def scan_x_kernel(recv, own, f1, l1, f2, l2, weights, consts, edge, send):
-    kx = lax.axis_index("gx")
-    n = recv.shape[0]
-    bs, ds = interface_factors(lambda j: (recv[j, 0], recv[j, 1], recv[j, 2]), (own[0], own[1], own[2]), n, kx, weights, consts)
-    fill_send(send, f2[...], l2[...], consts, n, kx)
-    A = jnp.zeros(f1.shape, F32)
-    for j in range(n - 1):
-        A = jnp.where(j < kx, recv[j, 4] + weights[j] * (A + bs[j] * recv[j, 3]), A)
-    C = jnp.zeros(f1.shape, F32)
-    for j in range(n - 1, 0, -1):
-        C = jnp.where(j > kx, recv[j, 3] + weights[j] * (C + ds[j] * recv[j, 4]), C)
-    lower, upper = boundary(A, C, f1[...], l1[...], consts)
-    edge[0] = lower
-    edge[1] = upper
-
-
-def half_z_kernel(edge, up, iy, sx, dm, cp, phx, psx, yk, yib, consts_y, sy_out, ufz_out, f_out, l_out, send):
+    f = ufy_out[0]
+    l = ufy_out[nx - 1] + below * (1.0 / H)
+    for j in range(nxd):
+        for i in range(3):
+            send[j, i] = coef_x[i]
+        send[j, 3] = pair_z[0]
+        send[j, 4] = pair_z[1]
+        send[j, 5] = f
+        send[j, 6] = l
+
+
+def half_z_kernel(ready, recv, cx, pair_z, up, iy, sx, ufy, sz, dm, cp, phx, psx, yk, yib, consts_y, sy_out, ufz_out, pair_out, edge_y_out, send, weights, mixed, consts):
     kx = lax.axis_index("gx")
     ky = lax.axis_index("gy")
     nx, ny, nz = dm.shape
-    lower = edge[0]
-    upper = edge[1]
+    n = recv.shape[0]
+    interface_factors(lambda j: (recv[j, 0], recv[j, 1], recv[j, 2]), (cx[0], cx[1], cx[2]), n, kx, weights, mixed, consts)
+    A, C = gather_sums_pair(lambda j: (recv[j, 5], recv[j, 6]), weights, mixed, n, kx)
+    ready()
+    lower, upper = boundary(A, C, ufy[0], ufy[nx - 1] + sz[nx - 1] * (1.0 / H), consts)
+    edge_y_out[0] = lower
+    edge_y_out[1] = upper
+    A, C = gather_sums_pair(lambda j: (recv[j, 3], recv[j, 4]), weights, mixed, n, kx)
+    lower, upper = boundary(A, C, pair_z[0], pair_z[1], consts)
     cz = up[0] + phx[0] * lower + psx[0] * upper
     below = jnp.where(kx == 0, 0.0, H * (cz - lower))
     for x in range(nx):
@@ -353,11 +354,11 @@
         rhs = dm[x] * cz + cp[x] * ((my - below) - (s - prev_y(s, 0.0)))
         u = reduce_apply(rhs, 0, z_load(yk, x), yib[x])
         ufz_out[x] = u
-        f_out[x:x + 1] = u[0:1]
-        l_out[x:x + 1] = u[ny - 1:ny] + s[ny - 1:ny] * (1.0 / H)
+        pair_out[0, x:x + 1] = u[0:1]
+        pair_out[1, x:x + 1] = u[ny - 1:ny] + s[ny - 1:ny] * (1.0 / H)
         cz = cn
         below = my
-    fill_send(send, f_out[...], l_out[...], consts_y, send.shape[0], ky)
+    fill_send(send, pair_out[0], pair_out[1], consts_y, send.shape[0], ky)
 
 
 def final_x_kernel(t4, sy, cp, zk, zib, fx_out, my_out):
@@ -369,11 +370,10 @@
         my_out[x] = s - H * (next_z(fx) - fx)
 
 
-def final_y_kernel(recv, weights, consts, f, l, up, sz, phx, psx, fy_out, mz_out):
-    kx = lax.axis_index("gx")
+def final_y_kernel(edge, up, sz, phx, psx, fy_out, mz_out):
     nx = up.shape[0]
-    A, C = gather_sums(recv, weights, recv.shape[0], kx)
-    lower, upper = boundary(A, C, f[...], l[...], consts)
+    lower = edge[0]
+    upper = edge[1]
     fy = up[0] + phx[0] * lower + psx[0] * upper
     for x in range(nx):
         fn = up[x + 1] + phx[x + 1] * lower + psx[x + 1] * upper if x < nx - 1 else upper
@@ -382,11 +382,12 @@
         fy = fn
 
 
-def final_z_kernel(recv, weights, consts, f, l, up, sx, phy, psy, fx, fy, my, mz, e_out, h_out, edge):
+def final_z_kernel(ready, recv, weights, consts, pair, up, sx, phy, psy, fx, fy, my, mz, e_out, h_out, edge):
     ky = lax.axis_index("gy")
     nx = up.shape[0]
     A, C = gather_sums(recv, weights, recv.shape[0], ky)
-    lower, upper = boundary(A, C, f[...], l[...], consts)
+    lower, upper = boundary(A, C, pair[0], pair[1], consts)
+    ready()
     edge[0] = lower
     edge[1] = upper
     for x in range(nx):
@@ -401,21 +402,74 @@
         h_out[2, x] = mz[x]
 
 
-def vmem():
-    return pl.BlockSpec(memory_space=pltpu.VMEM)
-
-
-def call(kernel, outs, *args, smem=(), scratch=(), name=None):
-    specs = [pl.BlockSpec(memory_space=pltpu.SMEM) if i in smem else vmem() for i in range(len(args))]
-    nbytes = sum(a.size * 4 for a in args) + sum(4 * _size(o) for o in outs)
+def staged(kernel, kinds_in, kinds_out, first):
+    def body(*refs):
+        ni = len(kinds_in)
+        no = len(kinds_out)
+        ins = refs[:ni]
+        outs = refs[ni:ni + no]
+        rest = list(refs[ni + no:])
+        sems = rest.pop()
+        work = []
+        copies = []
+        for ref, kind in zip(ins, kinds_in):
+            if kind == "v":
+                work.append(ref)
+                continue
+            held = rest.pop(0)
+            copy = pltpu.make_async_copy(ref, held, sems.at[len(copies)])
+            copy.start()
+            copies.append(copy)
+            work.append(held)
+        back = []
+        for ref, kind in zip(outs, kinds_out):
+            if kind == "v":
+                work.append(ref)
+                continue
+            held = rest.pop(0)
+            back.append((held, ref))
+            work.append(held)
+        head = len(copies) if first is None else first
+        for copy in copies[:head]:
+            copy.wait()
+
+        def ready():
+            for copy in copies[head:]:
+                copy.wait()
+
+        if first is None:
+            kernel(*work, *rest)
+        else:
+            kernel(ready, *work, *rest)
+        copies = [pltpu.make_async_copy(held, ref, sems.at[i]) for i, (held, ref) in enumerate(back)]
+        for copy in copies:
+            copy.start()
+        for copy in copies:
+            copy.wait()
+
+    return body
+
+
+def call(kernel, outs, *args, smem=(), near=(), near_out=(), scratch=(), first=None, name=None):
+    kinds_in = ["s" if i in smem else "v" if i in near else "h" for i in range(len(args))]
+    kinds_out = ["v" if i in near_out else "h" for i in range(len(outs))]
+    held = []
+    for a, kind in zip(args, kinds_in):
+        if kind != "v":
+            held.append((pltpu.SMEM if kind == "s" else pltpu.VMEM)(a.shape, a.dtype))
+    for o, kind in zip(outs, kinds_out):
+        if kind != "v":
+            held.append(pltpu.VMEM(o, F32))
+    spec = {"v": pltpu.VMEM, "h": HBM, "s": HBM}
+    nbytes = sum(4 * _size(a.shape) for a in args) + sum(4 * _size(o) for o in outs)
     return pl.pallas_call(
-        kernel,
+        staged(kernel, kinds_in, kinds_out, first),
         out_shape=[jax.ShapeDtypeStruct(o, F32) for o in outs],
-        in_specs=specs,
-        out_specs=[vmem() for _ in outs],
-        scratch_shapes=list(scratch),
+        in_specs=[pl.BlockSpec(memory_space=spec[k]) for k in kinds_in],
+        out_specs=[pl.BlockSpec(memory_space=spec[k]) for k in kinds_out],
+        scratch_shapes=held + list(scratch) + [pltpu.SemaphoreType.DMA((len(held),))],
         cost_estimate=pl.CostEstimate(flops=4 * nbytes, bytes_accessed=nbytes, transcendentals=0),
-        compiler_params=pltpu.CompilerParams(vmem_limit_bytes=40 << 20),
+        compiler_params=pltpu.CompilerParams(vmem_limit_bytes=60 << 20),
         name=name,
     )(*args)
 
@@ -449,43 +503,39 @@
             kernel(*lead, *refs)
         return body
 
-    dm, cp, yk, yib, phy, psy, xf, phx, psx, cy, cx, sendy = call(
+
+    dm, cp, yk, yib, phy, psy, xf, phx, psx, cy, cx = call(
         bind(coef_kernel, nxd, nyd),
-        [cell, cell, (2 * len(strides(ny)),) + cell, cell, cell, cell, (3,) + cell, cell, cell,
-         (3,) + py, (3,) + px, (nyd, 3) + py],
+        [cell, cell, (2 * len(strides(ny)),) + cell, cell, cell, cell, (3,) + cell, cell, cell, (3,) + py, (3,) + px],
         material, permittivity, conductivity, smem=(1, 2), name="coef")
-    recv_cy = exchange(sendy, "gy")
-
-    e1_up = shifted(electric[1, 0:1], "gx", -1)
+    e1_up = shifted(lax.optimization_barrier((electric[1, 0:1], cx))[0], "gx", -1)
+    iz, ux, send1 = call(bind(chain_x_kernel, nyd), [cell, cell, (nyd, 5) + py],
+                         electric, magnetic, dm, cp, yk, yib, cy, e1_up, scratch=[pltpu.VMEM((2,) + py, F32)], name="chain_x")
+    recv1 = exchange(send1, "gy")
+
     h0_low = shifted(magnetic[0, :, ny - 1:ny], "gy", 1)
     e2_up = shifted(electric[2, :, 0:1], "gy", -1)
     h2_low = shifted(magnetic[2, nx - 1:nx], "gx", 1)
-
     zk, zib = call(zfactor_kernel, [(2 * len(strides(nz)),) + cell, cell], cp, name="zfactor")
-    iz, ux, fx1, lx1 = call(chain_x_kernel, [cell, cell, py, py], electric, magnetic, dm, cp, yk, yib, e1_up, name="chain_x")
-    wy, ky, send = call(scan_y_kernel, [(nyd,) + py, (9,) + py, (nyd,) + py], recv_cy, cy, fx1, lx1, name="scan_y")
-    recv1 = exchange(send, "gy")
-
-    iy, uz, sendx = call(bind(chain_z_kernel, nxd), [cell, cell, (nxd, 5) + px], electric, magnetic, dm, cp, xf, cx, h0_low, name="chain_z")
-    recv2 = exchange(sendx, "gx")
+    iy, uz, pair_z = call(chain_z_kernel, [cell, cell, (2,) + px], electric, magnetic, dm, cp, xf, h0_low, name="chain_z")
     sx, t1 = call(center_y_kernel, [cell, cell], electric, magnetic, dm, cp, zk, zib, e2_up, h2_low, name="center_y")
 
-    sz, t4, ufy, f3, l3 = call(half_x_kernel, [cell, cell, cell, px, px],
-                               recv1, wy, ky, fx1, lx1, ux, iz, t1, dm, cp, phy, psy, xf,
-                               scratch=[pltpu.VMEM((2,) + py, F32)], name="half_x")
-    fz2 = sendx[0, 3]
-    lz2 = sendx[0, 4]
-    wx, kx, edge2, send3 = call(scan_x_kernel, [(nxd,) + px, (9,) + px, (2,) + px, (nxd,) + px],
-                                recv2, cx, fz2, lz2, f3, l3, name="scan_x")
-    recv3 = exchange(send3, "gx")
-    sy, ufz, f4, l4, send4 = call(half_z_kernel, [cell, cell, py, py, (nyd,) + py],
-                                  edge2, uz, iy, sx, dm, cp, phx, psx, yk, yib, ky, name="half_z")
-    recv4 = exchange(send4, "gy")
+    sz, t4, ufy, send2, wy, ky = call(
+        bind(half_x_kernel, nxd), [cell, cell, cell, (nxd, 7) + px, (nyd,) + py, (9,) + py],
+        recv1, cy, ux, iz, t1, dm, cp, phy, psy, xf, cx, pair_z,
+        first=2, scratch=[pltpu.VMEM((nyd,) + py, F32), pltpu.VMEM((2,) + py, F32)], name="half_x")
+    recv2 = exchange(send2, "gx")
+    sy, ufz, pair4, edge_y, send3 = call(
+        half_z_kernel, [cell, cell, (2,) + py, (2,) + px, (nyd,) + py],
+        recv2, cx, pair_z, uz, iy, sx, ufy, sz, dm, cp, phx, psx, yk, yib, ky,
+        first=2, scratch=[pltpu.VMEM((nxd,) + px, F32), pltpu.VMEM((nxd,) + px, F32), pltpu.VMEM((9,) + px, F32)],
+        name="half_z")
+    recv3 = exchange(send3, "gy")
     fx, my = call(final_x_kernel, [cell, cell], t4, sy, cp, zk, zib, name="final_x")
-    fy, mz = call(final_y_kernel, [cell, cell], recv3, wx, kx, f3, l3, ufy, sz, phx, psx, name="final_y")
+    fy, mz = call(final_y_kernel, [cell, cell], edge_y, ufy, sz, phx, psx, name="final_y")
     e, h = call(final_z_kernel, [(3,) + cell, (3,) + cell],
-                recv4, wy, ky, f4, l4, ufz, sx, phy, psy, fx, fy, my, mz,
-                scratch=[pltpu.VMEM((2,) + py, F32)], name="final_z")
+                recv3, wy, ky, pair4, ufz, sx, phy, psy, fx, fy, my, mz,
+                first=4, scratch=[pltpu.VMEM((2,) + py, F32)], name="final_z")
     return e, h
 
 

time: 115 us -> 89.2 us (0.78)
  local copies, waits for them, and re-layouts: 47.5 us -> 6.78 us
  Pallas kernels: 14.3 us -> 32.5 us
  starting transfers between devices: 43.5 us -> 25.7 us
  blocking collectives: 0 us -> 14.5 us
    unnamed x160 -> x12, local copies, waits for them, and re-layouts: 44.8 us -> 3.54 us
    all_to_all x5 -> x2, starting transfers between devices: 31.9 us -> 12.8 us  [exchange(): return lax.all_to_all(array, axis, 0, 0)]
    pallas_call x12 -> x10, Pallas kernels: 14.3 us -> 32.5 us  [call(): pl.pallas_call(staged(kernel, kinds_in, kinds_out, first), out_shape=[jax...]
    all_to_all x0 -> x1, blocking collectives: none -> 14.5 us  [exchange(): return lax.all_to_all(array, axis, 0, 0)]
    squeeze x2 -> x1, local copies, waits for them, and re-layouts: 2.08 us -> 0.7 us  [per_device(): electric[1, 0:1]]
    ppermute x4, starting transfers between devices: 11.6 us -> 12.8 us  [shifted(): lax.ppermute(array, axis, [(i, i + by) for i in range(count) if 0 <= i +...]
  transfers between devices with their start and end apart: 9 -> 6, of which waited for: 2 -> 2; matrix products, arithmetic and copies ran while one was open for 2% -> 3% of each run, Pallas kernels for 9% -> 21%
where the time goes in v2:
time: 89.2 us; the launch traced here: 88.4 us
  Pallas kernels  32.5 us (36%)
  starting transfers between devices  25.7 us (29%)
  blocking collectives  14.5 us (16%)
  waiting for transfers between devices  8.21 us (9%)
  local copies, waits for them, and re-layouts  6.78 us (8%)
    pallas_call x10, Pallas kernels, call(): pl.pallas_call(staged(kernel, kinds_in, kinds_out, first), out_shape=[jax...  32.5 us
    all_to_all x1, blocking collectives, exchange(): return lax.all_to_all(array, axis, 0, 0)  14.5 us
    all_to_all x2, starting transfers between devices, exchange(): return lax.all_to_all(array, axis, 0, 0)  12.8 us
    ppermute x4, starting transfers between devices, shifted(): lax.ppermute(array, axis, [(i, i + by) for i in range(count) if 0 <= i +...  12.8 us
    ppermute x4, waiting for transfers between devices, shifted(): lax.ppermute(array, axis, [(i, i + by) for i in range(count) if 0 <= i +...  6.08 us
    unnamed x12, local copies, waits for them, and re-layouts  3.54 us
    all_to_all x2, waiting for transfers between devices, exchange(): return lax.all_to_all(array, axis, 0, 0)  2.13 us
  transfers between devices with their start and end apart: 6, of which 2 were waited for; matrix products, arithmetic and copies ran while one was open for 3% of the time, Pallas kernels for 21%

profile of v2, /device:TPU:1, one launch (start us, length us, event | category | flops | bytes accessed | tf_op | source)
XLA Modules:
  0.0 88.4 jit_solution(7539357922734824914)
XLA Ops:
  0.6 0.7 slice_bitcast_fusion.3
  1.3 2.9 %coef.1 = (f32[16,8,256]{2,1,0:T(8,128)}, f32[16,8,256]{2,1,0:T(8,128)}, f32[6,16,8,256]{3,2,1,0:T(8,128)}, f32[16,8,256]{2,1,0:T(8,128)}, f32[16,8,256]{2,1,0:T...) custom-call(s32[16,8,256]{2,1,0:T(8,128)} %refs_0_.4, ...), custom_call_target="tpu_custom_call" | custom-call | flops 9208064 | bytes 2302016 | tf_op jit(solution)/shard_map/coef/pallas_call | solution.py:465
  4.2 1.3 %collective-permute-start = (f32[1,8,256]{2,1,0:T(8,128)S(1)}, f32[1,8,256]{2,1,0:T(8,128)S(1)}, u32[]{:S(2)}, u32[]{:S(2)}) collective-permute-start(f32[1,8,256]{2,1,0:T(8,128)S(1)} %slice_bitcast_fusion.3), channel_id=1, source_target_pairs={{16,0},{32,16},{48,32},{64,48},{80,64},{96,80},{112,96},{17,1},{33... | collective-permute-start | bytes 24584 | tf_op jit(solution)/shard_map/ppermute | solution.py:486
  5.5 6.1 %collective-permute-done.refs_7_ = f32[1,8,256]{2,1,0:T(8,128)S(1)} collective-permute-done((f32[1,8,256]{2,1,0:T(8,128)S(1)}, f32[1,8,256]{2,1,0:T(8,128)S(1)}, u32[]{:S(2)}, u32[]{:S(2)}) %collective-permute-start) | collective-permute-done | bytes 8224 | tf_op jit(solution)/shard_map/ppermute | solution.py:486
  11.6 0.6 copy-done.5
  12.2 3.0 %chain_x.1 = (f32[16,8,256]{2,1,0:T(8,128)}, f32[16,8,256]{2,1,0:T(8,128)}, f32[16,5,16,256]{3,2,1,0:T(8,128)}) custom-call(f32[3,16,8,256]{3,2,1,0:T(8,128)} %refs_0_.7, f32[3,16,8,256]{3,2,1,0:T(8,128)} %refs_1_.7, f32[16,8,256]{2,1,0:T(8,128)} %get-tuple-element.39.refs_2_.refs_5_.refs_8_, ...), custom_call_target="tpu_custom_call" | custom-call | flops 14385152 | bytes 3596288 | tf_op jit(solution)/shard_map/chain_x/pallas_call | solution.py:465
  15.2 6.9 %all-to-all-start = ((f32[16,5,16,256]{3,2,1,0:T(8,128)}), f32[16,5,16,256]{3,2,1,0:T(8,128)S(1)}, u32[]{:S(2)}, u32[]{:S(2)}) async-start(f32[16,5,16,256]{3,2,1,0:T(8,128)} %get-tuple-element.46), calls=%async_computation | async-start | bytes 2621440 | tf_op jit(solution)/shard_map/all_to_all | solution.py:490
  22.0 0.9 %slice_bitcast_fusion = f32[16,1,256]{2,1,0:T(1,128)S(1)} fusion(f32[3,16,8,256]{3,2,1,0:T(8,128)} %refs_1_.7), kind=kLoop, calls=%fused_computation | loop fusion | bytes 32768 | tf_op jit(solution)/shard_map/squeeze | solution.py:516
  22.9 3.5 %collective-permute-start.3 = (f32[16,1,256]{2,1,0:T(1,128)S(1)}, f32[16,1,256]{2,1,0:T(1,128)S(1)}, u32[]{:S(2)}, u32[]{:S(2)}) collective-permute-start(f32[16,1,256]{2,1,0:T(1,128)S(1)} %slice_bitcast_fusion), channel_id=1, source_target_pairs={{0,1},{1,2},{2,3},{3,4},{4,5},{5,6},{6,7},{7,8},{8,9},{9,10},{10,1... | collective-permute-start | bytes 49160 | tf_op jit(solution)/shard_map/ppermute | solution.py:486
  26.5 0.9 %slice_bitcast_fusion.1 = f32[16,1,256]{2,1,0:T(1,128)S(1)} fusion(f32[3,16,8,256]{3,2,1,0:T(8,128)} %refs_0_.7), kind=kLoop, calls=%fused_computation.1 | loop fusion | bytes 32768 | tf_op jit(solution)/shard_map/squeeze | solution.py:517
  27.4 1.9 %collective-permute-start.1 = (f32[16,1,256]{2,1,0:T(1,128)S(1)}, f32[16,1,256]{2,1,0:T(1,128)S(1)}, u32[]{:S(2)}, u32[]{:S(2)}) collective-permute-start(f32[16,1,256]{2,1,0:T(1,128)S(1)} %slice_bitcast_fusion.1), channel_id=1, source_target_pairs={{1,0},{2,1},{3,2},{4,3},{5,4},{6,5},{7,6},{8,7},{9,8},{10,9},{11,1... | collective-permute-start | bytes 49160 | tf_op jit(solution)/shard_map/ppermute | solution.py:486
  29.3 0.7 slice_bitcast_fusion.2
  30.0 6.1 %collective-permute-start.2 = (f32[1,8,256]{2,1,0:T(8,128)S(1)}, f32[1,8,256]{2,1,0:T(8,128)S(1)}, u32[]{:S(2)}, u32[]{:S(2)}) collective-permute-start(f32[1,8,256]{2,1,0:T(8,128)S(1)} %slice_bitcast_fusion.2), channel_id=1, source_target_pairs={{0,16},{16,32},{32,48},{48,64},{64,80},{80,96},{96,112},{1,17},{17... | collective-permute-start | bytes 24584 | tf_op jit(solution)/shard_map/ppermute | solution.py:486
  36.1 7.1 %zfactor.1 = (f32[16,16,8,256]{3,2,1,0:T(8,128)}, f32[16,8,256]{2,1,0:T(8,128)}) custom-call(f32[16,8,256]{2,1,0:T(8,128)} %get-tuple-element.40.refs_3_.refs_0_.refs_6_.refs_9_.refs_2_), custom_call_target="tpu_custom_call" | custom-call | flops 9437184 | bytes 2359296 | tf_op jit(solution)/shard_map/zfactor/pallas_call | solution.py:465
  43.3 0.0 collective-permute-done.3.refs_5_
  43.3 0.6 copy-done.3
  43.9 2.2 %chain_z.1 = (f32[16,8,256]{2,1,0:T(8,128)}, f32[16,8,256]{2,1,0:T(8,128)}, f32[2,8,256]{2,1,0:T(8,128)}) custom-call(f32[3,16,8,256]{3,2,1,0:T(8,128)} %refs_0_.7, f32[3,16,8,256]{3,2,1,0:T(8,128)} %refs_1_.7, f32[16,8,256]{2,1,0:T(8,128)} %get-tuple-element.39.refs_2_.refs_5_.refs_8_, ...), custom_call_target="tpu_custom_call" | custom-call | flops 6946816 | bytes 1736704 | tf_op jit(solution)/shard_map/chain_z/pallas_call | solution.py:465
  46.1 0.0 collective-permute-done.1.refs_6_
  46.2 0.6 copy-done.4
  46.7 0.0 copy-done.2
  46.7 3.6 %center_y.1 = (f32[16,8,256]{2,1,0:T(8,128)}, f32[16,8,256]{2,1,0:T(8,128)}) custom-call(f32[3,16,8,256]{3,2,1,0:T(8,128)} %refs_0_.7, f32[3,16,8,256]{3,2,1,0:T(8,128)} %refs_1_.7, f32[16,8,256]{2,1,0:T(8,128)} %get-tuple-element.39.refs_2_.refs_5_.refs_8_, f32[16,8,256]{2,1,0:T(8,128)} %get-tuple-element.40.refs_3_.refs_0_.refs_6_.refs_9_.refs_2_, ...), custom_call_target="tpu_custom_call" | custom-call | flops 14254080 | bytes 3563520 | tf_op jit(solution)/shard_map/center_y/pallas_call | solution.py:465
  50.3 0.0 all-to-all-done.refs_0_
  50.4 1.1 %copy-done = f32[16,5,16,256]{3,2,1,0:T(8,128)} copy-done((f32[16,5,16,256]{3,2,1,0:T(8,128)}, f32[16,5,16,256]{3,2,1,0:T(8,128)S(1)}, u32[]{:S(2)}) %copy-start) | copy-done | bytes 1310744
  51.4 3.1 %half_x.1 = (f32[16,8,256]{2,1,0:T(8,128)}, f32[16,8,256]{2,1,0:T(8,128)}, f32[16,8,256]{2,1,0:T(8,128)}, f32[8,7,8,256]{3,2,1,0:T(8,128)}, f32[16,16,256]{2,1,0:T(8,128)}, /*index=5*/f32[9,16,256]{2,1,0:T(8,128)}) custom-call(f32[16,5,16,256]{3,2,1,0:T(8,128)} %copy-done, f32[3,16,256]{2,1,0:T(8,128)} %get-tuple-element.43.refs_6_.refs_1_, ...), custom_call_target="tpu_custom_call" | custom-call | flops 15892480 | bytes 3973120 | tf_op jit(solution)/shard_map/half_x/pallas_call | solution.py:465
  54.5 14.5 %all_to_all.15.refs_0_ = f32[8,7,8,256]{3,2,1,0:T(8,128)} all-to-all(f32[8,7,8,256]{3,2,1,0:T(8,128)} %get-tuple-element.56), channel_id=1, replica_groups=mesh['gx'=8,'gy'=16] {'gx'}, dimensions={0} | all-to-all | bytes 917504 | tf_op jit(solution)/shard_map/all_to_all | solution.py:490
  69.0 2.9 %half_z.1 = (f32[16,8,256]{2,1,0:T(8,128)}, f32[16,8,256]{2,1,0:T(8,128)}, f32[2,16,256]{2,1,0:T(8,128)}, f32[2,8,256]{2,1,0:T(8,128)}, f32[16,16,256]{2,1,0:T(8,128)}) custom-call(f32[8,7,8,256]{3,2,1,0:T(8,128)} %all_to_all.15.refs_0_, f32[3,8,256]{2,1,0:T(8,128)} %get-tuple-element.44.refs_10_.refs_1_, f32[2,8,256]{2,1,0:T(8,128)} %get-tuple-element.55.refs_11_.refs_2_, ...), custom_call_target="tpu_custom_call" | custom-call | flops 13271040 | bytes 3317760 | tf_op jit(solution)/shard_map/half_z/pallas_call | solution.py:465
  71.9 6.0 %all-to-all-start.2 = ((f32[16,16,256]{2,1,0:T(8,128)}), f32[16,16,256]{2,1,0:T(8,128)S(1)}, u32[]{:S(2)}, u32[]{:S(2)}) async-start(f32[16,16,256]{2,1,0:T(8,128)} %get-tuple-element.65), calls=%async_computation.2 | async-start | bytes 524288 | tf_op jit(solution)/shard_map/all_to_all | solution.py:490
  77.8 1.9 %final_y.1 = (f32[16,8,256]{2,1,0:T(8,128)}, f32[16,8,256]{2,1,0:T(8,128)}) custom-call(f32[2,8,256]{2,1,0:T(8,128)} %get-tuple-element.72.refs_0_, f32[16,8,256]{2,1,0:T(8,128)} %get-tuple-element.60.refs_6_.refs_1_, f32[16,8,256]{2,1,0:T(8,128)} %get-tuple-element.61.refs_7_.refs_2_, f32[16,8,256]{2,1,0:T(8,128)} %get-tuple-element.62.refs_10_.refs_3_, ...), custom_call_target="tpu_custom_call" | custom-call | flops 3211264 | bytes 802816 | tf_op jit(solution)/shard_map/final_y/pallas_call | solution.py:465
  79.8 3.4 %final_x.1 = (f32[16,8,256]{2,1,0:T(8,128)}, f32[16,8,256]{2,1,0:T(8,128)}) custom-call(f32[16,8,256]{2,1,0:T(8,128)} %get-tuple-element.69.refs_0_, f32[16,8,256]{2,1,0:T(8,128)} %get-tuple-element.70.refs_1_, f32[16,8,256]{2,1,0:T(8,128)} %get-tuple-element.40.refs_3_.refs_0_.refs_6_.refs_9_.refs_2_, f32[16,16,8,256]{3,2,1,0:T(8,128)} %get-tuple-element.49.refs_4_.refs_3_, ...), custom_call_target="tpu_custom_call" | custom-call | flops 11534336 | bytes 2883584 | tf_op jit(solution)/shard_map/final_x/pallas_call | solution.py:465
  83.1 2.1 %all-to-all-done.2.refs_0_ = f32[16,16,256]{2,1,0:T(8,128)S(1)} async-done(((f32[16,16,256]{2,1,0:T(8,128)}), f32[16,16,256]{2,1,0:T(8,128)S(1)}, u32[]{:S(2)}, u32[]{:S(2)}) %all-to-all-start.2) | async-done | bytes 262176 | tf_op jit(solution)/shard_map/all_to_all | solution.py:490
  85.3 0.7 copy-done.1
  85.9 2.5 %final_z.1 = (f32[3,16,8,256]{3,2,1,0:T(8,128)}, f32[3,16,8,256]{3,2,1,0:T(8,128)}) custom-call(f32[16,16,256]{2,1,0:T(8,128)} %copy-done.1, f32[16,16,256]{2,1,0:T(8,128)} %get-tuple-element.66.refs_1_, f32[9,16,256]{2,1,0:T(8,128)} %get-tuple-element.64.refs_14_.refs_2_, f32[2,16,256]{2,1,0:T(8,128)} %get-tuple-element.67.refs_3_, ...), custom_call_target="tpu_custom_call" | custom-call | flops 10158080 | bytes 2539520 | tf_op jit(solution)/shard_map/final_z/pallas_call | solution.py:465
  (7 shorter events, 0.0 us)
Async XLA Ops:
  4.2 7.4 %collective-permute-start = (f32[1,8,256]{2,1,0:T(8,128)S(1)}, f32[1,8,256]{2,1,0:T(8,128)S(1)}, u32[]{:S(2)}, u32[]{:S(2)}) collective-permute-start(f32[1,8,256]{2,1,0:T(8,128)S(1)} %slice_bitcast_fusion.3), channel_id=1, source_target_pairs={{16,0},{32,16},{48,32},{64,48},{80,64},{96,80},{112,96},{17,1},{33... | collective-permute-start | bytes 24584 | tf_op jit(solution)/shard_map/ppermute | solution.py:486
  11.6 0.6 copy-start.5
  15.2 35.2 %all-to-all-start = ((f32[16,5,16,256]{3,2,1,0:T(8,128)}), f32[16,5,16,256]{3,2,1,0:T(8,128)S(1)}, u32[]{:S(2)}, u32[]{:S(2)}) async-start(f32[16,5,16,256]{3,2,1,0:T(8,128)} %get-tuple-element.46), calls=%async_computation | async-start | bytes 2621440 | tf_op jit(solution)/shard_map/all_to_all | solution.py:490
  22.9 20.3 %collective-permute-start.3 = (f32[16,1,256]{2,1,0:T(1,128)S(1)}, f32[16,1,256]{2,1,0:T(1,128)S(1)}, u32[]{:S(2)}, u32[]{:S(2)}) collective-permute-start(f32[16,1,256]{2,1,0:T(1,128)S(1)} %slice_bitcast_fusion), channel_id=1, source_target_pairs={{0,1},{1,2},{2,3},{3,4},{4,5},{5,6},{6,7},{7,8},{8,9},{9,10},{10,1... | collective-permute-start | bytes 49160 | tf_op jit(solution)/shard_map/ppermute | solution.py:486
  27.4 18.7 %collective-permute-start.1 = (f32[16,1,256]{2,1,0:T(1,128)S(1)}, f32[16,1,256]{2,1,0:T(1,128)S(1)}, u32[]{:S(2)}, u32[]{:S(2)}) collective-permute-start(f32[16,1,256]{2,1,0:T(1,128)S(1)} %slice_bitcast_fusion.1), channel_id=1, source_target_pairs={{1,0},{2,1},{3,2},{4,3},{5,4},{6,5},{7,6},{8,7},{9,8},{10,9},{11,1... | collective-permute-start | bytes 49160 | tf_op jit(solution)/shard_map/ppermute | solution.py:486
  30.0 16.1 %collective-permute-start.2 = (f32[1,8,256]{2,1,0:T(8,128)S(1)}, f32[1,8,256]{2,1,0:T(8,128)S(1)}, u32[]{:S(2)}, u32[]{:S(2)}) collective-permute-start(f32[1,8,256]{2,1,0:T(8,128)S(1)} %slice_bitcast_fusion.2), channel_id=1, source_target_pairs={{0,16},{16,32},{32,48},{48,64},{64,80},{80,96},{96,112},{1,17},{17... | collective-permute-start | bytes 24584 | tf_op jit(solution)/shard_map/ppermute | solution.py:486
  43.3 0.6 copy-start.3
  46.1 0.6 copy-start.4
  46.1 0.6 copy-start.2
  50.4 1.1 %copy-start = (f32[16,5,16,256]{3,2,1,0:T(8,128)}, f32[16,5,16,256]{3,2,1,0:T(8,128)S(1)}, u32[]{:S(2)}) copy-start(f32[16,5,16,256]{3,2,1,0:T(8,128)S(1)} %all-to-all-done.refs_0_) | copy-start | bytes 3932164
  71.9 13.4 %all-to-all-start.2 = ((f32[16,16,256]{2,1,0:T(8,128)}), f32[16,16,256]{2,1,0:T(8,128)S(1)}, u32[]{:S(2)}, u32[]{:S(2)}) async-start(f32[16,16,256]{2,1,0:T(8,128)} %get-tuple-element.65), calls=%async_computation.2 | async-start | bytes 524288 | tf_op jit(solution)/shard_map/all_to_all | solution.py:490
  85.3 0.7 copy-start.1

commit v3 on v2

--- a/solution.py
+++ b/solution.py
@@ -8,6 +8,7 @@
 H = 12.0
 F32 = jnp.float32
 HBM = pltpu.HBM
+ROOM = 60
 
 
 def iota(axis, shape):
@@ -41,16 +42,16 @@
     return out
 
 
-def reduce_factors(a, b, c, axis, store):
+def reduce_factors(a, b, axis, store):
     n = a.shape[axis]
     for level, s in enumerate(strides(n)):
         inv = 1.0 / b
+        c = pltpu.roll(a, n - s, axis)
         ka = -a * pltpu.roll(inv, s, axis)
         kc = -c * pltpu.roll(inv, n - s, axis)
         store(level, ka, kc)
-        b = b + ka * pltpu.roll(c, s, axis) + kc * pltpu.roll(a, n - s, axis)
+        b = b + ka * a + kc * c
         a = ka * pltpu.roll(a, s, axis)
-        c = kc * pltpu.roll(c, n - s, axis)
     return 1.0 / b
 
 
@@ -62,15 +63,15 @@
     return r * inv
 
 
-def sweep_x(rhs, xf, out):
+def sweep_x(rhs, ex, out):
     nx = len(rhs)
     fwd = [rhs[0]]
     for i in range(1, nx):
-        fwd.append(rhs[i] + xf[0, i] * fwd[i - 1])
-    u = xf[1, nx - 1] * fwd[nx - 1]
+        fwd.append(rhs[i] + ex[i - 1] * fwd[i - 1])
+    u = ex[nx - 1] * fwd[nx - 1]
     out[nx - 1] = u
     for i in range(nx - 2, -1, -1):
-        u = xf[1, i] * fwd[i] + xf[2, i] * u
+        u = ex[i] * (fwd[i] + u)
         out[i] = u
 
 
@@ -152,8 +153,7 @@
         send[j] = jnp.where(j > k, right, left)
 
 
-def coef_kernel(nxd, nyd, mat, perm, cond, dm, cp, yk, yib, phy, psy, xf, phx, psx, cy, cx):
-    kx = lax.axis_index("gx")
+def coef_kernel(nyd, ready, mat, perm, cond, el, mg, ds, si, yk, yib, phy, psy, cy, send, pe1, ph2, pe2, ph0):
     ky = lax.axis_index("gy")
     nx, ny, nz = mat.shape
     row = iota(0, (ny, nz))
@@ -164,18 +164,15 @@
         for t in range(1, perm.shape[0]):
             eps = jnp.where(m == t, perm[t], eps)
             sig = jnp.where(m == t, cond[t], sig)
-        ea = eps / H
-        sh = sig * 0.5
-        inv = 1.0 / (ea + sh)
-        cp[x] = inv
-        dm[x] = (ea - sh) * inv
-        s = H * inv
+        ea = eps * (1.0 / (H * H))
+        sh = sig * (0.5 / H)
+        ds[x] = ea - sh
+        inv_s = ea + sh
+        si[x] = inv_s
         first = row == 0
         last = row == ny - 1
-        a = jnp.where(first, 0.0, -s)
-        c = jnp.where(last, 0.0, -s)
-        edge = jnp.where(ky == 0, 1.0, 2.0)
-        b = 1.0 + s * jnp.where(first, edge, 2.0)
+        a = jnp.where(first, 0.0, jnp.full(m.shape, -1.0, F32))
+        b = inv_s + jnp.where(first, jnp.where(ky == 0, 1.0, 2.0), 2.0)
 
         def store(level, ka, kc):
             yk[2 * level, x] = ka
@@ -184,85 +181,84 @@
         def load(level):
             return yk[2 * level, x], yk[2 * level + 1, x]
 
-        ib = reduce_factors(a, b, c, 0, store)
+        ib = reduce_factors(a, b, 0, store)
         yib[x] = ib
-        lo = reduce_apply(jnp.where(first, jnp.where(ky == 0, 0.0, s), 0.0), 0, load, ib)
-        up = reduce_apply(jnp.where(last, jnp.where(ky == nyd - 1, 0.0, s), 0.0), 0, load, ib)
+        lo = reduce_apply(jnp.where(first, jnp.where(ky == 0, 0.0, 1.0), jnp.zeros(m.shape, F32)), 0, load, ib)
+        up = reduce_apply(jnp.where(last, jnp.where(ky == nyd - 1, 0.0, 1.0), jnp.zeros(m.shape, F32)), 0, load, ib)
         phy[x] = lo
         psy[x] = up
         cy[0, x:x + 1] = lo[0:1]
         cy[1, x:x + 1] = up[0:1]
         cy[2, x:x + 1] = up[ny - 1:ny]
-    s = H * cp[0]
-    d = 1.0 + s * jnp.where(kx == 0, 1.0, 2.0)
-    r = jnp.where(kx == 0, 0.0, s)
+    for j in range(nyd):
+        send[j, 0:3] = cy[...]
+    ready()
+    pe1[0] = el[1, 0]
+    ph2[0] = mg[2, nx - 1]
+    for x in range(nx):
+        pe2[x:x + 1] = el[2, x][0:1]
+        ph0[x:x + 1] = mg[0, x][ny - 1:ny]
+    for j in range(nyd):
+        send[j, 3] = jnp.where(j > ky, ph0[...], pe2[...])
+
+
+def factor_kernel(nxd, si, zk, zib, ex, phx, psx, cx):
+    kx = lax.axis_index("gx")
+    nx, ny, nz = si.shape
+    lane = iota(1, (ny, nz))
+    for x in range(nx):
+        a = jnp.where(lane == 0, 0.0, jnp.full((ny, nz), -1.0, F32))
+        b = si[x] + jnp.where(lane == 0, 1.0, jnp.full((ny, nz), 2.0, F32))
+
+        def store(level, ka, kc):
+            zk[2 * level, x] = ka
+            zk[2 * level + 1, x] = kc
+
+        zib[x] = reduce_factors(a, b, 1, store)
+    d = si[0] + jnp.where(kx == 0, 1.0, 2.0)
+    r = jnp.full((ny, nz), jnp.where(kx == 0, 0.0, 1.0), F32)
     phx[0] = r
-    xf[0, 0] = jnp.zeros_like(s)
     for x in range(nx):
         e = 1.0 / d
-        xf[1, x] = e
-        xf[2, x] = s * e
+        ex[x] = e
         if x < nx - 1:
-            sn = H * cp[x + 1]
-            p = sn * e
-            xf[0, x + 1] = p
-            d = 1.0 + 2.0 * sn - p * s
-            r = p * r
+            d = si[x + 1] + (2.0 - e)
+            r = e * r
             phx[x + 1] = r
-            s = sn
-    u = xf[1, nx - 1] * r
-    w = jnp.where(kx == nxd - 1, 0.0, xf[2, nx - 1])
+    u = ex[nx - 1] * r
+    w = ex[nx - 1] * jnp.where(kx == nxd - 1, 0.0, 1.0)
     phx[nx - 1] = u
     psx[nx - 1] = w
     cx[2] = w
     for x in range(nx - 2, -1, -1):
-        u = xf[1, x] * phx[x] + xf[2, x] * u
-        w = xf[2, x] * w
+        u = ex[x] * (phx[x] + u)
+        w = ex[x] * w
         phx[x] = u
         psx[x] = w
     cx[0] = u
     cx[1] = w
 
 
-def zfactor_kernel(cp, zk, zib):
-    nx, ny, nz = cp.shape
-    lane = iota(1, (ny, nz))
-    for x in range(nx):
-        s = H * cp[x]
-        a = jnp.where(lane == 0, 0.0, -s)
-        c = jnp.where(lane == nz - 1, 0.0, -s)
-        b = 1.0 + s * jnp.where(lane == 0, 1.0, 2.0)
-
-        def store(level, ka, kc):
-            zk[2 * level, x] = ka
-            zk[2 * level + 1, x] = kc
-
-        zib[x] = reduce_factors(a, b, c, 1, store)
-
-
 def z_load(zk, x):
     return lambda level: (zk[2 * level, x], zk[2 * level + 1, x])
 
 
-def chain_x_kernel(nyd, el, mg, dm, cp, yk, yib, cy, e1_up, iz_out, up_out, send, pair):
-    nx, ny, nz = dm.shape
+def chain_x_kernel(el, mg, ds, yk, yib, e1_up, iz_out, up_out, pair):
+    nx, ny, nz = ds.shape
     for x in range(nx):
         above = el[1, x + 1] if x < nx - 1 else e1_up[0]
         iz = mg[2, x] - H * (above - el[1, x])
         iz_out[x] = iz
         h1 = mg[1, x]
-        rhs = dm[x] * el[0, x] + cp[x] * ((iz - prev_y(iz, 0.0)) - (h1 - prev_z(h1)))
+        rhs = ds[x] * el[0, x] + ((iz - prev_y(iz, 0.0)) - (h1 - prev_z(h1))) * (1.0 / H)
         u = reduce_apply(rhs, 0, z_load(yk, x), yib[x])
         up_out[x] = u
         pair[0, x:x + 1] = u[0:1]
         pair[1, x:x + 1] = u[ny - 1:ny] - iz[ny - 1:ny] * (1.0 / H)
-    for j in range(nyd):
-        send[j, 0:3] = cy[...]
-        send[j, 3:5] = pair[...]
-
-
-def chain_z_kernel(el, mg, dm, cp, xf, h0_low, iy_out, up_out, pair):
-    nx, ny, nz = dm.shape
+
+
+def chain_z_kernel(el, mg, ds, ex, h0_low, iy_out, up_out, pair):
+    nx, ny, nz = ds.shape
     rhs = []
     below = jnp.zeros((ny, nz), F32)
     for x in range(nx):
@@ -270,40 +266,46 @@
         iy = mg[1, x] - H * (next_z(e0) - e0)
         iy_out[x] = iy
         h0 = mg[0, x]
-        rhs.append(dm[x] * el[2, x] + cp[x] * ((iy - below) - (h0 - prev_y(h0, h0_low[x]))))
+        rhs.append(ds[x] * el[2, x] + ((iy - below) - (h0 - prev_y(h0, h0_low[x:x + 1]))) * (1.0 / H))
         below = iy
-    sweep_x(rhs, xf, up_out)
+    sweep_x(rhs, ex, up_out)
     pair[0] = up_out[0]
     pair[1] = up_out[nx - 1] - below * (1.0 / H)
 
 
-def center_y_kernel(el, mg, dm, cp, zk, zib, e2_up, h2_low, sx_out, t1_out):
-    nx, ny, nz = dm.shape
+def center_y_kernel(el, mg, ds, zk, zib, e2_up, h2_low, sx_out, t1_out):
+    nx, ny, nz = ds.shape
     for x in range(nx):
         e2 = el[2, x]
-        ix = mg[0, x] - H * (next_y(e2, e2_up[x]) - e2)
+        ix = mg[0, x] - H * (next_y(e2, e2_up[x:x + 1]) - e2)
         below = mg[2, x - 1] if x > 0 else h2_low[0]
-        rhs = dm[x] * el[1, x] + cp[x] * ((ix - prev_z(ix)) - (mg[2, x] - below))
+        rhs = ds[x] * el[1, x] + ((ix - prev_z(ix)) - (mg[2, x] - below)) * (1.0 / H)
         cy = reduce_apply(rhs, 1, z_load(zk, x), zib[x])
         curl = H * (next_z(cy) - cy)
         mx = ix + curl
         sx_out[x] = mx + curl
-        t1_out[x] = dm[x] * cy + cp[x] * (mx - prev_z(mx))
-
-
-def half_x_kernel(nxd, ready, recv, cy, up, iz, t1, dm, cp, phy, psy, xf, coef_x, pair_z, sz_out, t4_out, ufy_out, send, weights, consts, mixed, edge):
+        t1_out[x] = ds[x] * cy + (mx - prev_z(mx)) * (1.0 / H)
+
+
+def scan_y_kernel(ready, recv, own, pair, weights, consts, send, h0_low, e2_up, mixed):
     ky = lax.axis_index("gy")
-    nx, ny, nz = dm.shape
     n = recv.shape[0]
-    interface_factors(lambda j: (recv[j, 0], recv[j, 1], recv[j, 2]), (cy[0], cy[1], cy[2]), n, ky, weights, mixed, consts)
-    A, C = gather_sums_pair(lambda j: (recv[j, 3], recv[j, 4]), weights, mixed, n, ky)
+    h0_low[...] = jnp.where(ky == 0, 0.0, recv[jnp.maximum(ky - 1, 0), 3])
+    e2_up[...] = jnp.where(ky == n - 1, 0.0, recv[jnp.minimum(ky + 1, n - 1), 3])
+    interface_factors(lambda j: (recv[j, 0], recv[j, 1], recv[j, 2]), (own[0], own[1], own[2]),
+                      n, ky, weights, mixed, consts)
     ready()
-    for x in range(nx):
-        edge[0, x:x + 1] = up[x][0:1]
-        edge[1, x:x + 1] = up[x][ny - 1:ny] - iz[x][ny - 1:ny] * (1.0 / H)
-    lower, upper = boundary(A, C, edge[0], edge[1], consts)
+    fill_send(send, pair[0], pair[1], consts, n, ky)
+
+
+def half_x_kernel(nxd, ready, recv, weights, consts, pair_x, up, iz, t1, ds, phy, psy, ex, coef_x, pair_z, sz_out, t4_out, ufy_out, send, edge):
+    ky = lax.axis_index("gy")
+    nx, ny, nz = ds.shape
+    A, C = gather_sums(recv, weights, recv.shape[0], ky)
+    lower, upper = boundary(A, C, pair_x[0], pair_x[1], consts)
     edge[0] = lower
     edge[1] = upper
+    ready()
     rhs = []
     below = jnp.zeros((ny, nz), F32)
     for x in range(nx):
@@ -315,10 +317,10 @@
         sz = mz + curl
         sz_out[x] = sz
         mlow = jnp.where(ky == 0, 0.0, H * (cx[0:1] - lo))
-        t4_out[x] = dm[x] * cx + cp[x] * (mz - prev_y(mz, mlow))
-        rhs.append(t1[x] - cp[x] * (sz - below))
+        t4_out[x] = ds[x] * cx + (mz - prev_y(mz, mlow)) * (1.0 / H)
+        rhs.append(t1[x] - (sz - below) * (1.0 / H))
         below = sz
-    sweep_x(rhs, xf, ufy_out)
+    sweep_x(rhs, ex, ufy_out)
     f = ufy_out[0]
     l = ufy_out[nx - 1] + below * (1.0 / H)
     for j in range(nxd):
@@ -330,10 +332,10 @@
         send[j, 6] = l
 
 
-def half_z_kernel(ready, recv, cx, pair_z, up, iy, sx, ufy, sz, dm, cp, phx, psx, yk, yib, consts_y, sy_out, ufz_out, pair_out, edge_y_out, send, weights, mixed, consts):
+def half_z_kernel(ready, recv, cx, pair_z, up, iy, sx, ufy, sz, ds, phx, psx, yk, yib, consts_y, sy_out, ufz_out, pair_out, edge_y_out, send, weights, mixed, consts):
     kx = lax.axis_index("gx")
     ky = lax.axis_index("gy")
-    nx, ny, nz = dm.shape
+    nx, ny, nz = ds.shape
     n = recv.shape[0]
     interface_factors(lambda j: (recv[j, 0], recv[j, 1], recv[j, 2]), (cx[0], cx[1], cx[2]), n, kx, weights, mixed, consts)
     A, C = gather_sums_pair(lambda j: (recv[j, 5], recv[j, 6]), weights, mixed, n, kx)
@@ -351,7 +353,7 @@
         my = iy[x] + curl
         sy_out[x] = my + curl
         s = sx[x]
-        rhs = dm[x] * cz + cp[x] * ((my - below) - (s - prev_y(s, 0.0)))
+        rhs = ds[x] * cz + ((my - below) - (s - prev_y(s, 0.0))) * (1.0 / H)
         u = reduce_apply(rhs, 0, z_load(yk, x), yib[x])
         ufz_out[x] = u
         pair_out[0, x:x + 1] = u[0:1]
@@ -361,11 +363,11 @@
     fill_send(send, pair_out[0], pair_out[1], consts_y, send.shape[0], ky)
 
 
-def final_x_kernel(t4, sy, cp, zk, zib, fx_out, my_out):
-    nx, ny, nz = cp.shape
+def final_x_kernel(t4, sy, zk, zib, fx_out, my_out):
+    nx = t4.shape[0]
     for x in range(nx):
         s = sy[x]
-        fx = reduce_apply(t4[x] - cp[x] * (s - prev_z(s)), 1, z_load(zk, x), zib[x])
+        fx = reduce_apply(t4[x] - (s - prev_z(s)) * (1.0 / H), 1, z_load(zk, x), zib[x])
         fx_out[x] = fx
         my_out[x] = s - H * (next_z(fx) - fx)
 
@@ -450,7 +452,7 @@
     return body
 
 
-def call(kernel, outs, *args, smem=(), near=(), near_out=(), scratch=(), first=None, name=None):
+def call(kernel, outs, *args, smem=(), near=(), near_out=(), scratch=(), first=None, room=ROOM, name=None):
     kinds_in = ["s" if i in smem else "v" if i in near else "h" for i in range(len(args))]
     kinds_out = ["v" if i in near_out else "h" for i in range(len(outs))]
     held = []
@@ -469,7 +471,7 @@
         out_specs=[pl.BlockSpec(memory_space=spec[k]) for k in kinds_out],
         scratch_shapes=held + list(scratch) + [pltpu.SemaphoreType.DMA((len(held),))],
         cost_estimate=pl.CostEstimate(flops=4 * nbytes, bytes_accessed=nbytes, transcendentals=0),
-        compiler_params=pltpu.CompilerParams(vmem_limit_bytes=60 << 20),
+        compiler_params=pltpu.CompilerParams(vmem_limit_bytes=room << 20),
         name=name,
     )(*args)
 
@@ -504,34 +506,39 @@
         return body
 
 
-    dm, cp, yk, yib, phy, psy, xf, phx, psx, cy, cx = call(
-        bind(coef_kernel, nxd, nyd),
-        [cell, cell, (2 * len(strides(ny)),) + cell, cell, cell, cell, (3,) + cell, cell, cell, (3,) + py, (3,) + px],
-        material, permittivity, conductivity, smem=(1, 2), name="coef")
-    e1_up = shifted(lax.optimization_barrier((electric[1, 0:1], cx))[0], "gx", -1)
-    iz, ux, send1 = call(bind(chain_x_kernel, nyd), [cell, cell, (nyd, 5) + py],
-                         electric, magnetic, dm, cp, yk, yib, cy, e1_up, scratch=[pltpu.VMEM((2,) + py, F32)], name="chain_x")
+    ds, si, yk, yib, phy, psy, cy, send_c, pe1, ph2 = call(
+        bind(coef_kernel, nyd),
+        [cell, cell, (2 * len(strides(ny)),) + cell, cell, cell, cell, (3,) + py, (nyd, 4) + py,
+         (1,) + px, (1,) + px],
+        material, permittivity, conductivity, electric, magnetic, smem=(1, 2), first=3, room=60,
+        scratch=[pltpu.VMEM(py, F32), pltpu.VMEM(py, F32)], name="coef")
+    recv_c = exchange(send_c, "gy")
+    e1_up = shifted(pe1, "gx", -1)
+    h2_low = shifted(ph2, "gx", 1)
+    zk, zib, ex, phx, psx, cx = call(
+        bind(factor_kernel, nxd), [(2 * len(strides(nz)),) + cell, cell, cell, cell, cell, (3,) + px], si, name="factor")
+    e1_up, h2_low, cx = lax.optimization_barrier((e1_up, h2_low, cx))
+    iz, ux, pair_x = call(chain_x_kernel, [cell, cell, (2,) + py],
+                          electric, magnetic, ds, yk, yib, e1_up, name="chain_x")
+    wy, ky, send1, h0_low, e2_up = call(scan_y_kernel, [(nyd,) + py, (9,) + py, (nyd,) + py, py, py], recv_c, cy, pair_x,
+                         first=2, scratch=[pltpu.VMEM((nyd,) + py, F32)], name="scan_y")
     recv1 = exchange(send1, "gy")
 
-    h0_low = shifted(magnetic[0, :, ny - 1:ny], "gy", 1)
-    e2_up = shifted(electric[2, :, 0:1], "gy", -1)
-    h2_low = shifted(magnetic[2, nx - 1:nx], "gx", 1)
-    zk, zib = call(zfactor_kernel, [(2 * len(strides(nz)),) + cell, cell], cp, name="zfactor")
-    iy, uz, pair_z = call(chain_z_kernel, [cell, cell, (2,) + px], electric, magnetic, dm, cp, xf, h0_low, name="chain_z")
-    sx, t1 = call(center_y_kernel, [cell, cell], electric, magnetic, dm, cp, zk, zib, e2_up, h2_low, name="center_y")
-
-    sz, t4, ufy, send2, wy, ky = call(
-        bind(half_x_kernel, nxd), [cell, cell, cell, (nxd, 7) + px, (nyd,) + py, (9,) + py],
-        recv1, cy, ux, iz, t1, dm, cp, phy, psy, xf, cx, pair_z,
-        first=2, scratch=[pltpu.VMEM((nyd,) + py, F32), pltpu.VMEM((2,) + py, F32)], name="half_x")
+    iy, uz, pair_z = call(chain_z_kernel, [cell, cell, (2,) + px], electric, magnetic, ds, ex, h0_low, name="chain_z")
+    sx, t1 = call(center_y_kernel, [cell, cell], electric, magnetic, ds, zk, zib, e2_up, h2_low, name="center_y")
+
+    sz, t4, ufy, send2 = call(
+        bind(half_x_kernel, nxd), [cell, cell, cell, (nxd, 7) + px],
+        recv1, wy, ky, pair_x, ux, iz, t1, ds, phy, psy, ex, cx, pair_z,
+        first=4, scratch=[pltpu.VMEM((2,) + py, F32)], name="half_x")
     recv2 = exchange(send2, "gx")
     sy, ufz, pair4, edge_y, send3 = call(
         half_z_kernel, [cell, cell, (2,) + py, (2,) + px, (nyd,) + py],
-        recv2, cx, pair_z, uz, iy, sx, ufy, sz, dm, cp, phx, psx, yk, yib, ky,
+        recv2, cx, pair_z, uz, iy, sx, ufy, sz, ds, phx, psx, yk, yib, ky,
         first=2, scratch=[pltpu.VMEM((nxd,) + px, F32), pltpu.VMEM((nxd,) + px, F32), pltpu.VMEM((9,) + px, F32)],
         name="half_z")
     recv3 = exchange(send3, "gy")
-    fx, my = call(final_x_kernel, [cell, cell], t4, sy, cp, zk, zib, name="final_x")
+    fx, my = call(final_x_kernel, [cell, cell], t4, sy, zk, zib, name="final_x")
     fy, mz = call(final_y_kernel, [cell, cell], edge_y, ufy, sz, phx, psx, name="final_y")
     e, h = call(final_z_kernel, [(3,) + cell, (3,) + cell],
                 recv3, wy, ky, pair4, ufz, sx, phy, psy, fx, fy, my, mz,

time: 89.2 us -> 83.2 us (0.933)
  local copies, waits for them, and re-layouts: 6.78 us -> 2.99 us
  waiting for transfers between devices: 8.21 us -> 4.97 us
  blocking collectives: 14.5 us -> 16 us
  Pallas kernels: 32.5 us -> 31.1 us
  starting transfers between devices: 25.7 us -> 26.6 us
    all_to_all x2 -> x3, starting transfers between devices: 12.8 us -> 19.4 us  [exchange(): return lax.all_to_all(array, axis, 0, 0)]
    ppermute x4 -> x2, waiting for transfers between devices: 6.08 us -> 0.01 us  [shifted(): lax.ppermute(array, axis, [(i, i + by) for i in range(count) if 0 <= i +...]
    ppermute x4 -> x2, starting transfers between devices: 12.8 us -> 7.15 us  [shifted(): lax.ppermute(array, axis, [(i, i + by) for i in range(count) if 0 <= i +...]
    squeeze x4 -> x0, local copies, waits for them, and re-layouts: 3.24 us -> none  [the longest x1 0.92 us: per_device(): h0_low = shifted(magnetic[0, :, ny - 1:ny], 'gy', 1)]
    all_to_all x2 -> x3, waiting for transfers between devices: 2.13 us -> 4.97 us  [exchange(): return lax.all_to_all(array, axis, 0, 0)]
    all_to_all x1, blocking collectives: 14.5 us -> 16 us  [exchange(): return lax.all_to_all(array, axis, 0, 0)]
    pallas_call x10 -> x11, Pallas kernels: 32.5 us -> 31.1 us  [call(): pl.pallas_call(staged(kernel, kinds_in, kinds_out, first), out_shape=[jax...]
    unnamed x12 -> x14, local copies, waits for them, and re-layouts: 3.54 us -> 2.99 us
  transfers between devices with their start and end apart: 6 -> 5, of which waited for: 2 -> 3; matrix products, arithmetic and copies ran while one was open for 3% -> 0% of each run, Pallas kernels for 21% -> 22%
where the time goes in v3:
time: 83.2 us; the launch traced here: 82.4 us
  Pallas kernels  31.1 us (37%)
  starting transfers between devices  26.6 us (32%)
  blocking collectives  16 us (19%)
  waiting for transfers between devices  4.97 us (6%)
  local copies, waits for them, and re-layouts  2.99 us (4%)
    pallas_call x11, Pallas kernels, call(): pl.pallas_call(staged(kernel, kinds_in, kinds_out, first), out_shape=[jax...  31.1 us
    all_to_all x3, starting transfers between devices, exchange(): return lax.all_to_all(array, axis, 0, 0)  19.4 us
    all_to_all x1, blocking collectives, exchange(): return lax.all_to_all(array, axis, 0, 0)  16 us
    ppermute x2, starting transfers between devices, shifted(): lax.ppermute(array, axis, [(i, i + by) for i in range(count) if 0 <= i +...  7.15 us
    all_to_all x3, waiting for transfers between devices, exchange(): return lax.all_to_all(array, axis, 0, 0)  4.97 us
    unnamed x14, local copies, waits for them, and re-layouts  2.99 us
  transfers between devices with their start and end apart: 5, of which 3 were waited for; matrix products, arithmetic and copies ran while one was open for 0% of the time, Pallas kernels for 22%

profile of v3, /device:TPU:1, one launch (start us, length us, event | category | flops | bytes accessed | tf_op | source)
XLA Modules:
  0.0 82.4 jit_solution(14974785755133678649)
XLA Ops:
  0.6 3.1 %coef.1 = (f32[16,8,256]{2,1,0:T(8,128)}, f32[16,8,256]{2,1,0:T(8,128)}, f32[6,16,8,256]{3,2,1,0:T(8,128)}, f32[16,8,256]{2,1,0:T(8,128)}, f32[16,8,256]{2,1,0:T...) custom-call(s32[16,8,256]{2,1,0:T(8,128)} %refs_0_.4, ...), custom_call_target="tpu_custom_call" | custom-call | flops 13893888 | bytes 3473472 | tf_op jit(solution)/shard_map/coef/pallas_call | solution.py:467
  3.7 0.0 copy-start.6
  3.7 0.0 copy-start.5
  3.7 7.3 %all-to-all-start = ((f32[16,4,16,256]{3,2,1,0:T(8,128)}), f32[16,4,16,256]{3,2,1,0:T(8,128)S(1)}, u32[]{:S(2)}, u32[]{:S(2)}) async-start(f32[16,4,16,256]{3,2,1,0:T(8,128)} %get-tuple-element.47), calls=%async_computation | async-start | bytes 2097152 | tf_op jit(solution)/shard_map/all_to_all | solution.py:492
  11.0 0.0 copy-done.6
  11.0 1.3 %collective-permute-start = (f32[1,8,256]{2,1,0:T(8,128)S(1)}, f32[1,8,256]{2,1,0:T(8,128)S(1)}, u32[]{:S(2)}, u32[]{:S(2)}) collective-permute-start(f32[1,8,256]{2,1,0:T(8,128)S(1)} %copy-done.6), channel_id=1, source_target_pairs={{16,0},{32,16},{48,32},{64,48},{80,64},{96,80},{112,96},{17,1},{33... | collective-permute-start | bytes 24584 | tf_op jit(solution)/shard_map/ppermute | solution.py:488
  12.3 0.0 copy-done.5
  12.4 5.9 %collective-permute-start.1 = (f32[1,8,256]{2,1,0:T(8,128)S(1)}, f32[1,8,256]{2,1,0:T(8,128)S(1)}, u32[]{:S(2)}, u32[]{:S(2)}) collective-permute-start(f32[1,8,256]{2,1,0:T(8,128)S(1)} %copy-done.5), channel_id=1, source_target_pairs={{0,16},{16,32},{32,48},{48,64},{64,80},{80,96},{96,112},{1,17},{17... | collective-permute-start | bytes 24584 | tf_op jit(solution)/shard_map/ppermute | solution.py:488
  18.2 4.5 %factor.1 = (f32[16,16,8,256]{3,2,1,0:T(8,128)}, f32[16,8,256]{2,1,0:T(8,128)}, f32[16,8,256]{2,1,0:T(8,128)}, f32[16,8,256]{2,1,0:T(8,128)}, f32[16,8,256]{2,1,0:T(8,128)}, /*index=5*/f32[3,8,256]{2,1,0:T(8,128)}) custom-call(f32[16,8,256]{2,1,0:T(8,128)} %get-tuple-element.54.refs_0_), custom_call_target="tpu_custom_call" | custom-call | flops 11108352 | bytes 2777088 | tf_op jit(solution)/shard_map/factor/pallas_call | solution.py:467
  22.7 0.0 collective-permute-done.refs_5_
  22.7 0.0 copy-start.4
  22.8 0.0 collective-permute-done.1.refs_6_
  22.8 0.0 copy-start.3
  22.8 0.6 copy-done.4
  23.3 2.4 %chain_x.1 = (f32[16,8,256]{2,1,0:T(8,128)}, f32[16,8,256]{2,1,0:T(8,128)}, f32[2,16,256]{2,1,0:T(8,128)}) custom-call(f32[3,16,8,256]{3,2,1,0:T(8,128)} %refs_0_.7, f32[3,16,8,256]{3,2,1,0:T(8,128)} %refs_1_.7, f32[16,8,256]{2,1,0:T(8,128)} %get-tuple-element.49.refs_2_.refs_7_.refs_8_, f32[6,16,8,256]{3,2,1,0:T(8,128)} %get-tuple-element.50.refs_3_.refs_11_, ...), custom_call_target="tpu_custom_call" | custom-call | flops 8552448 | bytes 2138112 | tf_op jit(solution)/shard_map/chain_x/pallas_call | solution.py:467
  25.8 1.0 %all-to-all-done.refs_0_ = f32[16,4,16,256]{3,2,1,0:T(8,128)S(1)} async-done(((f32[16,4,16,256]{3,2,1,0:T(8,128)}), f32[16,4,16,256]{3,2,1,0:T(8,128)S(1)}, u32[]{:S(2)}, u32[]{:S(2)}) %all-to-all-start) | async-done | bytes 1048608 | tf_op jit(solution)/shard_map/all_to_all | solution.py:492
  26.8 1.0 %copy-done = f32[16,4,16,256]{3,2,1,0:T(8,128)} copy-done((f32[16,4,16,256]{3,2,1,0:T(8,128)}, f32[16,4,16,256]{3,2,1,0:T(8,128)S(1)}, u32[]{:S(2)}) %copy-start) | copy-done | bytes 1048600
  27.7 2.4 %scan_y.1 = (f32[16,16,256]{2,1,0:T(8,128)}, f32[9,16,256]{2,1,0:T(8,128)}, f32[16,16,256]{2,1,0:T(8,128)}, f32[16,256]{1,0:T(8,128)}, f32[16,256]{1,0:T(8,128)}) custom-call(f32[16,4,16,256]{3,2,1,0:T(8,128)} %copy-done, f32[3,16,256]{2,1,0:T(8,128)} %get-tuple-element.48.refs_1_, f32[2,16,256]{2,1,0:T(8,128)} %get-tuple-element.57.refs_2_.refs_3_), custom_call_target="tpu_custom_call" | custom-call | flops 7340032 | bytes 1835008 | tf_op jit(solution)/shard_map/scan_y/pallas_call | solution.py:467
  30.1 6.7 %all-to-all-start.1 = ((f32[16,16,256]{2,1,0:T(8,128)}), f32[16,16,256]{2,1,0:T(8,128)S(1)}, u32[]{:S(2)}, u32[]{:S(2)}) async-start(f32[16,16,256]{2,1,0:T(8,128)} %get-tuple-element.58), calls=%async_computation.1 | async-start | bytes 524288 | tf_op jit(solution)/shard_map/all_to_all | solution.py:492
  36.9 2.1 %chain_z.1 = (f32[16,8,256]{2,1,0:T(8,128)}, f32[16,8,256]{2,1,0:T(8,128)}, f32[2,8,256]{2,1,0:T(8,128)}) custom-call(f32[3,16,8,256]{3,2,1,0:T(8,128)} %refs_0_.7, f32[3,16,8,256]{3,2,1,0:T(8,128)} %refs_1_.7, f32[16,8,256]{2,1,0:T(8,128)} %get-tuple-element.49.refs_2_.refs_7_.refs_8_, f32[16,8,256]{2,1,0:T(8,128)} %get-tuple-element.70.refs_3_.refs_10_, ...), custom_call_target="tpu_custom_call" | custom-call | flops 5373952 | bytes 1343488 | tf_op jit(solution)/shard_map/chain_z/pallas_call | solution.py:467
  39.0 3.6 %center_y.1 = (f32[16,8,256]{2,1,0:T(8,128)}, f32[16,8,256]{2,1,0:T(8,128)}) custom-call(f32[3,16,8,256]{3,2,1,0:T(8,128)} %refs_0_.7, f32[3,16,8,256]{3,2,1,0:T(8,128)} %refs_1_.7, f32[16,8,256]{2,1,0:T(8,128)} %get-tuple-element.49.refs_2_.refs_7_.refs_8_, f32[16,16,8,256]{3,2,1,0:T(8,128)} %get-tuple-element.63.refs_3_.refs_2_, ...), custom_call_target="tpu_custom_call" | custom-call | flops 13729792 | bytes 3432448 | tf_op jit(solution)/shard_map/center_y/pallas_call | solution.py:467
  42.5 1.7 %all-to-all-done.1.refs_0_ = f32[16,16,256]{2,1,0:T(8,128)S(1)} async-done(((f32[16,16,256]{2,1,0:T(8,128)}), f32[16,16,256]{2,1,0:T(8,128)S(1)}, u32[]{:S(2)}, u32[]{:S(2)}) %all-to-all-start.1) | async-done | bytes 262176 | tf_op jit(solution)/shard_map/all_to_all | solution.py:492
  44.3 0.7 copy-done.1
  45.0 2.5 %half_x.1 = (f32[16,8,256]{2,1,0:T(8,128)}, f32[16,8,256]{2,1,0:T(8,128)}, f32[16,8,256]{2,1,0:T(8,128)}, f32[8,7,8,256]{3,2,1,0:T(8,128)}) custom-call(f32[16,16,256]{2,1,0:T(8,128)} %copy-done.1, f32[16,16,256]{2,1,0:T(8,128)} %get-tuple-element.59.refs_1_, f32[9,16,256]{2,1,0:T(8,128)} %get-tuple-element.60.refs_2_.refs_13_, ...), custom_call_target="tpu_custom_call" | custom-call | flops 10059776 | bytes 2514944 | tf_op jit(solution)/shard_map/half_x/pallas_call | solution.py:467
  47.5 16.0 %all_to_all.20.refs_0_ = f32[8,7,8,256]{3,2,1,0:T(8,128)} all-to-all(f32[8,7,8,256]{3,2,1,0:T(8,128)} %get-tuple-element.74), channel_id=1, replica_groups=mesh['gx'=8,'gy'=16] {'gx'}, dimensions={0} | all-to-all | bytes 917504 | tf_op jit(solution)/shard_map/all_to_all | solution.py:492
  63.5 2.8 %half_z.1 = (f32[16,8,256]{2,1,0:T(8,128)}, f32[16,8,256]{2,1,0:T(8,128)}, f32[2,16,256]{2,1,0:T(8,128)}, f32[2,8,256]{2,1,0:T(8,128)}, f32[16,16,256]{2,1,0:T(8,128)}) custom-call(f32[8,7,8,256]{3,2,1,0:T(8,128)} %all_to_all.20.refs_0_, f32[3,8,256]{2,1,0:T(8,128)} %get-tuple-element.71.refs_11_.refs_1_, f32[2,8,256]{2,1,0:T(8,128)} %get-tuple-element.73.refs_12_.refs_2_, ...), custom_call_target="tpu_custom_call" | custom-call | flops 12746752 | bytes 3186688 | tf_op jit(solution)/shard_map/half_z/pallas_call | solution.py:467
  66.3 5.4 %all-to-all-start.3 = ((f32[16,16,256]{2,1,0:T(8,128)}), f32[16,16,256]{2,1,0:T(8,128)S(1)}, u32[]{:S(2)}, u32[]{:S(2)}) async-start(f32[16,16,256]{2,1,0:T(8,128)} %get-tuple-element.82), calls=%async_computation.3 | async-start | bytes 524288 | tf_op jit(solution)/shard_map/all_to_all | solution.py:492
  71.7 1.9 %final_y.1 = (f32[16,8,256]{2,1,0:T(8,128)}, f32[16,8,256]{2,1,0:T(8,128)}) custom-call(f32[2,8,256]{2,1,0:T(8,128)} %get-tuple-element.88.refs_0_, f32[16,8,256]{2,1,0:T(8,128)} %get-tuple-element.78.refs_6_.refs_1_, f32[16,8,256]{2,1,0:T(8,128)} %get-tuple-element.79.refs_7_.refs_2_, f32[16,8,256]{2,1,0:T(8,128)} %get-tuple-element.80.refs_9_.refs_3_, ...), custom_call_target="tpu_custom_call" | custom-call | flops 3211264 | bytes 802816 | tf_op jit(solution)/shard_map/final_y/pallas_call | solution.py:467
  73.6 3.3 %final_x.1 = (f32[16,8,256]{2,1,0:T(8,128)}, f32[16,8,256]{2,1,0:T(8,128)}) custom-call(f32[16,8,256]{2,1,0:T(8,128)} %get-tuple-element.85.refs_0_, f32[16,8,256]{2,1,0:T(8,128)} %get-tuple-element.86.refs_1_, f32[16,16,8,256]{3,2,1,0:T(8,128)} %get-tuple-element.63.refs_3_.refs_2_, f32[16,8,256]{2,1,0:T(8,128)} %get-tuple-element.64.refs_4_.refs_3_), custom_call_target="tpu_custom_call" | custom-call | flops 11010048 | bytes 2752512 | tf_op jit(solution)/shard_map/final_x/pallas_call | solution.py:467
  76.9 2.3 %all-to-all-done.3.refs_0_ = f32[16,16,256]{2,1,0:T(8,128)S(1)} async-done(((f32[16,16,256]{2,1,0:T(8,128)}), f32[16,16,256]{2,1,0:T(8,128)S(1)}, u32[]{:S(2)}, u32[]{:S(2)}) %all-to-all-start.3) | async-done | bytes 262176 | tf_op jit(solution)/shard_map/all_to_all | solution.py:492
  79.2 0.7 copy-done.2
  79.9 2.5 %final_z.1 = (f32[3,16,8,256]{3,2,1,0:T(8,128)}, f32[3,16,8,256]{3,2,1,0:T(8,128)}) custom-call(f32[16,16,256]{2,1,0:T(8,128)} %copy-done.2, f32[16,16,256]{2,1,0:T(8,128)} %get-tuple-element.59.refs_1_, f32[9,16,256]{2,1,0:T(8,128)} %get-tuple-element.60.refs_2_.refs_13_, f32[2,16,256]{2,1,0:T(8,128)} %get-tuple-element.83.refs_3_, ...), custom_call_target="tpu_custom_call" | custom-call | flops 10158080 | bytes 2539520 | tf_op jit(solution)/shard_map/final_z/pallas_call | solution.py:467
  (4 shorter events, 0.0 us)
Async XLA Ops:
  3.7 7.3 %copy-start.6 = (f32[1,8,256]{2,1,0:T(8,128)S(1)}, f32[1,8,256]{2,1,0:T(8,128)}, u32[]{:S(2)}) copy-start(f32[1,8,256]{2,1,0:T(8,128)} %get-tuple-element.52) | copy-start | bytes 24580
  3.7 8.6 %copy-start.5 = (f32[1,8,256]{2,1,0:T(8,128)S(1)}, f32[1,8,256]{2,1,0:T(8,128)}, u32[]{:S(2)}) copy-start(f32[1,8,256]{2,1,0:T(8,128)} %get-tuple-element.53) | copy-start | bytes 24580
  3.7 23.0 %all-to-all-start = ((f32[16,4,16,256]{3,2,1,0:T(8,128)}), f32[16,4,16,256]{3,2,1,0:T(8,128)S(1)}, u32[]{:S(2)}, u32[]{:S(2)}) async-start(f32[16,4,16,256]{3,2,1,0:T(8,128)} %get-tuple-element.47), calls=%async_computation | async-start | bytes 2097152 | tf_op jit(solution)/shard_map/all_to_all | solution.py:492
  11.0 11.7 %collective-permute-start = (f32[1,8,256]{2,1,0:T(8,128)S(1)}, f32[1,8,256]{2,1,0:T(8,128)S(1)}, u32[]{:S(2)}, u32[]{:S(2)}) collective-permute-start(f32[1,8,256]{2,1,0:T(8,128)S(1)} %copy-done.6), channel_id=1, source_target_pairs={{16,0},{32,16},{48,32},{64,48},{80,64},{96,80},{112,96},{17,1},{33... | collective-permute-start | bytes 24584 | tf_op jit(solution)/shard_map/ppermute | solution.py:488
  12.4 10.4 %collective-permute-start.1 = (f32[1,8,256]{2,1,0:T(8,128)S(1)}, f32[1,8,256]{2,1,0:T(8,128)S(1)}, u32[]{:S(2)}, u32[]{:S(2)}) collective-permute-start(f32[1,8,256]{2,1,0:T(8,128)S(1)} %copy-done.5), channel_id=1, source_target_pairs={{0,16},{16,32},{32,48},{48,64},{64,80},{80,96},{96,112},{1,17},{17... | collective-permute-start | bytes 24584 | tf_op jit(solution)/shard_map/ppermute | solution.py:488
  22.7 0.6 copy-start.4
  22.8 16.2 %copy-start.3 = (f32[1,8,256]{2,1,0:T(8,128)}, f32[1,8,256]{2,1,0:T(8,128)S(1)}, u32[]{:S(2)}) copy-start(f32[1,8,256]{2,1,0:T(8,128)S(1)} %collective-permute-done.1.refs_6_) | copy-start | bytes 24580
  26.7 1.0 %copy-start = (f32[16,4,16,256]{3,2,1,0:T(8,128)}, f32[16,4,16,256]{3,2,1,0:T(8,128)S(1)}, u32[]{:S(2)}) copy-start(f32[16,4,16,256]{3,2,1,0:T(8,128)S(1)} %all-to-all-done.refs_0_) | copy-start | bytes 3145732
  30.1 14.1 %all-to-all-start.1 = ((f32[16,16,256]{2,1,0:T(8,128)}), f32[16,16,256]{2,1,0:T(8,128)S(1)}, u32[]{:S(2)}, u32[]{:S(2)}) async-start(f32[16,16,256]{2,1,0:T(8,128)} %get-tuple-element.58), calls=%async_computation.1 | async-start | bytes 524288 | tf_op jit(solution)/shard_map/all_to_all | solution.py:492
  44.3 0.7 copy-start.1
  66.3 12.9 %all-to-all-start.3 = ((f32[16,16,256]{2,1,0:T(8,128)}), f32[16,16,256]{2,1,0:T(8,128)S(1)}, u32[]{:S(2)}, u32[]{:S(2)}) async-start(f32[16,16,256]{2,1,0:T(8,128)} %get-tuple-element.82), calls=%async_computation.3 | async-start | bytes 524288 | tf_op jit(solution)/shard_map/all_to_all | solution.py:492
  79.2 0.7 copy-start.2

commit v4 on v3

--- a/solution.py
+++ b/solution.py
@@ -202,6 +202,23 @@
         send[j, 3] = jnp.where(j > ky, ph0[...], pe2[...])
 
 
+def z_solve(si, rhs):
+    n = rhs.shape[1]
+    lane = iota(1, rhs.shape)
+    a = jnp.where(lane == 0, 0.0, jnp.full(rhs.shape, -1.0, F32))
+    b = si + jnp.where(lane == 0, 1.0, jnp.full(rhs.shape, 2.0, F32))
+    r = rhs
+    for s in strides(n):
+        inv = 1.0 / b
+        c = pltpu.roll(a, n - s, 1)
+        ka = -a * pltpu.roll(inv, s, 1)
+        kc = -c * pltpu.roll(inv, n - s, 1)
+        r = r + ka * pltpu.roll(r, s, 1) + kc * pltpu.roll(r, n - s, 1)
+        b = b + ka * a + kc * c
+        a = ka * pltpu.roll(a, s, 1)
+    return r / b
+
+
 def factor_kernel(nxd, si, zk, zib, ex, phx, psx, cx):
     kx = lax.axis_index("gx")
     nx, ny, nz = si.shape
@@ -257,7 +274,7 @@
         pair[1, x:x + 1] = u[ny - 1:ny] - iz[ny - 1:ny] * (1.0 / H)
 
 
-def chain_z_kernel(el, mg, ds, ex, h0_low, iy_out, up_out, pair):
+def chain_z_kernel(el, mg, ds, ex, halo_y, iy_out, up_out, pair):
     nx, ny, nz = ds.shape
     rhs = []
     below = jnp.zeros((ny, nz), F32)
@@ -266,18 +283,18 @@
         iy = mg[1, x] - H * (next_z(e0) - e0)
         iy_out[x] = iy
         h0 = mg[0, x]
-        rhs.append(ds[x] * el[2, x] + ((iy - below) - (h0 - prev_y(h0, h0_low[x:x + 1]))) * (1.0 / H))
+        rhs.append(ds[x] * el[2, x] + ((iy - below) - (h0 - prev_y(h0, halo_y[0, x:x + 1]))) * (1.0 / H))
         below = iy
     sweep_x(rhs, ex, up_out)
     pair[0] = up_out[0]
     pair[1] = up_out[nx - 1] - below * (1.0 / H)
 
 
-def center_y_kernel(el, mg, ds, zk, zib, e2_up, h2_low, sx_out, t1_out):
+def center_y_kernel(el, mg, ds, zk, zib, halo_y, h2_low, sx_out, t1_out):
     nx, ny, nz = ds.shape
     for x in range(nx):
         e2 = el[2, x]
-        ix = mg[0, x] - H * (next_y(e2, e2_up[x:x + 1]) - e2)
+        ix = mg[0, x] - H * (next_y(e2, halo_y[1, x:x + 1]) - e2)
         below = mg[2, x - 1] if x > 0 else h2_low[0]
         rhs = ds[x] * el[1, x] + ((ix - prev_z(ix)) - (mg[2, x] - below)) * (1.0 / H)
         cy = reduce_apply(rhs, 1, z_load(zk, x), zib[x])
@@ -287,11 +304,11 @@
         t1_out[x] = ds[x] * cy + (mx - prev_z(mx)) * (1.0 / H)
 
 
-def scan_y_kernel(ready, recv, own, pair, weights, consts, send, h0_low, e2_up, mixed):
+def scan_y_kernel(ready, recv, own, pair, weights, consts, send, halo, mixed):
     ky = lax.axis_index("gy")
     n = recv.shape[0]
-    h0_low[...] = jnp.where(ky == 0, 0.0, recv[jnp.maximum(ky - 1, 0), 3])
-    e2_up[...] = jnp.where(ky == n - 1, 0.0, recv[jnp.minimum(ky + 1, n - 1), 3])
+    halo[0] = jnp.where(ky == 0, 0.0, recv[jnp.maximum(ky - 1, 0), 3])
+    halo[1] = jnp.where(ky == n - 1, 0.0, recv[jnp.minimum(ky + 1, n - 1), 3])
     interface_factors(lambda j: (recv[j, 0], recv[j, 1], recv[j, 2]), (own[0], own[1], own[2]),
                       n, ky, weights, mixed, consts)
     ready()
@@ -363,11 +380,11 @@
     fill_send(send, pair_out[0], pair_out[1], consts_y, send.shape[0], ky)
 
 
-def final_x_kernel(t4, sy, zk, zib, fx_out, my_out):
+def final_x_kernel(t4, sy, si, fx_out, my_out):
     nx = t4.shape[0]
     for x in range(nx):
         s = sy[x]
-        fx = reduce_apply(t4[x] - (s - prev_z(s)) * (1.0 / H), 1, z_load(zk, x), zib[x])
+        fx = z_solve(si[x], t4[x] - (s - prev_z(s)) * (1.0 / H))
         fx_out[x] = fx
         my_out[x] = s - H * (next_z(fx) - fx)
 
@@ -452,9 +469,9 @@
     return body
 
 
-def call(kernel, outs, *args, smem=(), near=(), near_out=(), scratch=(), first=None, room=ROOM, name=None):
-    kinds_in = ["s" if i in smem else "v" if i in near else "h" for i in range(len(args))]
-    kinds_out = ["v" if i in near_out else "h" for i in range(len(outs))]
+def call(kernel, outs, *args, smem=(), near=(), near_out=(), scratch=(), first=None, room=ROOM, hot=False, far=(), name=None):
+    kinds_in = ["s" if i in smem else "v" if i in near or (hot and i not in far) else "h" for i in range(len(args))]
+    kinds_out = ["v" if i in near_out or (hot and name.startswith(("final_x", "final_y"))) else "h" for i in range(len(outs))]
     held = []
     for a, kind in zip(args, kinds_in):
         if kind != "v":
@@ -465,11 +482,11 @@
     spec = {"v": pltpu.VMEM, "h": HBM, "s": HBM}
     nbytes = sum(4 * _size(a.shape) for a in args) + sum(4 * _size(o) for o in outs)
     return pl.pallas_call(
-        staged(kernel, kinds_in, kinds_out, first),
+        staged(kernel, kinds_in, kinds_out, 0 if hot and first is not None else first),
         out_shape=[jax.ShapeDtypeStruct(o, F32) for o in outs],
         in_specs=[pl.BlockSpec(memory_space=spec[k]) for k in kinds_in],
         out_specs=[pl.BlockSpec(memory_space=spec[k]) for k in kinds_out],
-        scratch_shapes=held + list(scratch) + [pltpu.SemaphoreType.DMA((len(held),))],
+        scratch_shapes=held + list(scratch) + [pltpu.SemaphoreType.DMA((max(len(held), 1),))],
         cost_estimate=pl.CostEstimate(flops=4 * nbytes, bytes_accessed=nbytes, transcendentals=0),
         compiler_params=pltpu.CompilerParams(vmem_limit_bytes=room << 20),
         name=name,
@@ -519,30 +536,30 @@
         bind(factor_kernel, nxd), [(2 * len(strides(nz)),) + cell, cell, cell, cell, cell, (3,) + px], si, name="factor")
     e1_up, h2_low, cx = lax.optimization_barrier((e1_up, h2_low, cx))
     iz, ux, pair_x = call(chain_x_kernel, [cell, cell, (2,) + py],
-                          electric, magnetic, ds, yk, yib, e1_up, name="chain_x")
-    wy, ky, send1, h0_low, e2_up = call(scan_y_kernel, [(nyd,) + py, (9,) + py, (nyd,) + py, py, py], recv_c, cy, pair_x,
-                         first=2, scratch=[pltpu.VMEM((nyd,) + py, F32)], name="scan_y")
+                          electric, magnetic, ds, yk, yib, e1_up, hot=True, far=(0, 1), room=40, name="chain_x")
+    wy, ky, send1, halo_y = call(scan_y_kernel, [(nyd,) + py, (9,) + py, (nyd,) + py, (2,) + py], recv_c, cy, pair_x,
+                         first=2, scratch=[pltpu.VMEM((nyd,) + py, F32)], hot=True, room=40, name="scan_y")
     recv1 = exchange(send1, "gy")
 
-    iy, uz, pair_z = call(chain_z_kernel, [cell, cell, (2,) + px], electric, magnetic, ds, ex, h0_low, name="chain_z")
-    sx, t1 = call(center_y_kernel, [cell, cell], electric, magnetic, ds, zk, zib, e2_up, h2_low, name="center_y")
+    iy, uz, pair_z = call(chain_z_kernel, [cell, cell, (2,) + px], electric, magnetic, ds, ex, halo_y, name="chain_z")
+    sx, t1 = call(center_y_kernel, [cell, cell], electric, magnetic, ds, zk, zib, halo_y, h2_low, name="center_y")
 
     sz, t4, ufy, send2 = call(
         bind(half_x_kernel, nxd), [cell, cell, cell, (nxd, 7) + px],
         recv1, wy, ky, pair_x, ux, iz, t1, ds, phy, psy, ex, cx, pair_z,
-        first=4, scratch=[pltpu.VMEM((2,) + py, F32)], name="half_x")
+        first=4, scratch=[pltpu.VMEM((2,) + py, F32)], hot=True, room=40, name="half_x")
     recv2 = exchange(send2, "gx")
     sy, ufz, pair4, edge_y, send3 = call(
         half_z_kernel, [cell, cell, (2,) + py, (2,) + px, (nyd,) + py],
         recv2, cx, pair_z, uz, iy, sx, ufy, sz, ds, phx, psx, yk, yib, ky,
         first=2, scratch=[pltpu.VMEM((nxd,) + px, F32), pltpu.VMEM((nxd,) + px, F32), pltpu.VMEM((9,) + px, F32)],
-        name="half_z")
+        hot=True, room=40, name="half_z")
     recv3 = exchange(send3, "gy")
-    fx, my = call(final_x_kernel, [cell, cell], t4, sy, zk, zib, name="final_x")
-    fy, mz = call(final_y_kernel, [cell, cell], edge_y, ufy, sz, phx, psx, name="final_y")
+    fx, my = call(final_x_kernel, [cell, cell], t4, sy, si, hot=True, room=40, name="final_x")
+    fy, mz = call(final_y_kernel, [cell, cell], edge_y, ufy, sz, phx, psx, hot=True, room=40, name="final_y")
     e, h = call(final_z_kernel, [(3,) + cell, (3,) + cell],
                 recv3, wy, ky, pair4, ufz, sx, phy, psy, fx, fy, my, mz,
-                first=4, scratch=[pltpu.VMEM((2,) + py, F32)], name="final_z")
+                first=4, scratch=[pltpu.VMEM((2,) + py, F32)], hot=True, room=40, name="final_z")
     return e, h
 
 

time: 83.2 us -> 75.5 us (0.907)
  Pallas kernels: 31.1 us -> 24.6 us
  starting transfers between devices: 26.6 us -> 24.8 us
  waiting for transfers between devices: 4.97 us -> 6.61 us
  local copies, waits for them, and re-layouts: 2.99 us -> 1.76 us
    pallas_call x11, Pallas kernels: 31.1 us -> 24.6 us  [call(): pl.pallas_call(staged(kernel, kinds_in, kinds_out, 0 if hot and first is...]
    all_to_all x3, starting transfers between devices: 19.4 us -> 17.6 us  [exchange(): return lax.all_to_all(array, axis, 0, 0)]
    all_to_all x3, waiting for transfers between devices: 4.97 us -> 6.6 us  [exchange(): return lax.all_to_all(array, axis, 0, 0)]
    unnamed x14 -> x50, local copies, waits for them, and re-layouts: 2.99 us -> 1.76 us
where the time goes in v4:
time: 75.5 us; the launch traced here: 74.8 us
  starting transfers between devices  24.8 us (33%)
  Pallas kernels  24.6 us (33%)
  blocking collectives  16.1 us (21%)
  waiting for transfers between devices  6.61 us (9%)
  local copies, waits for them, and re-layouts  1.76 us (2%)
  between operations  1.06 us (1%)
    pallas_call x11, Pallas kernels, call(): pl.pallas_call(staged(kernel, kinds_in, kinds_out, 0 if hot and first is...  24.6 us
    all_to_all x3, starting transfers between devices, exchange(): return lax.all_to_all(array, axis, 0, 0)  17.6 us
    all_to_all x1, blocking collectives, exchange(): return lax.all_to_all(array, axis, 0, 0)  16.1 us
    ppermute x2, starting transfers between devices, shifted(): lax.ppermute(array, axis, [(i, i + by) for i in range(count) if 0 <= i +...  7.15 us
    all_to_all x3, waiting for transfers between devices, exchange(): return lax.all_to_all(array, axis, 0, 0)  6.6 us
    unnamed x50, local copies, waits for them, and re-layouts  1.76 us
  transfers between devices with their start and end apart: 5, of which 3 were waited for; matrix products, arithmetic and copies ran while one was open for 0% of the time, Pallas kernels for 22%

profile of v4, /device:TPU:1, one launch (start us, length us, event | category | flops | bytes accessed | tf_op | source)
XLA Modules:
  0.0 74.8 jit_solution(12082276560383649011)
XLA Ops:
  0.6 0.0 copy-start.1
  0.6 0.0 copy-start
  0.7 3.1 %coef.1 = (f32[16,8,256]{2,1,0:T(8,128)}, f32[16,8,256]{2,1,0:T(8,128)}, f32[6,16,8,256]{3,2,1,0:T(8,128)}, f32[16,8,256]{2,1,0:T(8,128)}, f32[16,8,256]{2,1,0:T...) custom-call(s32[16,8,256]{2,1,0:T(8,128)} %refs_0_.4, ...), custom_call_target="tpu_custom_call" | custom-call | flops 13893888 | bytes 3473472 | tf_op jit(solution)/shard_map/coef/pallas_call | solution.py:484
  3.8 0.0 copy-start.24
  3.8 0.0 copy-start.2
  3.9 0.0 copy-start.5
  3.9 0.0 copy-start.21
  3.9 7.3 %all-to-all-start = ((f32[16,4,16,256]{3,2,1,0:T(8,128)}), f32[16,4,16,256]{3,2,1,0:T(8,128)S(1)}, u32[]{:S(2)}, u32[]{:S(2)}) async-start(f32[16,4,16,256]{3,2,1,0:T(8,128)} %get-tuple-element.46), calls=%async_computation | async-start | bytes 2097152 | tf_op jit(solution)/shard_map/all_to_all | solution.py:509
  11.2 1.3 %collective-permute-start = (f32[1,8,256]{2,1,0:T(8,128)S(1)}, f32[1,8,256]{2,1,0:T(8,128)S(1)}, u32[]{:S(2)}, u32[]{:S(2)}) collective-permute-start(f32[1,8,256]{2,1,0:T(8,128)S(1)} %copy-done.24), channel_id=1, source_target_pairs={{16,0},{32,16},{48,32},{64,48},{80,64},{96,80},{112,96},{17,1},{33... | collective-permute-start | bytes 24584 | tf_op jit(solution)/shard_map/ppermute | solution.py:505
  12.5 5.9 %collective-permute-start.1 = (f32[1,8,256]{2,1,0:T(8,128)S(1)}, f32[1,8,256]{2,1,0:T(8,128)S(1)}, u32[]{:S(2)}, u32[]{:S(2)}) collective-permute-start(f32[1,8,256]{2,1,0:T(8,128)S(1)} %copy-done.23), channel_id=1, source_target_pairs={{0,16},{16,32},{32,48},{48,64},{64,80},{80,96},{96,112},{1,17},{17... | collective-permute-start | bytes 24584 | tf_op jit(solution)/shard_map/ppermute | solution.py:505
  18.4 4.5 %factor.1 = (f32[16,16,8,256]{3,2,1,0:T(8,128)}, f32[16,8,256]{2,1,0:T(8,128)}, f32[16,8,256]{2,1,0:T(8,128)}, f32[16,8,256]{2,1,0:T(8,128)}, f32[16,8,256]{2,1,0:T(8,128)}, /*index=5*/f32[3,8,256]{2,1,0:T(8,128)}) custom-call(f32[16,8,256]{2,1,0:T(8,128)} %get-tuple-element.53.refs_0_.refs_2_), custom_call_target="tpu_custom_call" | custom-call | flops 11108352 | bytes 2777088 | tf_op jit(solution)/shard_map/factor/pallas_call | solution.py:484
  22.9 0.0 collective-permute-done.refs_5_
  22.9 0.0 collective-permute-done.1.refs_6_
  23.0 1.0 %chain_x.1 = (f32[16,8,256]{2,1,0:T(8,128)S(1)}, f32[16,8,256]{2,1,0:T(8,128)S(1)}, f32[2,16,256]{2,1,0:T(8,128)S(1)}) custom-call(f32[3,16,8,256]{3,2,1,0:T(8,128)S(1)} %copy-done, f32[3,16,8,256]{3,2,1,0:T(8,128)S(1)} %copy-done.1, f32[16,8,256]{2,1,0:T(8,128)S(1)} %copy-done.2, f32[6,16,8,256]{3,2,1,0:T(8,128)S(1)} %copy-done.4, ...), custom_call_target="tpu_custom_call" | custom-call | flops 8552448 | bytes 2138112 | tf_op jit(solution)/shard_map/chain_x/pallas_call | solution.py:484
  24.0 2.9 %all-to-all-done.refs_0_ = f32[16,4,16,256]{3,2,1,0:T(8,128)S(1)} async-done(((f32[16,4,16,256]{3,2,1,0:T(8,128)}), f32[16,4,16,256]{3,2,1,0:T(8,128)S(1)}, u32[]{:S(2)}, u32[]{:S(2)}) %all-to-all-start) | async-done | bytes 1048608 | tf_op jit(solution)/shard_map/all_to_all | solution.py:509
  26.9 1.2 %scan_y.1 = (f32[16,16,256]{2,1,0:T(8,128)S(1)}, f32[9,16,256]{2,1,0:T(8,128)S(1)}, f32[16,16,256]{2,1,0:T(8,128)}, f32[2,16,256]{2,1,0:T(8,128)S(1)}) custom-call(f32[16,4,16,256]{3,2,1,0:T(8,128)S(1)} %all-to-all-done.refs_0_, f32[3,16,256]{2,1,0:T(8,128)S(1)} %copy-done.21, f32[2,16,256]{2,1,0:T(8,128)S(1)} %get-tuple-element.56.refs_2_.refs_3_), custom_call_target="tpu_custom_call" | custom-call | flops 7340032 | bytes 1835008 | tf_op jit(solution)/shard_map/scan_y/pallas_call | solution.py:484
  28.1 4.8 %all-to-all-start.1 = ((f32[16,16,256]{2,1,0:T(8,128)}), f32[16,16,256]{2,1,0:T(8,128)S(1)}, u32[]{:S(2)}, u32[]{:S(2)}) async-start(f32[16,16,256]{2,1,0:T(8,128)} %get-tuple-element.57), calls=%async_computation.1 | async-start | bytes 524288 | tf_op jit(solution)/shard_map/all_to_all | solution.py:509
  32.9 0.0 copy-start.3
  33.0 2.2 %chain_z.1 = (f32[16,8,256]{2,1,0:T(8,128)}, f32[16,8,256]{2,1,0:T(8,128)}, f32[2,8,256]{2,1,0:T(8,128)}) custom-call(f32[3,16,8,256]{3,2,1,0:T(8,128)} %refs_0_.7, f32[3,16,8,256]{3,2,1,0:T(8,128)} %refs_1_.7, f32[16,8,256]{2,1,0:T(8,128)} %get-tuple-element.48.refs_2_.refs_7_.refs_8_, f32[16,8,256]{2,1,0:T(8,128)} %get-tuple-element.69.refs_3_.refs_10_, ...), custom_call_target="tpu_custom_call" | custom-call | flops 5439488 | bytes 1359872 | tf_op jit(solution)/shard_map/chain_z/pallas_call | solution.py:484
  35.2 3.6 %center_y.1 = (f32[16,8,256]{2,1,0:T(8,128)}, f32[16,8,256]{2,1,0:T(8,128)}) custom-call(f32[3,16,8,256]{3,2,1,0:T(8,128)} %refs_0_.7, f32[3,16,8,256]{3,2,1,0:T(8,128)} %refs_1_.7, f32[16,8,256]{2,1,0:T(8,128)} %get-tuple-element.48.refs_2_.refs_7_.refs_8_, f32[16,16,8,256]{3,2,1,0:T(8,128)} %get-tuple-element.62.refs_3_, ...), custom_call_target="tpu_custom_call" | custom-call | flops 13795328 | bytes 3448832 | tf_op jit(solution)/shard_map/center_y/pallas_call | solution.py:484
  38.8 1.5 %all-to-all-done.1.refs_0_ = f32[16,16,256]{2,1,0:T(8,128)S(1)} async-done(((f32[16,16,256]{2,1,0:T(8,128)}), f32[16,16,256]{2,1,0:T(8,128)S(1)}, u32[]{:S(2)}, u32[]{:S(2)}) %all-to-all-start.1) | async-done | bytes 262176 | tf_op jit(solution)/shard_map/all_to_all | solution.py:509
  40.4 0.9 %copy-done.16 = f32[16,8,256]{2,1,0:T(8,128)S(1)} copy-done((f32[16,8,256]{2,1,0:T(8,128)S(1)}, f32[16,8,256]{2,1,0:T(8,128)}, u32[]{:S(2)}) %copy-start.16) | copy-done | bytes 131096
  41.3 0.8 %copy-done.18 = f32[2,16,256]{2,1,0:T(8,128)S(1)} copy-done((f32[2,16,256]{2,1,0:T(8,128)S(1)}, f32[2,16,256]{2,1,0:T(8,128)}, u32[]{:S(2)}) %copy-start.18) | copy-done | bytes 32792
  42.0 1.2 %half_x.1 = (f32[16,8,256]{2,1,0:T(8,128)S(1)}, f32[16,8,256]{2,1,0:T(8,128)S(1)}, f32[16,8,256]{2,1,0:T(8,128)S(1)}, f32[8,7,8,256]{3,2,1,0:T(8,128)S(1)}) custom-call(f32[16,16,256]{2,1,0:T(8,128)S(1)} %all-to-all-done.1.refs_0_, f32[16,16,256]{2,1,0:T(8,128)S(1)} %get-tuple-element.58.refs_1_, f32[9,16,256]{2,1,0:T(8,128)S(1)} %get-tuple-element.59.refs_2_.refs_13_, ...), custom_call_target="tpu_custom_call" | custom-call | flops 10059776 | bytes 2514944 | tf_op jit(solution)/shard_map/half_x/pallas_call | solution.py:484
  43.2 16.1 %all_to_all.20.refs_0_ = f32[8,7,8,256]{3,2,1,0:T(8,128)S(1)} all-to-all(f32[8,7,8,256]{3,2,1,0:T(8,128)S(1)} %get-tuple-element.72), channel_id=1, replica_groups=mesh['gx'=8,'gy'=16] {'gx'}, dimensions={0} | all-to-all | bytes 917504 | tf_op jit(solution)/shard_map/all_to_all | solution.py:509
  59.3 0.0 copy-done.9
  59.3 1.6 %half_z.1 = (f32[16,8,256]{2,1,0:T(8,128)S(1)}, f32[16,8,256]{2,1,0:T(8,128)S(1)}, f32[2,16,256]{2,1,0:T(8,128)S(1)}, f32[2,8,256]{2,1,0:T(8,128)S(1)}, f32[16,16,256]{2,1,0:T(8,128)}) custom-call(f32[8,7,8,256]{3,2,1,0:T(8,128)S(1)} %all_to_all.20.refs_0_, f32[3,8,256]{2,1,0:T(8,128)S(1)} %copy-done.19, f32[2,8,256]{2,1,0:T(8,128)S(1)} %copy-done.20, ...), custom_call_target="tpu_custom_call" | custom-call | flops 12746752 | bytes 3186688 | tf_op jit(solution)/shard_map/half_z/pallas_call | solution.py:484
  60.9 5.5 %all-to-all-start.3 = ((f32[16,16,256]{2,1,0:T(8,128)}), f32[16,16,256]{2,1,0:T(8,128)S(1)}, u32[]{:S(2)}, u32[]{:S(2)}) async-start(f32[16,16,256]{2,1,0:T(8,128)} %get-tuple-element.80), calls=%async_computation.3 | async-start | bytes 524288 | tf_op jit(solution)/shard_map/all_to_all | solution.py:509
  66.4 5.1 %final_x.1 = (f32[16,8,256]{2,1,0:T(8,128)S(1)}, f32[16,8,256]{2,1,0:T(8,128)S(1)}) custom-call(f32[16,8,256]{2,1,0:T(8,128)S(1)} %get-tuple-element.83.refs_0_, f32[16,8,256]{2,1,0:T(8,128)S(1)} %get-tuple-element.84.refs_1_, f32[16,8,256]{2,1,0:T(8,128)S(1)} %copy-done.7), custom_call_target="tpu_custom_call" | custom-call | flops 2621440 | bytes 655360 | tf_op jit(solution)/shard_map/final_x/pallas_call | solution.py:484
  71.5 0.1 final_y.1
  71.6 2.2 %all-to-all-done.3.refs_0_ = f32[16,16,256]{2,1,0:T(8,128)S(1)} async-done(((f32[16,16,256]{2,1,0:T(8,128)}), f32[16,16,256]{2,1,0:T(8,128)S(1)}, u32[]{:S(2)}, u32[]{:S(2)}) %all-to-all-start.3) | async-done | bytes 262176 | tf_op jit(solution)/shard_map/all_to_all | solution.py:509
  73.8 1.0 %final_z.1 = (f32[3,16,8,256]{3,2,1,0:T(8,128)}, f32[3,16,8,256]{3,2,1,0:T(8,128)}) custom-call(f32[16,16,256]{2,1,0:T(8,128)S(1)} %all-to-all-done.3.refs_0_, f32[16,16,256]{2,1,0:T(8,128)S(1)} %get-tuple-element.58.refs_1_, f32[9,16,256]{2,1,0:T(8,128)S(1)} %get-tuple-element.59.refs_2_.refs_13_, f32[2,16,256]{2,1,0:T(8,128)S(1)} %get-tuple-element.81.refs_3_, ...), custom_call_target="tpu_custom_call" | custom-call | flops 10158080 | bytes 2539520 | tf_op jit(solution)/shard_map/final_z/pallas_call | solution.py:484
  (40 shorter events, 0.1 us)
Async XLA Ops:
  0.6 22.3 %copy-start.1 = (f32[3,16,8,256]{3,2,1,0:T(8,128)S(1)}, f32[3,16,8,256]{3,2,1,0:T(8,128)}, u32[]{:S(2)}) copy-start(f32[3,16,8,256]{3,2,1,0:T(8,128)} %refs_1_.7) | copy-start | bytes 1179652
  0.6 22.3 %copy-start = (f32[3,16,8,256]{3,2,1,0:T(8,128)S(1)}, f32[3,16,8,256]{3,2,1,0:T(8,128)}, u32[]{:S(2)}) copy-start(f32[3,16,8,256]{3,2,1,0:T(8,128)} %refs_0_.7) | copy-start | bytes 1179652
  3.8 7.4 %copy-start.24 = (f32[1,8,256]{2,1,0:T(8,128)S(1)}, f32[1,8,256]{2,1,0:T(8,128)}, u32[]{:S(2)}) copy-start(f32[1,8,256]{2,1,0:T(8,128)} %get-tuple-element.51) | copy-start | bytes 24580
  3.8 8.7 %copy-start.23 = (f32[1,8,256]{2,1,0:T(8,128)S(1)}, f32[1,8,256]{2,1,0:T(8,128)}, u32[]{:S(2)}) copy-start(f32[1,8,256]{2,1,0:T(8,128)} %get-tuple-element.52) | copy-start | bytes 24580
  3.8 19.1 %copy-start.2 = (f32[16,8,256]{2,1,0:T(8,128)S(1)}, f32[16,8,256]{2,1,0:T(8,128)}, u32[]{:S(2)}) copy-start(f32[16,8,256]{2,1,0:T(8,128)} %get-tuple-element.48.refs_2_.refs_7_.refs_8_) | copy-start | bytes 393220
  3.8 19.1 %copy-start.4 = (f32[6,16,8,256]{3,2,1,0:T(8,128)S(1)}, f32[6,16,8,256]{3,2,1,0:T(8,128)}, u32[]{:S(2)}) copy-start(f32[6,16,8,256]{3,2,1,0:T(8,128)} %get-tuple-element.49.refs_3_.refs_11_) | copy-start | bytes 2359300
  3.9 19.1 %copy-start.5 = (f32[16,8,256]{2,1,0:T(8,128)S(1)}, f32[16,8,256]{2,1,0:T(8,128)}, u32[]{:S(2)}) copy-start(f32[16,8,256]{2,1,0:T(8,128)} %get-tuple-element.50.refs_4_.refs_12_) | copy-start | bytes 393220
  3.9 23.0 %copy-start.21 = (f32[3,16,256]{2,1,0:T(8,128)S(1)}, f32[3,16,256]{2,1,0:T(8,128)}, u32[]{:S(2)}) copy-start(f32[3,16,256]{2,1,0:T(8,128)} %get-tuple-element.47.refs_1_) | copy-start | bytes 147460
  3.9 23.0 %all-to-all-start = ((f32[16,4,16,256]{3,2,1,0:T(8,128)}), f32[16,4,16,256]{3,2,1,0:T(8,128)S(1)}, u32[]{:S(2)}, u32[]{:S(2)}) async-start(f32[16,4,16,256]{3,2,1,0:T(8,128)} %get-tuple-element.46), calls=%async_computation | async-start | bytes 2097152 | tf_op jit(solution)/shard_map/all_to_all | solution.py:509
  11.2 11.7 %collective-permute-start = (f32[1,8,256]{2,1,0:T(8,128)S(1)}, f32[1,8,256]{2,1,0:T(8,128)S(1)}, u32[]{:S(2)}, u32[]{:S(2)}) collective-permute-start(f32[1,8,256]{2,1,0:T(8,128)S(1)} %copy-done.24), channel_id=1, source_target_pairs={{16,0},{32,16},{48,32},{64,48},{80,64},{96,80},{112,96},{17,1},{33... | collective-permute-start | bytes 24584 | tf_op jit(solution)/shard_map/ppermute | solution.py:505
  12.5 10.4 %collective-permute-start.1 = (f32[1,8,256]{2,1,0:T(8,128)S(1)}, f32[1,8,256]{2,1,0:T(8,128)S(1)}, u32[]{:S(2)}, u32[]{:S(2)}) collective-permute-start(f32[1,8,256]{2,1,0:T(8,128)S(1)} %copy-done.23), channel_id=1, source_target_pairs={{0,16},{16,32},{32,48},{48,64},{64,80},{80,96},{96,112},{1,17},{17... | collective-permute-start | bytes 24584 | tf_op jit(solution)/shard_map/ppermute | solution.py:505
  22.9 12.2 %copy-start.22 = (f32[1,8,256]{2,1,0:T(8,128)}, f32[1,8,256]{2,1,0:T(8,128)S(1)}, u32[]{:S(2)}) copy-start(f32[1,8,256]{2,1,0:T(8,128)S(1)} %collective-permute-done.1.refs_6_) | copy-start | bytes 24580
  24.0 14.7 %copy-start.17 = (f32[2,16,256]{2,1,0:T(8,128)}, f32[2,16,256]{2,1,0:T(8,128)S(1)}, u32[]{:S(2)}) copy-start(f32[2,16,256]{2,1,0:T(8,128)S(1)} %get-tuple-element.56.refs_2_.refs_3_) | copy-start | bytes 98308
  28.1 4.8 %copy-start.13 = (f32[2,16,256]{2,1,0:T(8,128)}, f32[2,16,256]{2,1,0:T(8,128)S(1)}, u32[]{:S(2)}) copy-start(f32[2,16,256]{2,1,0:T(8,128)S(1)} %get-tuple-element.64.refs_5_.refs_4_) | copy-start | bytes 98308
  28.1 12.2 %all-to-all-start.1 = ((f32[16,16,256]{2,1,0:T(8,128)}), f32[16,16,256]{2,1,0:T(8,128)S(1)}, u32[]{:S(2)}, u32[]{:S(2)}) async-start(f32[16,16,256]{2,1,0:T(8,128)} %get-tuple-element.57), calls=%async_computation.1 | async-start | bytes 524288 | tf_op jit(solution)/shard_map/all_to_all | solution.py:509
  32.9 7.4 %copy-start.3 = (f32[16,8,256]{2,1,0:T(8,128)S(1)}, f32[16,8,256]{2,1,0:T(8,128)}, u32[]{:S(2)}) copy-start(f32[16,8,256]{2,1,0:T(8,128)} %get-tuple-element.48.refs_2_.refs_7_.refs_8_) | copy-start | bytes 393220
  32.9 7.4 %copy-start.6 = (f32[16,8,256]{2,1,0:T(8,128)S(1)}, f32[16,8,256]{2,1,0:T(8,128)}, u32[]{:S(2)}) copy-start(f32[16,8,256]{2,1,0:T(8,128)} %get-tuple-element.69.refs_3_.refs_10_) | copy-start | bytes 393220
  32.9 7.4 %copy-start.10 = (f32[16,8,256]{2,1,0:T(8,128)S(1)}, f32[16,8,256]{2,1,0:T(8,128)}, u32[]{:S(2)}) copy-start(f32[16,8,256]{2,1,0:T(8,128)} %get-tuple-element.67.refs_8_.refs_6_) | copy-start | bytes 393220
  33.0 7.4 %copy-start.11 = (f32[16,8,256]{2,1,0:T(8,128)S(1)}, f32[16,8,256]{2,1,0:T(8,128)}, u32[]{:S(2)}) copy-start(f32[16,8,256]{2,1,0:T(8,128)} %get-tuple-element.68.refs_9_.refs_7_) | copy-start | bytes 393220
  33.0 7.4 %copy-start.19 = (f32[3,8,256]{2,1,0:T(8,128)S(1)}, f32[3,8,256]{2,1,0:T(8,128)}, u32[]{:S(2)}) copy-start(f32[3,8,256]{2,1,0:T(8,128)} %get-tuple-element.70.refs_11_.refs_1_) | copy-start | bytes 73732
  35.2 5.2 %copy-start.20 = (f32[2,8,256]{2,1,0:T(8,128)S(1)}, f32[2,8,256]{2,1,0:T(8,128)}, u32[]{:S(2)}) copy-start(f32[2,8,256]{2,1,0:T(8,128)} %get-tuple-element.71.refs_12_.refs_2_) | copy-start | bytes 49156
  38.7 20.5 %copy-start.8 = (f32[16,8,256]{2,1,0:T(8,128)S(1)}, f32[16,8,256]{2,1,0:T(8,128)}, u32[]{:S(2)}) copy-start(f32[16,8,256]{2,1,0:T(8,128)} %get-tuple-element.78.refs_9_.refs_3_) | copy-start | bytes 393220
  38.8 20.5 %copy-start.9 = (f32[16,8,256]{2,1,0:T(8,128)S(1)}, f32[16,8,256]{2,1,0:T(8,128)}, u32[]{:S(2)}) copy-start(f32[16,8,256]{2,1,0:T(8,128)} %get-tuple-element.79.refs_10_.refs_4_) | copy-start | bytes 393220
  38.8 20.5 %copy-start.12 = (f32[16,8,256]{2,1,0:T(8,128)S(1)}, f32[16,8,256]{2,1,0:T(8,128)}, u32[]{:S(2)}) copy-start(f32[16,8,256]{2,1,0:T(8,128)} %get-tuple-element.75.refs_5_) | copy-start | bytes 393220
  38.8 20.5 %copy-start.14 = (f32[16,8,256]{2,1,0:T(8,128)S(1)}, f32[16,8,256]{2,1,0:T(8,128)}, u32[]{:S(2)}) copy-start(f32[16,8,256]{2,1,0:T(8,128)} %get-tuple-element.74.refs_4_) | copy-start | bytes 393220
  38.8 20.5 %copy-start.15 = (f32[16,8,256]{2,1,0:T(8,128)S(1)}, f32[16,8,256]{2,1,0:T(8,128)}, u32[]{:S(2)}) copy-start(f32[16,8,256]{2,1,0:T(8,128)} %get-tuple-element.73.refs_3_) | copy-start | bytes 393220
  40.4 0.9 %copy-start.16 = (f32[16,8,256]{2,1,0:T(8,128)S(1)}, f32[16,8,256]{2,1,0:T(8,128)}, u32[]{:S(2)}) copy-start(f32[16,8,256]{2,1,0:T(8,128)} %get-tuple-element.66.refs_6_) | copy-start | bytes 393220
  41.3 0.8 %copy-start.18 = (f32[2,16,256]{2,1,0:T(8,128)S(1)}, f32[2,16,256]{2,1,0:T(8,128)}, u32[]{:S(2)}) copy-start(f32[2,16,256]{2,1,0:T(8,128)} %copy-done.17) | copy-start | bytes 98308
  43.2 23.2 %copy-start.7 = (f32[16,8,256]{2,1,0:T(8,128)S(1)}, f32[16,8,256]{2,1,0:T(8,128)}, u32[]{:S(2)}) copy-start(f32[16,8,256]{2,1,0:T(8,128)} %get-tuple-element.53.refs_0_.refs_2_) | copy-start | bytes 393220
  60.9 12.9 %all-to-all-start.3 = ((f32[16,16,256]{2,1,0:T(8,128)}), f32[16,16,256]{2,1,0:T(8,128)S(1)}, u32[]{:S(2)}, u32[]{:S(2)}) async-start(f32[16,16,256]{2,1,0:T(8,128)} %get-tuple-element.80), calls=%async_computation.3 | async-start | bytes 524288 | tf_op jit(solution)/shard_map/all_to_all | solution.py:509

commit v5 on v4

--- a/solution.py
+++ b/solution.py
@@ -315,11 +315,14 @@
     fill_send(send, pair[0], pair[1], consts, n, ky)
 
 
-def half_x_kernel(nxd, ready, recv, weights, consts, pair_x, up, iz, t1, ds, phy, psy, ex, coef_x, pair_z, sz_out, t4_out, ufy_out, send, edge):
+def half_x_kernel(nxd, ready, recv, weights, consts, up, iz, t1, ds, phy, psy, ex, coef_x, pair_z, sz_out, t4_out, ufy_out, send, edge):
     ky = lax.axis_index("gy")
     nx, ny, nz = ds.shape
     A, C = gather_sums(recv, weights, recv.shape[0], ky)
-    lower, upper = boundary(A, C, pair_x[0], pair_x[1], consts)
+    for x in range(nx):
+        edge[0, x:x + 1] = up[x][0:1]
+        edge[1, x:x + 1] = up[x][ny - 1:ny] - iz[x][ny - 1:ny] * (1.0 / H)
+    lower, upper = boundary(A, C, edge[0], edge[1], consts)
     edge[0] = lower
     edge[1] = upper
     ready()
@@ -546,7 +549,7 @@
 
     sz, t4, ufy, send2 = call(
         bind(half_x_kernel, nxd), [cell, cell, cell, (nxd, 7) + px],
-        recv1, wy, ky, pair_x, ux, iz, t1, ds, phy, psy, ex, cx, pair_z,
+        recv1, wy, ky, ux, iz, t1, ds, phy, psy, ex, cx, pair_z,
         first=4, scratch=[pltpu.VMEM((2,) + py, F32)], hot=True, room=40, name="half_x")
     recv2 = exchange(send2, "gx")
     sy, ufz, pair4, edge_y, send3 = call(

time: 75.5 us -> 74.6 us (0.988)
  local copies, waits for them, and re-layouts: 1.76 us -> 1 us
    unnamed x50 -> x46, local copies, waits for them, and re-layouts: 1.76 us -> 1 us
where the time goes in v5:
time: 74.6 us; the launch traced here: 74 us
  starting transfers between devices  24.7 us (33%)
  Pallas kernels  24.5 us (33%)
  blocking collectives  16.1 us (22%)
  waiting for transfers between devices  6.65 us (9%)
  between operations  1.04 us (1%)
  local copies, waits for them, and re-layouts  1 us (1%)
    pallas_call x11, Pallas kernels, call(): pl.pallas_call(staged(kernel, kinds_in, kinds_out, 0 if hot and first is...  24.5 us
    all_to_all x3, starting transfers between devices, exchange(): return lax.all_to_all(array, axis, 0, 0)  17.5 us
    all_to_all x1, blocking collectives, exchange(): return lax.all_to_all(array, axis, 0, 0)  16.1 us
    ppermute x2, starting transfers between devices, shifted(): lax.ppermute(array, axis, [(i, i + by) for i in range(count) if 0 <= i +...  7.15 us
    all_to_all x3, waiting for transfers between devices, exchange(): return lax.all_to_all(array, axis, 0, 0)  6.64 us
  transfers between devices with their start and end apart: 5, of which 3 were waited for; matrix products, arithmetic and copies ran while one was open for 0% of the time, Pallas kernels for 22%

profile of v5, /device:TPU:1, one launch (start us, length us, event | category | flops | bytes accessed | tf_op | source)
XLA Modules:
  0.0 74.0 jit_solution(2354371715587424096)
XLA Ops:
  0.6 0.0 copy-start.1
  0.6 0.0 copy-start
  0.7 3.1 %coef.1 = (f32[16,8,256]{2,1,0:T(8,128)}, f32[16,8,256]{2,1,0:T(8,128)}, f32[6,16,8,256]{3,2,1,0:T(8,128)}, f32[16,8,256]{2,1,0:T(8,128)}, f32[16,8,256]{2,1,0:T...) custom-call(s32[16,8,256]{2,1,0:T(8,128)} %refs_0_.4, ...), custom_call_target="tpu_custom_call" | custom-call | flops 13893888 | bytes 3473472 | tf_op jit(solution)/shard_map/coef/pallas_call | solution.py:487
  3.8 0.0 copy-start.22
  3.8 0.0 copy-start.21
  3.8 0.0 copy-start.2
  3.8 0.0 copy-start.5
  3.9 7.3 %all-to-all-start = ((f32[16,4,16,256]{3,2,1,0:T(8,128)}), f32[16,4,16,256]{3,2,1,0:T(8,128)S(1)}, u32[]{:S(2)}, u32[]{:S(2)}) async-start(f32[16,4,16,256]{3,2,1,0:T(8,128)} %get-tuple-element.46), calls=%async_computation | async-start | bytes 2097152 | tf_op jit(solution)/shard_map/all_to_all | solution.py:512
  11.2 0.0 copy-done.22
  11.2 1.3 %collective-permute-start = (f32[1,8,256]{2,1,0:T(8,128)S(1)}, f32[1,8,256]{2,1,0:T(8,128)S(1)}, u32[]{:S(2)}, u32[]{:S(2)}) collective-permute-start(f32[1,8,256]{2,1,0:T(8,128)S(1)} %copy-done.22), channel_id=1, source_target_pairs={{16,0},{32,16},{48,32},{64,48},{80,64},{96,80},{112,96},{17,1},{33... | collective-permute-start | bytes 24584 | tf_op jit(solution)/shard_map/ppermute | solution.py:508
  12.5 0.0 copy-done.21
  12.5 5.9 %collective-permute-start.1 = (f32[1,8,256]{2,1,0:T(8,128)S(1)}, f32[1,8,256]{2,1,0:T(8,128)S(1)}, u32[]{:S(2)}, u32[]{:S(2)}) collective-permute-start(f32[1,8,256]{2,1,0:T(8,128)S(1)} %copy-done.21), channel_id=1, source_target_pairs={{0,16},{16,32},{32,48},{48,64},{64,80},{80,96},{96,112},{1,17},{17... | collective-permute-start | bytes 24584 | tf_op jit(solution)/shard_map/ppermute | solution.py:508
  18.3 4.5 %factor.1 = (f32[16,16,8,256]{3,2,1,0:T(8,128)}, f32[16,8,256]{2,1,0:T(8,128)}, f32[16,8,256]{2,1,0:T(8,128)}, f32[16,8,256]{2,1,0:T(8,128)}, f32[16,8,256]{2,1,0:T(8,128)}, /*index=5*/f32[3,8,256]{2,1,0:T(8,128)}) custom-call(f32[16,8,256]{2,1,0:T(8,128)} %get-tuple-element.53.refs_0_.refs_2_), custom_call_target="tpu_custom_call" | custom-call | flops 11108352 | bytes 2777088 | tf_op jit(solution)/shard_map/factor/pallas_call | solution.py:487
  22.9 0.0 collective-permute-done.refs_5_
  22.9 0.0 collective-permute-done.1.refs_6_
  22.9 1.0 %chain_x.1 = (f32[16,8,256]{2,1,0:T(8,128)S(1)}, f32[16,8,256]{2,1,0:T(8,128)S(1)}, f32[2,16,256]{2,1,0:T(8,128)S(1)}) custom-call(f32[3,16,8,256]{3,2,1,0:T(8,128)S(1)} %copy-done, f32[3,16,8,256]{3,2,1,0:T(8,128)S(1)} %copy-done.1, f32[16,8,256]{2,1,0:T(8,128)S(1)} %copy-done.2, f32[6,16,8,256]{3,2,1,0:T(8,128)S(1)} %copy-done.4, ...), custom_call_target="tpu_custom_call" | custom-call | flops 8552448 | bytes 2138112 | tf_op jit(solution)/shard_map/chain_x/pallas_call | solution.py:487
  24.0 2.9 %all-to-all-done.refs_0_ = f32[16,4,16,256]{3,2,1,0:T(8,128)S(1)} async-done(((f32[16,4,16,256]{3,2,1,0:T(8,128)}), f32[16,4,16,256]{3,2,1,0:T(8,128)S(1)}, u32[]{:S(2)}, u32[]{:S(2)}) %all-to-all-start) | async-done | bytes 1048608 | tf_op jit(solution)/shard_map/all_to_all | solution.py:512
  26.9 1.2 %scan_y.1 = (f32[16,16,256]{2,1,0:T(8,128)S(1)}, f32[9,16,256]{2,1,0:T(8,128)S(1)}, f32[16,16,256]{2,1,0:T(8,128)}, f32[2,16,256]{2,1,0:T(8,128)S(1)}) custom-call(f32[16,4,16,256]{3,2,1,0:T(8,128)S(1)} %all-to-all-done.refs_0_, f32[3,16,256]{2,1,0:T(8,128)S(1)} %copy-done.19, f32[2,16,256]{2,1,0:T(8,128)S(1)} %get-tuple-element.56.refs_2_), custom_call_target="tpu_custom_call" | custom-call | flops 7340032 | bytes 1835008 | tf_op jit(solution)/shard_map/scan_y/pallas_call | solution.py:487
  28.1 4.8 %all-to-all-start.1 = ((f32[16,16,256]{2,1,0:T(8,128)}), f32[16,16,256]{2,1,0:T(8,128)S(1)}, u32[]{:S(2)}, u32[]{:S(2)}) async-start(f32[16,16,256]{2,1,0:T(8,128)} %get-tuple-element.57), calls=%async_computation.1 | async-start | bytes 524288 | tf_op jit(solution)/shard_map/all_to_all | solution.py:512
  32.9 0.0 copy-start.3
  32.9 2.2 %chain_z.1 = (f32[16,8,256]{2,1,0:T(8,128)}, f32[16,8,256]{2,1,0:T(8,128)}, f32[2,8,256]{2,1,0:T(8,128)}) custom-call(f32[3,16,8,256]{3,2,1,0:T(8,128)} %refs_0_.7, f32[3,16,8,256]{3,2,1,0:T(8,128)} %refs_1_.7, f32[16,8,256]{2,1,0:T(8,128)} %get-tuple-element.48.refs_2_.refs_6_.refs_8_, f32[16,8,256]{2,1,0:T(8,128)} %get-tuple-element.69.refs_3_.refs_9_, ...), custom_call_target="tpu_custom_call" | custom-call | flops 5439488 | bytes 1359872 | tf_op jit(solution)/shard_map/chain_z/pallas_call | solution.py:487
  35.2 3.6 %center_y.1 = (f32[16,8,256]{2,1,0:T(8,128)}, f32[16,8,256]{2,1,0:T(8,128)}) custom-call(f32[3,16,8,256]{3,2,1,0:T(8,128)} %refs_0_.7, f32[3,16,8,256]{3,2,1,0:T(8,128)} %refs_1_.7, f32[16,8,256]{2,1,0:T(8,128)} %get-tuple-element.48.refs_2_.refs_6_.refs_8_, f32[16,16,8,256]{3,2,1,0:T(8,128)} %get-tuple-element.62.refs_3_, ...), custom_call_target="tpu_custom_call" | custom-call | flops 13795328 | bytes 3448832 | tf_op jit(solution)/shard_map/center_y/pallas_call | solution.py:487
  38.8 1.5 %all-to-all-done.1.refs_0_ = f32[16,16,256]{2,1,0:T(8,128)S(1)} async-done(((f32[16,16,256]{2,1,0:T(8,128)}), f32[16,16,256]{2,1,0:T(8,128)S(1)}, u32[]{:S(2)}, u32[]{:S(2)}) %all-to-all-start.1) | async-done | bytes 262176 | tf_op jit(solution)/shard_map/all_to_all | solution.py:512
  40.3 0.9 %copy-done.16 = f32[16,8,256]{2,1,0:T(8,128)S(1)} copy-done((f32[16,8,256]{2,1,0:T(8,128)S(1)}, f32[16,8,256]{2,1,0:T(8,128)}, u32[]{:S(2)}) %copy-start.16) | copy-done | bytes 131096
  41.2 1.2 %half_x.1 = (f32[16,8,256]{2,1,0:T(8,128)S(1)}, f32[16,8,256]{2,1,0:T(8,128)S(1)}, f32[16,8,256]{2,1,0:T(8,128)S(1)}, f32[8,7,8,256]{3,2,1,0:T(8,128)S(1)}) custom-call(f32[16,16,256]{2,1,0:T(8,128)S(1)} %all-to-all-done.1.refs_0_, f32[16,16,256]{2,1,0:T(8,128)S(1)} %get-tuple-element.58.refs_1_, f32[9,16,256]{2,1,0:T(8,128)S(1)} %get-tuple-element.59.refs_2_.refs_13_, ...), custom_call_target="tpu_custom_call" | custom-call | flops 9928704 | bytes 2482176 | tf_op jit(solution)/shard_map/half_x/pallas_call | solution.py:487
  42.4 16.1 %all_to_all.20.refs_0_ = f32[8,7,8,256]{3,2,1,0:T(8,128)S(1)} all-to-all(f32[8,7,8,256]{3,2,1,0:T(8,128)S(1)} %get-tuple-element.72), channel_id=1, replica_groups=mesh['gx'=8,'gy'=16] {'gx'}, dimensions={0} | all-to-all | bytes 917504 | tf_op jit(solution)/shard_map/all_to_all | solution.py:512
  58.5 1.6 %half_z.1 = (f32[16,8,256]{2,1,0:T(8,128)S(1)}, f32[16,8,256]{2,1,0:T(8,128)S(1)}, f32[2,16,256]{2,1,0:T(8,128)S(1)}, f32[2,8,256]{2,1,0:T(8,128)S(1)}, f32[16,16,256]{2,1,0:T(8,128)}) custom-call(f32[8,7,8,256]{3,2,1,0:T(8,128)S(1)} %all_to_all.20.refs_0_, f32[3,8,256]{2,1,0:T(8,128)S(1)} %copy-done.17, f32[2,8,256]{2,1,0:T(8,128)S(1)} %copy-done.18, ...), custom_call_target="tpu_custom_call" | custom-call | flops 12746752 | bytes 3186688 | tf_op jit(solution)/shard_map/half_z/pallas_call | solution.py:487
  60.1 5.4 %all-to-all-start.3 = ((f32[16,16,256]{2,1,0:T(8,128)}), f32[16,16,256]{2,1,0:T(8,128)S(1)}, u32[]{:S(2)}, u32[]{:S(2)}) async-start(f32[16,16,256]{2,1,0:T(8,128)} %get-tuple-element.80), calls=%async_computation.3 | async-start | bytes 524288 | tf_op jit(solution)/shard_map/all_to_all | solution.py:512
  65.5 5.1 %final_x.1 = (f32[16,8,256]{2,1,0:T(8,128)S(1)}, f32[16,8,256]{2,1,0:T(8,128)S(1)}) custom-call(f32[16,8,256]{2,1,0:T(8,128)S(1)} %get-tuple-element.83.refs_0_, f32[16,8,256]{2,1,0:T(8,128)S(1)} %get-tuple-element.84.refs_1_, f32[16,8,256]{2,1,0:T(8,128)S(1)} %copy-done.7), custom_call_target="tpu_custom_call" | custom-call | flops 2621440 | bytes 655360 | tf_op jit(solution)/shard_map/final_x/pallas_call | solution.py:487
  70.7 0.1 final_y.1
  70.7 2.2 %all-to-all-done.3.refs_0_ = f32[16,16,256]{2,1,0:T(8,128)S(1)} async-done(((f32[16,16,256]{2,1,0:T(8,128)}), f32[16,16,256]{2,1,0:T(8,128)S(1)}, u32[]{:S(2)}, u32[]{:S(2)}) %all-to-all-start.3) | async-done | bytes 262176 | tf_op jit(solution)/shard_map/all_to_all | solution.py:512
  73.0 1.0 %final_z.1 = (f32[3,16,8,256]{3,2,1,0:T(8,128)}, f32[3,16,8,256]{3,2,1,0:T(8,128)}) custom-call(f32[16,16,256]{2,1,0:T(8,128)S(1)} %all-to-all-done.3.refs_0_, f32[16,16,256]{2,1,0:T(8,128)S(1)} %get-tuple-element.58.refs_1_, f32[9,16,256]{2,1,0:T(8,128)S(1)} %get-tuple-element.59.refs_2_.refs_13_, f32[2,16,256]{2,1,0:T(8,128)S(1)} %get-tuple-element.81.refs_3_, ...), custom_call_target="tpu_custom_call" | custom-call | flops 10158080 | bytes 2539520 | tf_op jit(solution)/shard_map/final_z/pallas_call | solution.py:487
  (36 shorter events, 0.1 us)
Async XLA Ops:
  0.6 22.3 %copy-start.1 = (f32[3,16,8,256]{3,2,1,0:T(8,128)S(1)}, f32[3,16,8,256]{3,2,1,0:T(8,128)}, u32[]{:S(2)}) copy-start(f32[3,16,8,256]{3,2,1,0:T(8,128)} %refs_1_.7) | copy-start | bytes 1179652
  0.6 22.3 %copy-start = (f32[3,16,8,256]{3,2,1,0:T(8,128)S(1)}, f32[3,16,8,256]{3,2,1,0:T(8,128)}, u32[]{:S(2)}) copy-start(f32[3,16,8,256]{3,2,1,0:T(8,128)} %refs_0_.7) | copy-start | bytes 1179652
  3.8 7.4 %copy-start.22 = (f32[1,8,256]{2,1,0:T(8,128)S(1)}, f32[1,8,256]{2,1,0:T(8,128)}, u32[]{:S(2)}) copy-start(f32[1,8,256]{2,1,0:T(8,128)} %get-tuple-element.51) | copy-start | bytes 24580
  3.8 8.7 %copy-start.21 = (f32[1,8,256]{2,1,0:T(8,128)S(1)}, f32[1,8,256]{2,1,0:T(8,128)}, u32[]{:S(2)}) copy-start(f32[1,8,256]{2,1,0:T(8,128)} %get-tuple-element.52) | copy-start | bytes 24580
  3.8 19.1 %copy-start.2 = (f32[16,8,256]{2,1,0:T(8,128)S(1)}, f32[16,8,256]{2,1,0:T(8,128)}, u32[]{:S(2)}) copy-start(f32[16,8,256]{2,1,0:T(8,128)} %get-tuple-element.48.refs_2_.refs_6_.refs_8_) | copy-start | bytes 393220
  3.8 19.1 %copy-start.4 = (f32[6,16,8,256]{3,2,1,0:T(8,128)S(1)}, f32[6,16,8,256]{3,2,1,0:T(8,128)}, u32[]{:S(2)}) copy-start(f32[6,16,8,256]{3,2,1,0:T(8,128)} %get-tuple-element.49.refs_3_.refs_11_) | copy-start | bytes 2359300
  3.8 19.1 %copy-start.5 = (f32[16,8,256]{2,1,0:T(8,128)S(1)}, f32[16,8,256]{2,1,0:T(8,128)}, u32[]{:S(2)}) copy-start(f32[16,8,256]{2,1,0:T(8,128)} %get-tuple-element.50.refs_4_.refs_12_) | copy-start | bytes 393220
  3.8 23.0 %copy-start.19 = (f32[3,16,256]{2,1,0:T(8,128)S(1)}, f32[3,16,256]{2,1,0:T(8,128)}, u32[]{:S(2)}) copy-start(f32[3,16,256]{2,1,0:T(8,128)} %get-tuple-element.47.refs_1_) | copy-start | bytes 147460
  3.9 23.0 %all-to-all-start = ((f32[16,4,16,256]{3,2,1,0:T(8,128)}), f32[16,4,16,256]{3,2,1,0:T(8,128)S(1)}, u32[]{:S(2)}, u32[]{:S(2)}) async-start(f32[16,4,16,256]{3,2,1,0:T(8,128)} %get-tuple-element.46), calls=%async_computation | async-start | bytes 2097152 | tf_op jit(solution)/shard_map/all_to_all | solution.py:512
  11.2 11.7 %collective-permute-start = (f32[1,8,256]{2,1,0:T(8,128)S(1)}, f32[1,8,256]{2,1,0:T(8,128)S(1)}, u32[]{:S(2)}, u32[]{:S(2)}) collective-permute-start(f32[1,8,256]{2,1,0:T(8,128)S(1)} %copy-done.22), channel_id=1, source_target_pairs={{16,0},{32,16},{48,32},{64,48},{80,64},{96,80},{112,96},{17,1},{33... | collective-permute-start | bytes 24584 | tf_op jit(solution)/shard_map/ppermute | solution.py:508
  12.5 10.4 %collective-permute-start.1 = (f32[1,8,256]{2,1,0:T(8,128)S(1)}, f32[1,8,256]{2,1,0:T(8,128)S(1)}, u32[]{:S(2)}, u32[]{:S(2)}) collective-permute-start(f32[1,8,256]{2,1,0:T(8,128)S(1)} %copy-done.21), channel_id=1, source_target_pairs={{0,16},{16,32},{32,48},{48,64},{64,80},{80,96},{96,112},{1,17},{17... | collective-permute-start | bytes 24584 | tf_op jit(solution)/shard_map/ppermute | solution.py:508
  22.9 12.2 %copy-start.20 = (f32[1,8,256]{2,1,0:T(8,128)}, f32[1,8,256]{2,1,0:T(8,128)S(1)}, u32[]{:S(2)}) copy-start(f32[1,8,256]{2,1,0:T(8,128)S(1)} %collective-permute-done.1.refs_6_) | copy-start | bytes 24580
  28.1 4.8 %copy-start.13 = (f32[2,16,256]{2,1,0:T(8,128)}, f32[2,16,256]{2,1,0:T(8,128)S(1)}, u32[]{:S(2)}) copy-start(f32[2,16,256]{2,1,0:T(8,128)S(1)} %get-tuple-element.64.refs_5_.refs_4_) | copy-start | bytes 98308
  28.1 12.2 %all-to-all-start.1 = ((f32[16,16,256]{2,1,0:T(8,128)}), f32[16,16,256]{2,1,0:T(8,128)S(1)}, u32[]{:S(2)}, u32[]{:S(2)}) async-start(f32[16,16,256]{2,1,0:T(8,128)} %get-tuple-element.57), calls=%async_computation.1 | async-start | bytes 524288 | tf_op jit(solution)/shard_map/all_to_all | solution.py:512
  32.9 7.4 %copy-start.3 = (f32[16,8,256]{2,1,0:T(8,128)S(1)}, f32[16,8,256]{2,1,0:T(8,128)}, u32[]{:S(2)}) copy-start(f32[16,8,256]{2,1,0:T(8,128)} %get-tuple-element.48.refs_2_.refs_6_.refs_8_) | copy-start | bytes 393220
  32.9 7.4 %copy-start.6 = (f32[16,8,256]{2,1,0:T(8,128)S(1)}, f32[16,8,256]{2,1,0:T(8,128)}, u32[]{:S(2)}) copy-start(f32[16,8,256]{2,1,0:T(8,128)} %get-tuple-element.69.refs_3_.refs_9_) | copy-start | bytes 393220
  32.9 7.4 %copy-start.10 = (f32[16,8,256]{2,1,0:T(8,128)S(1)}, f32[16,8,256]{2,1,0:T(8,128)}, u32[]{:S(2)}) copy-start(f32[16,8,256]{2,1,0:T(8,128)} %get-tuple-element.67.refs_7_.refs_6_) | copy-start | bytes 393220
  32.9 7.4 %copy-start.11 = (f32[16,8,256]{2,1,0:T(8,128)S(1)}, f32[16,8,256]{2,1,0:T(8,128)}, u32[]{:S(2)}) copy-start(f32[16,8,256]{2,1,0:T(8,128)} %get-tuple-element.68.refs_8_.refs_7_) | copy-start | bytes 393220
  32.9 7.4 %copy-start.17 = (f32[3,8,256]{2,1,0:T(8,128)S(1)}, f32[3,8,256]{2,1,0:T(8,128)}, u32[]{:S(2)}) copy-start(f32[3,8,256]{2,1,0:T(8,128)} %get-tuple-element.70.refs_10_.refs_1_) | copy-start | bytes 73732
  35.1 5.2 %copy-start.18 = (f32[2,8,256]{2,1,0:T(8,128)S(1)}, f32[2,8,256]{2,1,0:T(8,128)}, u32[]{:S(2)}) copy-start(f32[2,8,256]{2,1,0:T(8,128)} %get-tuple-element.71.refs_11_.refs_2_) | copy-start | bytes 49156
  35.1 23.4 %copy-start.8 = (f32[16,8,256]{2,1,0:T(8,128)S(1)}, f32[16,8,256]{2,1,0:T(8,128)}, u32[]{:S(2)}) copy-start(f32[16,8,256]{2,1,0:T(8,128)} %get-tuple-element.78.refs_9_.refs_3_) | copy-start | bytes 393220
  35.1 23.3 %copy-start.9 = (f32[16,8,256]{2,1,0:T(8,128)S(1)}, f32[16,8,256]{2,1,0:T(8,128)}, u32[]{:S(2)}) copy-start(f32[16,8,256]{2,1,0:T(8,128)} %get-tuple-element.79.refs_10_.refs_4_) | copy-start | bytes 393220
  35.2 23.3 %copy-start.14 = (f32[16,8,256]{2,1,0:T(8,128)S(1)}, f32[16,8,256]{2,1,0:T(8,128)}, u32[]{:S(2)}) copy-start(f32[16,8,256]{2,1,0:T(8,128)} %get-tuple-element.74.refs_4_) | copy-start | bytes 393220
  35.2 23.3 %copy-start.15 = (f32[16,8,256]{2,1,0:T(8,128)S(1)}, f32[16,8,256]{2,1,0:T(8,128)}, u32[]{:S(2)}) copy-start(f32[16,8,256]{2,1,0:T(8,128)} %get-tuple-element.73.refs_3_) | copy-start | bytes 393220
  38.8 19.7 %copy-start.12 = (f32[16,8,256]{2,1,0:T(8,128)S(1)}, f32[16,8,256]{2,1,0:T(8,128)}, u32[]{:S(2)}) copy-start(f32[16,8,256]{2,1,0:T(8,128)} %get-tuple-element.75.refs_5_) | copy-start | bytes 393220
  40.3 0.9 %copy-start.16 = (f32[16,8,256]{2,1,0:T(8,128)S(1)}, f32[16,8,256]{2,1,0:T(8,128)}, u32[]{:S(2)}) copy-start(f32[16,8,256]{2,1,0:T(8,128)} %get-tuple-element.66.refs_5_) | copy-start | bytes 393220
  42.4 23.1 %copy-start.7 = (f32[16,8,256]{2,1,0:T(8,128)S(1)}, f32[16,8,256]{2,1,0:T(8,128)}, u32[]{:S(2)}) copy-start(f32[16,8,256]{2,1,0:T(8,128)} %get-tuple-element.53.refs_0_.refs_2_) | copy-start | bytes 393220
  60.1 12.9 %all-to-all-start.3 = ((f32[16,16,256]{2,1,0:T(8,128)}), f32[16,16,256]{2,1,0:T(8,128)S(1)}, u32[]{:S(2)}, u32[]{:S(2)}) async-start(f32[16,16,256]{2,1,0:T(8,128)} %get-tuple-element.80), calls=%async_computation.3 | async-start | bytes 524288 | tf_op jit(solution)/shard_map/all_to_all | solution.py:512

commit v6 on v5

--- a/solution.py
+++ b/solution.py
@@ -153,7 +153,17 @@
         send[j] = jnp.where(j > k, right, left)
 
 
-def coef_kernel(nyd, ready, mat, perm, cond, el, mg, ds, si, yk, yib, phy, psy, cy, send, pe1, ph2, pe2, ph0):
+def y_factors(si, ky):
+    row = iota(0, si.shape)
+    zero = jnp.zeros(si.shape, F32)
+    a = jnp.where(row == 0, 0.0, zero - 1.0)
+    b = si + jnp.where(row == 0, jnp.where(ky == 0, 1.0, 2.0), 2.0)
+    kept = []
+    inv = reduce_factors(a, b, 0, lambda level, ka, kc: kept.append((ka, kc)))
+    return kept, inv
+
+
+def coef_kernel(nyd, ready, mat, perm, cond, el, mg, ds, si, phy, psy, cy, send, pe1, ph2, pe2, ph0):
     ky = lax.axis_index("gy")
     nx, ny, nz = mat.shape
     row = iota(0, (ny, nz))
@@ -174,15 +184,9 @@
         a = jnp.where(first, 0.0, jnp.full(m.shape, -1.0, F32))
         b = inv_s + jnp.where(first, jnp.where(ky == 0, 1.0, 2.0), 2.0)
 
-        def store(level, ka, kc):
-            yk[2 * level, x] = ka
-            yk[2 * level + 1, x] = kc
-
-        def load(level):
-            return yk[2 * level, x], yk[2 * level + 1, x]
-
-        ib = reduce_factors(a, b, 0, store)
-        yib[x] = ib
+        kept = []
+        ib = reduce_factors(a, b, 0, lambda level, ka, kc: kept.append((ka, kc)))
+        load = kept.__getitem__
         lo = reduce_apply(jnp.where(first, jnp.where(ky == 0, 0.0, 1.0), jnp.zeros(m.shape, F32)), 0, load, ib)
         up = reduce_apply(jnp.where(last, jnp.where(ky == nyd - 1, 0.0, 1.0), jnp.zeros(m.shape, F32)), 0, load, ib)
         phy[x] = lo
@@ -260,7 +264,8 @@
     return lambda level: (zk[2 * level, x], zk[2 * level + 1, x])
 
 
-def chain_x_kernel(el, mg, ds, yk, yib, e1_up, iz_out, up_out, pair):
+def chain_x_kernel(el, mg, ds, si, e1_up, iz_out, up_out, pair):
+    ky = lax.axis_index("gy")
     nx, ny, nz = ds.shape
     for x in range(nx):
         above = el[1, x + 1] if x < nx - 1 else e1_up[0]
@@ -268,7 +273,8 @@
         iz_out[x] = iz
         h1 = mg[1, x]
         rhs = ds[x] * el[0, x] + ((iz - prev_y(iz, 0.0)) - (h1 - prev_z(h1))) * (1.0 / H)
-        u = reduce_apply(rhs, 0, z_load(yk, x), yib[x])
+        kept, inv = y_factors(si[x], ky)
+        u = reduce_apply(rhs, 0, kept.__getitem__, inv)
         up_out[x] = u
         pair[0, x:x + 1] = u[0:1]
         pair[1, x:x + 1] = u[ny - 1:ny] - iz[ny - 1:ny] * (1.0 / H)
@@ -352,7 +358,7 @@
         send[j, 6] = l
 
 
-def half_z_kernel(ready, recv, cx, pair_z, up, iy, sx, ufy, sz, ds, phx, psx, yk, yib, consts_y, sy_out, ufz_out, pair_out, edge_y_out, send, weights, mixed, consts):
+def half_z_kernel(ready, recv, cx, pair_z, up, iy, sx, ufy, sz, ds, phx, psx, si, consts_y, sy_out, ufz_out, pair_out, edge_y_out, send, weights, mixed, consts):
     kx = lax.axis_index("gx")
     ky = lax.axis_index("gy")
     nx, ny, nz = ds.shape
@@ -374,7 +380,8 @@
         sy_out[x] = my + curl
         s = sx[x]
         rhs = ds[x] * cz + ((my - below) - (s - prev_y(s, 0.0))) * (1.0 / H)
-        u = reduce_apply(rhs, 0, z_load(yk, x), yib[x])
+        kept, inv = y_factors(si[x], ky)
+        u = reduce_apply(rhs, 0, kept.__getitem__, inv)
         ufz_out[x] = u
         pair_out[0, x:x + 1] = u[0:1]
         pair_out[1, x:x + 1] = u[ny - 1:ny] + s[ny - 1:ny] * (1.0 / H)
@@ -526,9 +533,9 @@
         return body
 
 
-    ds, si, yk, yib, phy, psy, cy, send_c, pe1, ph2 = call(
+    ds, si, phy, psy, cy, send_c, pe1, ph2 = call(
         bind(coef_kernel, nyd),
-        [cell, cell, (2 * len(strides(ny)),) + cell, cell, cell, cell, (3,) + py, (nyd, 4) + py,
+        [cell, cell, cell, cell, (3,) + py, (nyd, 4) + py,
          (1,) + px, (1,) + px],
         material, permittivity, conductivity, electric, magnetic, smem=(1, 2), first=3, room=60,
         scratch=[pltpu.VMEM(py, F32), pltpu.VMEM(py, F32)], name="coef")
@@ -539,7 +546,7 @@
         bind(factor_kernel, nxd), [(2 * len(strides(nz)),) + cell, cell, cell, cell, cell, (3,) + px], si, name="factor")
     e1_up, h2_low, cx = lax.optimization_barrier((e1_up, h2_low, cx))
     iz, ux, pair_x = call(chain_x_kernel, [cell, cell, (2,) + py],
-                          electric, magnetic, ds, yk, yib, e1_up, hot=True, far=(0, 1), room=40, name="chain_x")
+                          electric, magnetic, ds, si, e1_up, hot=True, far=(0, 1), room=40, name="chain_x")
     wy, ky, send1, halo_y = call(scan_y_kernel, [(nyd,) + py, (9,) + py, (nyd,) + py, (2,) + py], recv_c, cy, pair_x,
                          first=2, scratch=[pltpu.VMEM((nyd,) + py, F32)], hot=True, room=40, name="scan_y")
     recv1 = exchange(send1, "gy")
@@ -554,7 +561,7 @@
     recv2 = exchange(send2, "gx")
     sy, ufz, pair4, edge_y, send3 = call(
         half_z_kernel, [cell, cell, (2,) + py, (2,) + px, (nyd,) + py],
-        recv2, cx, pair_z, uz, iy, sx, ufy, sz, ds, phx, psx, yk, yib, ky,
+        recv2, cx, pair_z, uz, iy, sx, ufy, sz, ds, phx, psx, si, ky,
         first=2, scratch=[pltpu.VMEM((nxd,) + px, F32), pltpu.VMEM((nxd,) + px, F32), pltpu.VMEM((9,) + px, F32)],
         hot=True, room=40, name="half_z")
     recv3 = exchange(send3, "gy")

time: 74.6 us -> 74.2 us (level)
  transfers between devices with their start and end apart: 5 -> 5, of which waited for: 3 -> 3; matrix products, arithmetic and copies ran while one was open for 0% -> 0% of each run, Pallas kernels for 22% -> 23%
where the time goes in v6:
time: 74.2 us; the launch traced here: 73.7 us
  starting transfers between devices  24.8 us (33%)
  Pallas kernels  24.6 us (33%)
  blocking collectives  15.8 us (21%)
  waiting for transfers between devices  6.46 us (9%)
  between operations  1.01 us (1%)
  local copies, waits for them, and re-layouts  0.99 us (1%)
    pallas_call x11, Pallas kernels, call(): pl.pallas_call(staged(kernel, kinds_in, kinds_out, 0 if hot and first is...  24.6 us
    all_to_all x3, starting transfers between devices, exchange(): return lax.all_to_all(array, axis, 0, 0)  17.7 us
    all_to_all x1, blocking collectives, exchange(): return lax.all_to_all(array, axis, 0, 0)  15.8 us
    ppermute x2, starting transfers between devices, shifted(): lax.ppermute(array, axis, [(i, i + by) for i in range(count) if 0 <= i +...  7.15 us
    all_to_all x3, waiting for transfers between devices, exchange(): return lax.all_to_all(array, axis, 0, 0)  6.45 us
  transfers between devices with their start and end apart: 5, of which 3 were waited for; matrix products, arithmetic and copies ran while one was open for 0% of the time, Pallas kernels for 23%

profile of v6, /device:TPU:1, one launch (start us, length us, event | category | flops | bytes accessed | tf_op | source)
XLA Modules:
  0.0 73.7 jit_solution(5585199476694334034)
XLA Ops:
  0.6 0.0 copy-start.1
  0.6 0.0 copy-start
  0.7 2.8 %coef.1 = (f32[16,8,256]{2,1,0:T(8,128)}, f32[16,8,256]{2,1,0:T(8,128)}, f32[16,8,256]{2,1,0:T(8,128)}, f32[16,8,256]{2,1,0:T(8,128)}, f32[3,16,256]{2,1,0:T(8,1...) custom-call(s32[16,8,256]{2,1,0:T(8,128)} %refs_0_.4, f32[8]{0:T(128)} %refs_1_.4, ...), custom_call_target="tpu_custom_call" | custom-call | flops 10223872 | bytes 2555968 | tf_op jit(solution)/shard_map/coef/pallas_call | solution.py:494
  3.5 0.0 copy-start.2
  3.5 0.0 copy-start.4
  3.5 0.0 copy-start.17
  3.5 7.3 %all-to-all-start = ((f32[16,4,16,256]{3,2,1,0:T(8,128)}), f32[16,4,16,256]{3,2,1,0:T(8,128)S(1)}, u32[]{:S(2)}, u32[]{:S(2)}) async-start(f32[16,4,16,256]{3,2,1,0:T(8,128)} %get-tuple-element.44), calls=%async_computation | async-start | bytes 2097152 | tf_op jit(solution)/shard_map/all_to_all | solution.py:519
  10.8 1.3 %collective-permute-start = (f32[1,8,256]{2,1,0:T(8,128)S(1)}, f32[1,8,256]{2,1,0:T(8,128)S(1)}, u32[]{:S(2)}, u32[]{:S(2)}) collective-permute-start(f32[1,8,256]{2,1,0:T(8,128)S(1)} %copy-done.20), channel_id=1, source_target_pairs={{16,0},{32,16},{48,32},{64,48},{80,64},{96,80},{112,96},{17,1},{33... | collective-permute-start | bytes 24584 | tf_op jit(solution)/shard_map/ppermute | solution.py:515
  12.2 5.9 %collective-permute-start.1 = (f32[1,8,256]{2,1,0:T(8,128)S(1)}, f32[1,8,256]{2,1,0:T(8,128)S(1)}, u32[]{:S(2)}, u32[]{:S(2)}) collective-permute-start(f32[1,8,256]{2,1,0:T(8,128)S(1)} %copy-done.19), channel_id=1, source_target_pairs={{0,16},{16,32},{32,48},{48,64},{64,80},{80,96},{96,112},{1,17},{17... | collective-permute-start | bytes 24584 | tf_op jit(solution)/shard_map/ppermute | solution.py:515
  18.0 4.6 %factor.1 = (f32[16,16,8,256]{3,2,1,0:T(8,128)}, f32[16,8,256]{2,1,0:T(8,128)}, f32[16,8,256]{2,1,0:T(8,128)}, f32[16,8,256]{2,1,0:T(8,128)}, f32[16,8,256]{2,1,0:T(8,128)}, /*index=5*/f32[3,8,256]{2,1,0:T(8,128)}) custom-call(f32[16,8,256]{2,1,0:T(8,128)} %get-tuple-element.47.refs_0_.refs_3_.refs_11_.refs_2_), custom_call_target="tpu_custom_call" | custom-call | flops 11108352 | bytes 2777088 | tf_op jit(solution)/shard_map/factor/pallas_call | solution.py:494
  22.6 0.0 collective-permute-done.refs_4_
  22.6 0.0 collective-permute-done.1.refs_6_
  22.7 1.1 %chain_x.1 = (f32[16,8,256]{2,1,0:T(8,128)S(1)}, f32[16,8,256]{2,1,0:T(8,128)S(1)}, f32[2,16,256]{2,1,0:T(8,128)S(1)}) custom-call(f32[3,16,8,256]{3,2,1,0:T(8,128)S(1)} %copy-done, f32[3,16,8,256]{3,2,1,0:T(8,128)S(1)} %copy-done.1, f32[16,8,256]{2,1,0:T(8,128)S(1)} %copy-done.2, f32[16,8,256]{2,1,0:T(8,128)S(1)} %copy-done.4, ...), custom_call_target="tpu_custom_call" | custom-call | flops 5406720 | bytes 1351680 | tf_op jit(solution)/shard_map/chain_x/pallas_call | solution.py:494
  23.8 2.7 %all-to-all-done.refs_0_ = f32[16,4,16,256]{3,2,1,0:T(8,128)S(1)} async-done(((f32[16,4,16,256]{3,2,1,0:T(8,128)}), f32[16,4,16,256]{3,2,1,0:T(8,128)S(1)}, u32[]{:S(2)}, u32[]{:S(2)}) %all-to-all-start) | async-done | bytes 1048608 | tf_op jit(solution)/shard_map/all_to_all | solution.py:519
  26.5 1.2 %scan_y.1 = (f32[16,16,256]{2,1,0:T(8,128)S(1)}, f32[9,16,256]{2,1,0:T(8,128)S(1)}, f32[16,16,256]{2,1,0:T(8,128)}, f32[2,16,256]{2,1,0:T(8,128)S(1)}) custom-call(f32[16,4,16,256]{3,2,1,0:T(8,128)S(1)} %all-to-all-done.refs_0_, f32[3,16,256]{2,1,0:T(8,128)S(1)} %copy-done.17, f32[2,16,256]{2,1,0:T(8,128)S(1)} %get-tuple-element.52.refs_2_), custom_call_target="tpu_custom_call" | custom-call | flops 7340032 | bytes 1835008 | tf_op jit(solution)/shard_map/scan_y/pallas_call | solution.py:494
  27.8 4.9 %all-to-all-start.1 = ((f32[16,16,256]{2,1,0:T(8,128)}), f32[16,16,256]{2,1,0:T(8,128)S(1)}, u32[]{:S(2)}, u32[]{:S(2)}) async-start(f32[16,16,256]{2,1,0:T(8,128)} %get-tuple-element.53), calls=%async_computation.1 | async-start | bytes 524288 | tf_op jit(solution)/shard_map/all_to_all | solution.py:519
  32.7 0.0 copy-start.3
  32.7 0.0 copy-start.5
  32.7 0.0 copy-start.8
  32.7 0.0 copy-start.9
  32.7 2.2 %chain_z.1 = (f32[16,8,256]{2,1,0:T(8,128)}, f32[16,8,256]{2,1,0:T(8,128)}, f32[2,8,256]{2,1,0:T(8,128)}) custom-call(f32[3,16,8,256]{3,2,1,0:T(8,128)} %refs_0_.7, f32[3,16,8,256]{3,2,1,0:T(8,128)} %refs_1_.7, f32[16,8,256]{2,1,0:T(8,128)} %get-tuple-element.46.refs_2_.refs_6_.refs_8_, f32[16,8,256]{2,1,0:T(8,128)} %get-tuple-element.65.refs_3_.refs_9_, ...), custom_call_target="tpu_custom_call" | custom-call | flops 5439488 | bytes 1359872 | tf_op jit(solution)/shard_map/chain_z/pallas_call | solution.py:494
  35.0 3.6 %center_y.1 = (f32[16,8,256]{2,1,0:T(8,128)}, f32[16,8,256]{2,1,0:T(8,128)}) custom-call(f32[3,16,8,256]{3,2,1,0:T(8,128)} %refs_0_.7, f32[3,16,8,256]{3,2,1,0:T(8,128)} %refs_1_.7, f32[16,8,256]{2,1,0:T(8,128)} %get-tuple-element.46.refs_2_.refs_6_.refs_8_, f32[16,16,8,256]{3,2,1,0:T(8,128)} %get-tuple-element.58.refs_3_, ...), custom_call_target="tpu_custom_call" | custom-call | flops 13795328 | bytes 3448832 | tf_op jit(solution)/shard_map/center_y/pallas_call | solution.py:494
  38.6 1.5 %all-to-all-done.1.refs_0_ = f32[16,16,256]{2,1,0:T(8,128)S(1)} async-done(((f32[16,16,256]{2,1,0:T(8,128)}), f32[16,16,256]{2,1,0:T(8,128)S(1)}, u32[]{:S(2)}, u32[]{:S(2)}) %all-to-all-start.1) | async-done | bytes 262176 | tf_op jit(solution)/shard_map/all_to_all | solution.py:519
  40.1 0.9 %copy-done.14 = f32[16,8,256]{2,1,0:T(8,128)S(1)} copy-done((f32[16,8,256]{2,1,0:T(8,128)S(1)}, f32[16,8,256]{2,1,0:T(8,128)}, u32[]{:S(2)}) %copy-start.14) | copy-done | bytes 131096
  41.0 1.2 %half_x.1 = (f32[16,8,256]{2,1,0:T(8,128)S(1)}, f32[16,8,256]{2,1,0:T(8,128)S(1)}, f32[16,8,256]{2,1,0:T(8,128)S(1)}, f32[8,7,8,256]{3,2,1,0:T(8,128)S(1)}) custom-call(f32[16,16,256]{2,1,0:T(8,128)S(1)} %all-to-all-done.1.refs_0_, f32[16,16,256]{2,1,0:T(8,128)S(1)} %get-tuple-element.54.refs_1_, f32[9,16,256]{2,1,0:T(8,128)S(1)} %get-tuple-element.55.refs_2_.refs_12_, ...), custom_call_target="tpu_custom_call" | custom-call | flops 9928704 | bytes 2482176 | tf_op jit(solution)/shard_map/half_x/pallas_call | solution.py:494
  42.2 15.8 %all_to_all.20.refs_0_ = f32[8,7,8,256]{3,2,1,0:T(8,128)S(1)} all-to-all(f32[8,7,8,256]{3,2,1,0:T(8,128)S(1)} %get-tuple-element.68), channel_id=1, replica_groups=mesh['gx'=8,'gy'=16] {'gx'}, dimensions={0} | all-to-all | bytes 917504 | tf_op jit(solution)/shard_map/all_to_all | solution.py:519
  58.0 1.7 %half_z.1 = (f32[16,8,256]{2,1,0:T(8,128)S(1)}, f32[16,8,256]{2,1,0:T(8,128)S(1)}, f32[2,16,256]{2,1,0:T(8,128)S(1)}, f32[2,8,256]{2,1,0:T(8,128)S(1)}, f32[16,16,256]{2,1,0:T(8,128)}) custom-call(f32[8,7,8,256]{3,2,1,0:T(8,128)S(1)} %all_to_all.20.refs_0_, f32[3,8,256]{2,1,0:T(8,128)S(1)} %copy-done.15, f32[2,8,256]{2,1,0:T(8,128)S(1)} %copy-done.16, ...), custom_call_target="tpu_custom_call" | custom-call | flops 9601024 | bytes 2400256 | tf_op jit(solution)/shard_map/half_z/pallas_call | solution.py:494
  59.7 5.4 %all-to-all-start.3 = ((f32[16,16,256]{2,1,0:T(8,128)}), f32[16,16,256]{2,1,0:T(8,128)S(1)}, u32[]{:S(2)}, u32[]{:S(2)}) async-start(f32[16,16,256]{2,1,0:T(8,128)} %get-tuple-element.76), calls=%async_computation.3 | async-start | bytes 524288 | tf_op jit(solution)/shard_map/all_to_all | solution.py:519
  65.2 5.1 %final_x.1 = (f32[16,8,256]{2,1,0:T(8,128)S(1)}, f32[16,8,256]{2,1,0:T(8,128)S(1)}) custom-call(f32[16,8,256]{2,1,0:T(8,128)S(1)} %get-tuple-element.79.refs_0_, f32[16,8,256]{2,1,0:T(8,128)S(1)} %get-tuple-element.80.refs_1_, f32[16,8,256]{2,1,0:T(8,128)S(1)} %copy-done.4), custom_call_target="tpu_custom_call" | custom-call | flops 2621440 | bytes 655360 | tf_op jit(solution)/shard_map/final_x/pallas_call | solution.py:494
  70.3 0.1 final_y.1
  70.4 2.3 %all-to-all-done.3.refs_0_ = f32[16,16,256]{2,1,0:T(8,128)S(1)} async-done(((f32[16,16,256]{2,1,0:T(8,128)}), f32[16,16,256]{2,1,0:T(8,128)S(1)}, u32[]{:S(2)}, u32[]{:S(2)}) %all-to-all-start.3) | async-done | bytes 262176 | tf_op jit(solution)/shard_map/all_to_all | solution.py:519
  72.6 1.0 %final_z.1 = (f32[3,16,8,256]{3,2,1,0:T(8,128)}, f32[3,16,8,256]{3,2,1,0:T(8,128)}) custom-call(f32[16,16,256]{2,1,0:T(8,128)S(1)} %all-to-all-done.3.refs_0_, f32[16,16,256]{2,1,0:T(8,128)S(1)} %get-tuple-element.54.refs_1_, f32[9,16,256]{2,1,0:T(8,128)S(1)} %get-tuple-element.55.refs_2_.refs_12_, f32[2,16,256]{2,1,0:T(8,128)S(1)} %get-tuple-element.77.refs_3_, ...), custom_call_target="tpu_custom_call" | custom-call | flops 10158080 | bytes 2539520 | tf_op jit(solution)/shard_map/final_z/pallas_call | solution.py:494
  (32 shorter events, 0.1 us)
Async XLA Ops:
  0.6 22.0 %copy-start.1 = (f32[3,16,8,256]{3,2,1,0:T(8,128)S(1)}, f32[3,16,8,256]{3,2,1,0:T(8,128)}, u32[]{:S(2)}) copy-start(f32[3,16,8,256]{3,2,1,0:T(8,128)} %refs_1_.7) | copy-start | bytes 1179652
  0.6 22.0 %copy-start = (f32[3,16,8,256]{3,2,1,0:T(8,128)S(1)}, f32[3,16,8,256]{3,2,1,0:T(8,128)}, u32[]{:S(2)}) copy-start(f32[3,16,8,256]{3,2,1,0:T(8,128)} %refs_0_.7) | copy-start | bytes 1179652
  3.5 7.4 %copy-start.20 = (f32[1,8,256]{2,1,0:T(8,128)S(1)}, f32[1,8,256]{2,1,0:T(8,128)}, u32[]{:S(2)}) copy-start(f32[1,8,256]{2,1,0:T(8,128)} %get-tuple-element.48) | copy-start | bytes 24580
  3.5 8.7 %copy-start.19 = (f32[1,8,256]{2,1,0:T(8,128)S(1)}, f32[1,8,256]{2,1,0:T(8,128)}, u32[]{:S(2)}) copy-start(f32[1,8,256]{2,1,0:T(8,128)} %get-tuple-element.49) | copy-start | bytes 24580
  3.5 19.2 %copy-start.2 = (f32[16,8,256]{2,1,0:T(8,128)S(1)}, f32[16,8,256]{2,1,0:T(8,128)}, u32[]{:S(2)}) copy-start(f32[16,8,256]{2,1,0:T(8,128)} %get-tuple-element.46.refs_2_.refs_6_.refs_8_) | copy-start | bytes 393220
  3.5 19.2 %copy-start.4 = (f32[16,8,256]{2,1,0:T(8,128)S(1)}, f32[16,8,256]{2,1,0:T(8,128)}, u32[]{:S(2)}) copy-start(f32[16,8,256]{2,1,0:T(8,128)} %get-tuple-element.47.refs_0_.refs_3_.refs_11_.refs_2_) | copy-start | bytes 393220
  3.5 23.0 %copy-start.17 = (f32[3,16,256]{2,1,0:T(8,128)S(1)}, f32[3,16,256]{2,1,0:T(8,128)}, u32[]{:S(2)}) copy-start(f32[3,16,256]{2,1,0:T(8,128)} %get-tuple-element.45.refs_1_) | copy-start | bytes 147460
  3.5 23.0 %all-to-all-start = ((f32[16,4,16,256]{3,2,1,0:T(8,128)}), f32[16,4,16,256]{3,2,1,0:T(8,128)S(1)}, u32[]{:S(2)}, u32[]{:S(2)}) async-start(f32[16,4,16,256]{3,2,1,0:T(8,128)} %get-tuple-element.44), calls=%async_computation | async-start | bytes 2097152 | tf_op jit(solution)/shard_map/all_to_all | solution.py:519
  10.8 11.8 %collective-permute-start = (f32[1,8,256]{2,1,0:T(8,128)S(1)}, f32[1,8,256]{2,1,0:T(8,128)S(1)}, u32[]{:S(2)}, u32[]{:S(2)}) collective-permute-start(f32[1,8,256]{2,1,0:T(8,128)S(1)} %copy-done.20), channel_id=1, source_target_pairs={{16,0},{32,16},{48,32},{64,48},{80,64},{96,80},{112,96},{17,1},{33... | collective-permute-start | bytes 24584 | tf_op jit(solution)/shard_map/ppermute | solution.py:515
  12.2 10.5 %collective-permute-start.1 = (f32[1,8,256]{2,1,0:T(8,128)S(1)}, f32[1,8,256]{2,1,0:T(8,128)S(1)}, u32[]{:S(2)}, u32[]{:S(2)}) collective-permute-start(f32[1,8,256]{2,1,0:T(8,128)S(1)} %copy-done.19), channel_id=1, source_target_pairs={{0,16},{16,32},{32,48},{48,64},{64,80},{80,96},{96,112},{1,17},{17... | collective-permute-start | bytes 24584 | tf_op jit(solution)/shard_map/ppermute | solution.py:515
  22.6 12.3 %copy-start.18 = (f32[1,8,256]{2,1,0:T(8,128)}, f32[1,8,256]{2,1,0:T(8,128)S(1)}, u32[]{:S(2)}) copy-start(f32[1,8,256]{2,1,0:T(8,128)S(1)} %collective-permute-done.1.refs_6_) | copy-start | bytes 24580
  27.8 4.9 %copy-start.11 = (f32[2,16,256]{2,1,0:T(8,128)}, f32[2,16,256]{2,1,0:T(8,128)S(1)}, u32[]{:S(2)}) copy-start(f32[2,16,256]{2,1,0:T(8,128)S(1)} %get-tuple-element.60.refs_5_.refs_4_) | copy-start | bytes 98308
  27.8 12.3 %all-to-all-start.1 = ((f32[16,16,256]{2,1,0:T(8,128)}), f32[16,16,256]{2,1,0:T(8,128)S(1)}, u32[]{:S(2)}, u32[]{:S(2)}) async-start(f32[16,16,256]{2,1,0:T(8,128)} %get-tuple-element.53), calls=%async_computation.1 | async-start | bytes 524288 | tf_op jit(solution)/shard_map/all_to_all | solution.py:519
  32.7 7.4 %copy-start.3 = (f32[16,8,256]{2,1,0:T(8,128)S(1)}, f32[16,8,256]{2,1,0:T(8,128)}, u32[]{:S(2)}) copy-start(f32[16,8,256]{2,1,0:T(8,128)} %get-tuple-element.46.refs_2_.refs_6_.refs_8_) | copy-start | bytes 393220
  32.7 7.4 %copy-start.5 = (f32[16,8,256]{2,1,0:T(8,128)S(1)}, f32[16,8,256]{2,1,0:T(8,128)}, u32[]{:S(2)}) copy-start(f32[16,8,256]{2,1,0:T(8,128)} %get-tuple-element.65.refs_3_.refs_9_) | copy-start | bytes 393220
  32.7 7.4 %copy-start.8 = (f32[16,8,256]{2,1,0:T(8,128)S(1)}, f32[16,8,256]{2,1,0:T(8,128)}, u32[]{:S(2)}) copy-start(f32[16,8,256]{2,1,0:T(8,128)} %get-tuple-element.63.refs_7_.refs_6_) | copy-start | bytes 393220
  32.7 7.4 %copy-start.9 = (f32[16,8,256]{2,1,0:T(8,128)S(1)}, f32[16,8,256]{2,1,0:T(8,128)}, u32[]{:S(2)}) copy-start(f32[16,8,256]{2,1,0:T(8,128)} %get-tuple-element.64.refs_8_.refs_7_) | copy-start | bytes 393220
  32.7 7.4 %copy-start.15 = (f32[3,8,256]{2,1,0:T(8,128)S(1)}, f32[3,8,256]{2,1,0:T(8,128)}, u32[]{:S(2)}) copy-start(f32[3,8,256]{2,1,0:T(8,128)} %get-tuple-element.66.refs_10_.refs_1_) | copy-start | bytes 73732
  34.9 5.2 %copy-start.16 = (f32[2,8,256]{2,1,0:T(8,128)S(1)}, f32[2,8,256]{2,1,0:T(8,128)}, u32[]{:S(2)}) copy-start(f32[2,8,256]{2,1,0:T(8,128)} %get-tuple-element.67.refs_11_.refs_2_) | copy-start | bytes 49156
  34.9 23.1 %copy-start.6 = (f32[16,8,256]{2,1,0:T(8,128)S(1)}, f32[16,8,256]{2,1,0:T(8,128)}, u32[]{:S(2)}) copy-start(f32[16,8,256]{2,1,0:T(8,128)} %get-tuple-element.74.refs_9_.refs_3_) | copy-start | bytes 393220
  34.9 23.1 %copy-start.7 = (f32[16,8,256]{2,1,0:T(8,128)S(1)}, f32[16,8,256]{2,1,0:T(8,128)}, u32[]{:S(2)}) copy-start(f32[16,8,256]{2,1,0:T(8,128)} %get-tuple-element.75.refs_10_.refs_4_) | copy-start | bytes 393220
  34.9 23.1 %copy-start.12 = (f32[16,8,256]{2,1,0:T(8,128)S(1)}, f32[16,8,256]{2,1,0:T(8,128)}, u32[]{:S(2)}) copy-start(f32[16,8,256]{2,1,0:T(8,128)} %get-tuple-element.70.refs_4_) | copy-start | bytes 393220
  34.9 23.1 %copy-start.13 = (f32[16,8,256]{2,1,0:T(8,128)S(1)}, f32[16,8,256]{2,1,0:T(8,128)}, u32[]{:S(2)}) copy-start(f32[16,8,256]{2,1,0:T(8,128)} %get-tuple-element.69.refs_3_) | copy-start | bytes 393220
  38.6 19.5 %copy-start.10 = (f32[16,8,256]{2,1,0:T(8,128)S(1)}, f32[16,8,256]{2,1,0:T(8,128)}, u32[]{:S(2)}) copy-start(f32[16,8,256]{2,1,0:T(8,128)} %get-tuple-element.71.refs_5_) | copy-start | bytes 393220
  40.1 0.9 %copy-start.14 = (f32[16,8,256]{2,1,0:T(8,128)S(1)}, f32[16,8,256]{2,1,0:T(8,128)}, u32[]{:S(2)}) copy-start(f32[16,8,256]{2,1,0:T(8,128)} %get-tuple-element.62.refs_5_) | copy-start | bytes 393220
  59.7 12.9 %all-to-all-start.3 = ((f32[16,16,256]{2,1,0:T(8,128)}), f32[16,16,256]{2,1,0:T(8,128)S(1)}, u32[]{:S(2)}, u32[]{:S(2)}) async-start(f32[16,16,256]{2,1,0:T(8,128)} %get-tuple-element.76), calls=%async_computation.3 | async-start | bytes 524288 | tf_op jit(solution)/shard_map/all_to_all | solution.py:519

commit v7 on v6

--- a/solution.py
+++ b/solution.py
@@ -431,7 +431,7 @@
         h_out[2, x] = mz[x]
 
 
-def staged(kernel, kinds_in, kinds_out, first):
+def staged(kernel, kinds_in, kinds_out, first, late):
     def body(*refs):
         ni = len(kinds_in)
         no = len(kinds_out)
@@ -447,7 +447,8 @@
                 continue
             held = rest.pop(0)
             copy = pltpu.make_async_copy(ref, held, sems.at[len(copies)])
-            copy.start()
+            if not late or len(copies) < first:
+                copy.start()
             copies.append(copy)
             work.append(held)
         back = []
@@ -462,6 +463,10 @@
         for copy in copies[:head]:
             copy.wait()
 
+        if late:
+            for copy in copies[head:]:
+                copy.start()
+
         def ready():
             for copy in copies[head:]:
                 copy.wait()
@@ -492,7 +497,7 @@
     spec = {"v": pltpu.VMEM, "h": HBM, "s": HBM}
     nbytes = sum(4 * _size(a.shape) for a in args) + sum(4 * _size(o) for o in outs)
     return pl.pallas_call(
-        staged(kernel, kinds_in, kinds_out, 0 if hot and first is not None else first),
+        staged(kernel, kinds_in, kinds_out, 0 if hot and first is not None else first, name == "coef"),
         out_shape=[jax.ShapeDtypeStruct(o, F32) for o in outs],
         in_specs=[pl.BlockSpec(memory_space=spec[k]) for k in kinds_in],
         out_specs=[pl.BlockSpec(memory_space=spec[k]) for k in kinds_out],

time: 74.2 us -> 74.8 us (level)
  transfers between devices with their start and end apart: 5 -> 5, of which waited for: 3 -> 3; matrix products, arithmetic and copies ran while one was open for 0% -> 0% of each run, Pallas kernels for 23% -> 22%
where the time goes in v7:
time: 74.8 us; the launch traced here: 74.3 us
  Pallas kernels  25.2 us (34%)
  starting transfers between devices  24.8 us (33%)
  blocking collectives  15.8 us (21%)
  waiting for transfers between devices  6.46 us (9%)
  between operations  1.01 us (1%)
  local copies, waits for them, and re-layouts  0.99 us (1%)
    pallas_call x11, Pallas kernels, call(): pl.pallas_call(staged(kernel, kinds_in, kinds_out, 0 if hot and first is...  25.2 us
    all_to_all x3, starting transfers between devices, exchange(): return lax.all_to_all(array, axis, 0, 0)  17.7 us
    all_to_all x1, blocking collectives, exchange(): return lax.all_to_all(array, axis, 0, 0)  15.8 us
    ppermute x2, starting transfers between devices, shifted(): lax.ppermute(array, axis, [(i, i + by) for i in range(count) if 0 <= i +...  7.15 us
    all_to_all x3, waiting for transfers between devices, exchange(): return lax.all_to_all(array, axis, 0, 0)  6.45 us
  transfers between devices with their start and end apart: 5, of which 3 were waited for; matrix products, arithmetic and copies ran while one was open for 0% of the time, Pallas kernels for 22%

profile of v7, /device:TPU:1, one launch (start us, length us, event | category | flops | bytes accessed | tf_op | source)
XLA Modules:
  0.0 74.3 jit_solution(8250619352776241335)
XLA Ops:
  0.6 0.0 copy-start.1
  0.6 0.0 copy-start
  0.7 3.4 %coef.1 = (f32[16,8,256]{2,1,0:T(8,128)}, f32[16,8,256]{2,1,0:T(8,128)}, f32[16,8,256]{2,1,0:T(8,128)}, f32[16,8,256]{2,1,0:T(8,128)}, f32[3,16,256]{2,1,0:T(8,1...) custom-call(s32[16,8,256]{2,1,0:T(8,128)} %refs_0_.4, f32[8]{0:T(128)} %refs_1_.4, ...), custom_call_target="tpu_custom_call" | custom-call | flops 10223872 | bytes 2555968 | tf_op jit(solution)/shard_map/coef/pallas_call | solution.py:499
  4.1 0.0 copy-start.2
  4.1 0.0 copy-start.4
  4.1 7.3 %all-to-all-start = ((f32[16,4,16,256]{3,2,1,0:T(8,128)}), f32[16,4,16,256]{3,2,1,0:T(8,128)S(1)}, u32[]{:S(2)}, u32[]{:S(2)}) async-start(f32[16,4,16,256]{3,2,1,0:T(8,128)} %get-tuple-element.44), calls=%async_computation | async-start | bytes 2097152 | tf_op jit(solution)/shard_map/all_to_all | solution.py:524
  11.4 1.3 %collective-permute-start = (f32[1,8,256]{2,1,0:T(8,128)S(1)}, f32[1,8,256]{2,1,0:T(8,128)S(1)}, u32[]{:S(2)}, u32[]{:S(2)}) collective-permute-start(f32[1,8,256]{2,1,0:T(8,128)S(1)} %copy-done.20), channel_id=1, source_target_pairs={{16,0},{32,16},{48,32},{64,48},{80,64},{96,80},{112,96},{17,1},{33... | collective-permute-start | bytes 24584 | tf_op jit(solution)/shard_map/ppermute | solution.py:520
  12.7 0.0 copy-done.19
  12.8 5.9 %collective-permute-start.1 = (f32[1,8,256]{2,1,0:T(8,128)S(1)}, f32[1,8,256]{2,1,0:T(8,128)S(1)}, u32[]{:S(2)}, u32[]{:S(2)}) collective-permute-start(f32[1,8,256]{2,1,0:T(8,128)S(1)} %copy-done.19), channel_id=1, source_target_pairs={{0,16},{16,32},{32,48},{48,64},{64,80},{80,96},{96,112},{1,17},{17... | collective-permute-start | bytes 24584 | tf_op jit(solution)/shard_map/ppermute | solution.py:520
  18.6 4.6 %factor.1 = (f32[16,16,8,256]{3,2,1,0:T(8,128)}, f32[16,8,256]{2,1,0:T(8,128)}, f32[16,8,256]{2,1,0:T(8,128)}, f32[16,8,256]{2,1,0:T(8,128)}, f32[16,8,256]{2,1,0:T(8,128)}, /*index=5*/f32[3,8,256]{2,1,0:T(8,128)}) custom-call(f32[16,8,256]{2,1,0:T(8,128)} %get-tuple-element.47.refs_0_.refs_3_.refs_11_.refs_2_), custom_call_target="tpu_custom_call" | custom-call | flops 11108352 | bytes 2777088 | tf_op jit(solution)/shard_map/factor/pallas_call | solution.py:499
  23.2 0.0 collective-permute-done.refs_4_
  23.2 0.0 collective-permute-done.1.refs_6_
  23.2 0.0 copy-start.18
  23.2 0.0 copy-done.1
  23.3 0.0 copy-done
  23.3 1.1 %chain_x.1 = (f32[16,8,256]{2,1,0:T(8,128)S(1)}, f32[16,8,256]{2,1,0:T(8,128)S(1)}, f32[2,16,256]{2,1,0:T(8,128)S(1)}) custom-call(f32[3,16,8,256]{3,2,1,0:T(8,128)S(1)} %copy-done, f32[3,16,8,256]{3,2,1,0:T(8,128)S(1)} %copy-done.1, f32[16,8,256]{2,1,0:T(8,128)S(1)} %copy-done.2, f32[16,8,256]{2,1,0:T(8,128)S(1)} %copy-done.4, ...), custom_call_target="tpu_custom_call" | custom-call | flops 5406720 | bytes 1351680 | tf_op jit(solution)/shard_map/chain_x/pallas_call | solution.py:499
  24.4 2.7 %all-to-all-done.refs_0_ = f32[16,4,16,256]{3,2,1,0:T(8,128)S(1)} async-done(((f32[16,4,16,256]{3,2,1,0:T(8,128)}), f32[16,4,16,256]{3,2,1,0:T(8,128)S(1)}, u32[]{:S(2)}, u32[]{:S(2)}) %all-to-all-start) | async-done | bytes 1048608 | tf_op jit(solution)/shard_map/all_to_all | solution.py:524
  27.1 1.2 %scan_y.1 = (f32[16,16,256]{2,1,0:T(8,128)S(1)}, f32[9,16,256]{2,1,0:T(8,128)S(1)}, f32[16,16,256]{2,1,0:T(8,128)}, f32[2,16,256]{2,1,0:T(8,128)S(1)}) custom-call(f32[16,4,16,256]{3,2,1,0:T(8,128)S(1)} %all-to-all-done.refs_0_, f32[3,16,256]{2,1,0:T(8,128)S(1)} %copy-done.17, f32[2,16,256]{2,1,0:T(8,128)S(1)} %get-tuple-element.52.refs_2_), custom_call_target="tpu_custom_call" | custom-call | flops 7340032 | bytes 1835008 | tf_op jit(solution)/shard_map/scan_y/pallas_call | solution.py:499
  28.4 4.9 %all-to-all-start.1 = ((f32[16,16,256]{2,1,0:T(8,128)}), f32[16,16,256]{2,1,0:T(8,128)S(1)}, u32[]{:S(2)}, u32[]{:S(2)}) async-start(f32[16,16,256]{2,1,0:T(8,128)} %get-tuple-element.53), calls=%async_computation.1 | async-start | bytes 524288 | tf_op jit(solution)/shard_map/all_to_all | solution.py:524
  33.3 0.0 copy-start.3
  33.3 2.2 %chain_z.1 = (f32[16,8,256]{2,1,0:T(8,128)}, f32[16,8,256]{2,1,0:T(8,128)}, f32[2,8,256]{2,1,0:T(8,128)}) custom-call(f32[3,16,8,256]{3,2,1,0:T(8,128)} %refs_0_.7, f32[3,16,8,256]{3,2,1,0:T(8,128)} %refs_1_.7, f32[16,8,256]{2,1,0:T(8,128)} %get-tuple-element.46.refs_2_.refs_6_.refs_8_, f32[16,8,256]{2,1,0:T(8,128)} %get-tuple-element.65.refs_3_.refs_9_, ...), custom_call_target="tpu_custom_call" | custom-call | flops 5439488 | bytes 1359872 | tf_op jit(solution)/shard_map/chain_z/pallas_call | solution.py:499
  35.6 3.6 %center_y.1 = (f32[16,8,256]{2,1,0:T(8,128)}, f32[16,8,256]{2,1,0:T(8,128)}) custom-call(f32[3,16,8,256]{3,2,1,0:T(8,128)} %refs_0_.7, f32[3,16,8,256]{3,2,1,0:T(8,128)} %refs_1_.7, f32[16,8,256]{2,1,0:T(8,128)} %get-tuple-element.46.refs_2_.refs_6_.refs_8_, f32[16,16,8,256]{3,2,1,0:T(8,128)} %get-tuple-element.58.refs_3_, ...), custom_call_target="tpu_custom_call" | custom-call | flops 13795328 | bytes 3448832 | tf_op jit(solution)/shard_map/center_y/pallas_call | solution.py:499
  39.2 1.5 %all-to-all-done.1.refs_0_ = f32[16,16,256]{2,1,0:T(8,128)S(1)} async-done(((f32[16,16,256]{2,1,0:T(8,128)}), f32[16,16,256]{2,1,0:T(8,128)S(1)}, u32[]{:S(2)}, u32[]{:S(2)}) %all-to-all-start.1) | async-done | bytes 262176 | tf_op jit(solution)/shard_map/all_to_all | solution.py:524
  40.7 0.9 %copy-done.14 = f32[16,8,256]{2,1,0:T(8,128)S(1)} copy-done((f32[16,8,256]{2,1,0:T(8,128)S(1)}, f32[16,8,256]{2,1,0:T(8,128)}, u32[]{:S(2)}) %copy-start.14) | copy-done | bytes 131096
  41.6 1.2 %half_x.1 = (f32[16,8,256]{2,1,0:T(8,128)S(1)}, f32[16,8,256]{2,1,0:T(8,128)S(1)}, f32[16,8,256]{2,1,0:T(8,128)S(1)}, f32[8,7,8,256]{3,2,1,0:T(8,128)S(1)}) custom-call(f32[16,16,256]{2,1,0:T(8,128)S(1)} %all-to-all-done.1.refs_0_, f32[16,16,256]{2,1,0:T(8,128)S(1)} %get-tuple-element.54.refs_1_, f32[9,16,256]{2,1,0:T(8,128)S(1)} %get-tuple-element.55.refs_2_.refs_12_, ...), custom_call_target="tpu_custom_call" | custom-call | flops 9928704 | bytes 2482176 | tf_op jit(solution)/shard_map/half_x/pallas_call | solution.py:499
  42.8 15.8 %all_to_all.20.refs_0_ = f32[8,7,8,256]{3,2,1,0:T(8,128)S(1)} all-to-all(f32[8,7,8,256]{3,2,1,0:T(8,128)S(1)} %get-tuple-element.68), channel_id=1, replica_groups=mesh['gx'=8,'gy'=16] {'gx'}, dimensions={0} | all-to-all | bytes 917504 | tf_op jit(solution)/shard_map/all_to_all | solution.py:524
  58.6 1.7 %half_z.1 = (f32[16,8,256]{2,1,0:T(8,128)S(1)}, f32[16,8,256]{2,1,0:T(8,128)S(1)}, f32[2,16,256]{2,1,0:T(8,128)S(1)}, f32[2,8,256]{2,1,0:T(8,128)S(1)}, f32[16,16,256]{2,1,0:T(8,128)}) custom-call(f32[8,7,8,256]{3,2,1,0:T(8,128)S(1)} %all_to_all.20.refs_0_, f32[3,8,256]{2,1,0:T(8,128)S(1)} %copy-done.15, f32[2,8,256]{2,1,0:T(8,128)S(1)} %copy-done.16, ...), custom_call_target="tpu_custom_call" | custom-call | flops 9601024 | bytes 2400256 | tf_op jit(solution)/shard_map/half_z/pallas_call | solution.py:499
  60.3 5.4 %all-to-all-start.3 = ((f32[16,16,256]{2,1,0:T(8,128)}), f32[16,16,256]{2,1,0:T(8,128)S(1)}, u32[]{:S(2)}, u32[]{:S(2)}) async-start(f32[16,16,256]{2,1,0:T(8,128)} %get-tuple-element.76), calls=%async_computation.3 | async-start | bytes 524288 | tf_op jit(solution)/shard_map/all_to_all | solution.py:524
  65.8 5.1 %final_x.1 = (f32[16,8,256]{2,1,0:T(8,128)S(1)}, f32[16,8,256]{2,1,0:T(8,128)S(1)}) custom-call(f32[16,8,256]{2,1,0:T(8,128)S(1)} %get-tuple-element.79.refs_0_, f32[16,8,256]{2,1,0:T(8,128)S(1)} %get-tuple-element.80.refs_1_, f32[16,8,256]{2,1,0:T(8,128)S(1)} %copy-done.4), custom_call_target="tpu_custom_call" | custom-call | flops 2621440 | bytes 655360 | tf_op jit(solution)/shard_map/final_x/pallas_call | solution.py:499
  70.9 0.1 final_y.1
  71.0 2.3 %all-to-all-done.3.refs_0_ = f32[16,16,256]{2,1,0:T(8,128)S(1)} async-done(((f32[16,16,256]{2,1,0:T(8,128)}), f32[16,16,256]{2,1,0:T(8,128)S(1)}, u32[]{:S(2)}, u32[]{:S(2)}) %all-to-all-start.3) | async-done | bytes 262176 | tf_op jit(solution)/shard_map/all_to_all | solution.py:524
  73.2 1.0 %final_z.1 = (f32[3,16,8,256]{3,2,1,0:T(8,128)}, f32[3,16,8,256]{3,2,1,0:T(8,128)}) custom-call(f32[16,16,256]{2,1,0:T(8,128)S(1)} %all-to-all-done.3.refs_0_, f32[16,16,256]{2,1,0:T(8,128)S(1)} %get-tuple-element.54.refs_1_, f32[9,16,256]{2,1,0:T(8,128)S(1)} %get-tuple-element.55.refs_2_.refs_12_, f32[2,16,256]{2,1,0:T(8,128)S(1)} %get-tuple-element.77.refs_3_, ...), custom_call_target="tpu_custom_call" | custom-call | flops 10158080 | bytes 2539520 | tf_op jit(solution)/shard_map/final_z/pallas_call | solution.py:499
  (32 shorter events, 0.1 us)
Async XLA Ops:
  0.6 22.6 %copy-start.1 = (f32[3,16,8,256]{3,2,1,0:T(8,128)S(1)}, f32[3,16,8,256]{3,2,1,0:T(8,128)}, u32[]{:S(2)}) copy-start(f32[3,16,8,256]{3,2,1,0:T(8,128)} %refs_1_.7) | copy-start | bytes 1179652
  0.6 22.6 %copy-start = (f32[3,16,8,256]{3,2,1,0:T(8,128)S(1)}, f32[3,16,8,256]{3,2,1,0:T(8,128)}, u32[]{:S(2)}) copy-start(f32[3,16,8,256]{3,2,1,0:T(8,128)} %refs_0_.7) | copy-start | bytes 1179652
  4.1 7.4 %copy-start.20 = (f32[1,8,256]{2,1,0:T(8,128)S(1)}, f32[1,8,256]{2,1,0:T(8,128)}, u32[]{:S(2)}) copy-start(f32[1,8,256]{2,1,0:T(8,128)} %get-tuple-element.48) | copy-start | bytes 24580
  4.1 8.7 %copy-start.19 = (f32[1,8,256]{2,1,0:T(8,128)S(1)}, f32[1,8,256]{2,1,0:T(8,128)}, u32[]{:S(2)}) copy-start(f32[1,8,256]{2,1,0:T(8,128)} %get-tuple-element.49) | copy-start | bytes 24580
  4.1 19.2 %copy-start.2 = (f32[16,8,256]{2,1,0:T(8,128)S(1)}, f32[16,8,256]{2,1,0:T(8,128)}, u32[]{:S(2)}) copy-start(f32[16,8,256]{2,1,0:T(8,128)} %get-tuple-element.46.refs_2_.refs_6_.refs_8_) | copy-start | bytes 393220
  4.1 19.2 %copy-start.4 = (f32[16,8,256]{2,1,0:T(8,128)S(1)}, f32[16,8,256]{2,1,0:T(8,128)}, u32[]{:S(2)}) copy-start(f32[16,8,256]{2,1,0:T(8,128)} %get-tuple-element.47.refs_0_.refs_3_.refs_11_.refs_2_) | copy-start | bytes 393220
  4.1 23.0 %copy-start.17 = (f32[3,16,256]{2,1,0:T(8,128)S(1)}, f32[3,16,256]{2,1,0:T(8,128)}, u32[]{:S(2)}) copy-start(f32[3,16,256]{2,1,0:T(8,128)} %get-tuple-element.45.refs_1_) | copy-start | bytes 147460
  4.1 23.0 %all-to-all-start = ((f32[16,4,16,256]{3,2,1,0:T(8,128)}), f32[16,4,16,256]{3,2,1,0:T(8,128)S(1)}, u32[]{:S(2)}, u32[]{:S(2)}) async-start(f32[16,4,16,256]{3,2,1,0:T(8,128)} %get-tuple-element.44), calls=%async_computation | async-start | bytes 2097152 | tf_op jit(solution)/shard_map/all_to_all | solution.py:524
  11.4 11.8 %collective-permute-start = (f32[1,8,256]{2,1,0:T(8,128)S(1)}, f32[1,8,256]{2,1,0:T(8,128)S(1)}, u32[]{:S(2)}, u32[]{:S(2)}) collective-permute-start(f32[1,8,256]{2,1,0:T(8,128)S(1)} %copy-done.20), channel_id=1, source_target_pairs={{16,0},{32,16},{48,32},{64,48},{80,64},{96,80},{112,96},{17,1},{33... | collective-permute-start | bytes 24584 | tf_op jit(solution)/shard_map/ppermute | solution.py:520
  12.8 10.5 %collective-permute-start.1 = (f32[1,8,256]{2,1,0:T(8,128)S(1)}, f32[1,8,256]{2,1,0:T(8,128)S(1)}, u32[]{:S(2)}, u32[]{:S(2)}) collective-permute-start(f32[1,8,256]{2,1,0:T(8,128)S(1)} %copy-done.19), channel_id=1, source_target_pairs={{0,16},{16,32},{32,48},{48,64},{64,80},{80,96},{96,112},{1,17},{17... | collective-permute-start | bytes 24584 | tf_op jit(solution)/shard_map/ppermute | solution.py:520
  23.2 12.3 %copy-start.18 = (f32[1,8,256]{2,1,0:T(8,128)}, f32[1,8,256]{2,1,0:T(8,128)S(1)}, u32[]{:S(2)}) copy-start(f32[1,8,256]{2,1,0:T(8,128)S(1)} %collective-permute-done.1.refs_6_) | copy-start | bytes 24580
  28.4 4.9 %copy-start.11 = (f32[2,16,256]{2,1,0:T(8,128)}, f32[2,16,256]{2,1,0:T(8,128)S(1)}, u32[]{:S(2)}) copy-start(f32[2,16,256]{2,1,0:T(8,128)S(1)} %get-tuple-element.60.refs_5_.refs_4_) | copy-start | bytes 98308
  28.4 12.3 %all-to-all-start.1 = ((f32[16,16,256]{2,1,0:T(8,128)}), f32[16,16,256]{2,1,0:T(8,128)S(1)}, u32[]{:S(2)}, u32[]{:S(2)}) async-start(f32[16,16,256]{2,1,0:T(8,128)} %get-tuple-element.53), calls=%async_computation.1 | async-start | bytes 524288 | tf_op jit(solution)/shard_map/all_to_all | solution.py:524
  33.3 7.4 %copy-start.3 = (f32[16,8,256]{2,1,0:T(8,128)S(1)}, f32[16,8,256]{2,1,0:T(8,128)}, u32[]{:S(2)}) copy-start(f32[16,8,256]{2,1,0:T(8,128)} %get-tuple-element.46.refs_2_.refs_6_.refs_8_) | copy-start | bytes 393220
  33.3 7.4 %copy-start.5 = (f32[16,8,256]{2,1,0:T(8,128)S(1)}, f32[16,8,256]{2,1,0:T(8,128)}, u32[]{:S(2)}) copy-start(f32[16,8,256]{2,1,0:T(8,128)} %get-tuple-element.65.refs_3_.refs_9_) | copy-start | bytes 393220
  33.3 7.4 %copy-start.8 = (f32[16,8,256]{2,1,0:T(8,128)S(1)}, f32[16,8,256]{2,1,0:T(8,128)}, u32[]{:S(2)}) copy-start(f32[16,8,256]{2,1,0:T(8,128)} %get-tuple-element.63.refs_7_.refs_6_) | copy-start | bytes 393220
  33.3 7.4 %copy-start.9 = (f32[16,8,256]{2,1,0:T(8,128)S(1)}, f32[16,8,256]{2,1,0:T(8,128)}, u32[]{:S(2)}) copy-start(f32[16,8,256]{2,1,0:T(8,128)} %get-tuple-element.64.refs_8_.refs_7_) | copy-start | bytes 393220
  33.3 7.4 %copy-start.15 = (f32[3,8,256]{2,1,0:T(8,128)S(1)}, f32[3,8,256]{2,1,0:T(8,128)}, u32[]{:S(2)}) copy-start(f32[3,8,256]{2,1,0:T(8,128)} %get-tuple-element.66.refs_10_.refs_1_) | copy-start | bytes 73732
  35.5 5.2 %copy-start.16 = (f32[2,8,256]{2,1,0:T(8,128)S(1)}, f32[2,8,256]{2,1,0:T(8,128)}, u32[]{:S(2)}) copy-start(f32[2,8,256]{2,1,0:T(8,128)} %get-tuple-element.67.refs_11_.refs_2_) | copy-start | bytes 49156
  35.5 23.1 %copy-start.6 = (f32[16,8,256]{2,1,0:T(8,128)S(1)}, f32[16,8,256]{2,1,0:T(8,128)}, u32[]{:S(2)}) copy-start(f32[16,8,256]{2,1,0:T(8,128)} %get-tuple-element.74.refs_9_.refs_3_) | copy-start | bytes 393220
  35.5 23.1 %copy-start.7 = (f32[16,8,256]{2,1,0:T(8,128)S(1)}, f32[16,8,256]{2,1,0:T(8,128)}, u32[]{:S(2)}) copy-start(f32[16,8,256]{2,1,0:T(8,128)} %get-tuple-element.75.refs_10_.refs_4_) | copy-start | bytes 393220
  35.5 23.1 %copy-start.12 = (f32[16,8,256]{2,1,0:T(8,128)S(1)}, f32[16,8,256]{2,1,0:T(8,128)}, u32[]{:S(2)}) copy-start(f32[16,8,256]{2,1,0:T(8,128)} %get-tuple-element.70.refs_4_) | copy-start | bytes 393220
  35.5 23.1 %copy-start.13 = (f32[16,8,256]{2,1,0:T(8,128)S(1)}, f32[16,8,256]{2,1,0:T(8,128)}, u32[]{:S(2)}) copy-start(f32[16,8,256]{2,1,0:T(8,128)} %get-tuple-element.69.refs_3_) | copy-start | bytes 393220
  39.2 19.5 %copy-start.10 = (f32[16,8,256]{2,1,0:T(8,128)S(1)}, f32[16,8,256]{2,1,0:T(8,128)}, u32[]{:S(2)}) copy-start(f32[16,8,256]{2,1,0:T(8,128)} %get-tuple-element.71.refs_5_) | copy-start | bytes 393220
  40.7 0.9 %copy-start.14 = (f32[16,8,256]{2,1,0:T(8,128)S(1)}, f32[16,8,256]{2,1,0:T(8,128)}, u32[]{:S(2)}) copy-start(f32[16,8,256]{2,1,0:T(8,128)} %get-tuple-element.62.refs_5_) | copy-start | bytes 393220
  60.3 12.9 %all-to-all-start.3 = ((f32[16,16,256]{2,1,0:T(8,128)}), f32[16,16,256]{2,1,0:T(8,128)S(1)}, u32[]{:S(2)}, u32[]{:S(2)}) async-start(f32[16,16,256]{2,1,0:T(8,128)} %get-tuple-element.76), calls=%async_computation.3 | async-start | bytes 524288 | tf_op jit(solution)/shard_map/all_to_all | solution.py:524
